TPU v7x, 32 devices: a whole 2x2x4 slice. The times are simulated.
32 devices in a mesh: section: 2 (over x), expert: 16 (over z, y, core).
Axes of the slice: x: 2, y: 2, z: 4, core: 2. Of those that a mesh axis runs over, the one named last changes fastest.
Arguments:
- grad_out: bfloat16 [2, 2048, 4096], P('section', 'expert'), may hold values from -6 to 6
- expert_ids: int32 [2, 2048, 8], P('section', 'expert'), may hold values from 0 to 15, all different within a row; in each aligned block of 128 rows (0 to 127, 128 to 255, ..., all dimensions but the last counted through in order) at most 72 rows name the same one
- gate_weights: float32 [2, 2048, 8], P('section', 'expert'), may hold values from 0.05 to 0.6
- saved_gate: bfloat16 [2, 16, 1152, 768], P('section', 'expert'), may hold values from -6 to 6
- saved_up: bfloat16 [2, 16, 1152, 768], P('section', 'expert'), may hold values from -6 to 6
- w_gate: bfloat16 [2, 16, 4096, 768], P('section', 'expert'), may hold values from -0.09375 to 0.09375
- w_up: bfloat16 [2, 16, 4096, 768], P('section', 'expert'), may hold values from -0.09375 to 0.09375
- w_down: bfloat16 [2, 16, 768, 4096], P('section', 'expert'), may hold values from -0.21875 to 0.21875
Outputs:
- upstream: bfloat16 [2, 2048, 4096], P('section', 'expert')
Inputs may be any that keep to these rules, and one draw needn't show every extreme that they name: `expert_ids`: each token names 8 different experts of its section's 16; no expert is named by more than 72 of the tokens of one device, a bound that some block reaches of some device in every draw.
All inputs are finite; a program needn't handle non-finite values.
Results may differ from a plain program's by a relative error of at most 0.0057.
Values may be sent and summed in bfloat16 or wider, within the bound.
No kernel may reach another device: no remote copies, remote signals or barrier semaphores. Data moves between devices by JAX's collectives and lax.ppermute only.
A program may use at most 128 MiB of HBM per device.

v0:
```python
import functools
import math

import jax
import jax.numpy as jnp
import numpy as np
from jax import lax
from jax.experimental import pallas as pl
from jax.experimental.pallas import tpu as pltpu
from jax.sharding import PartitionSpec as P

PIECES = 2
CONTRACT = (((1,), (1,)), ((), ()))


def chip_ring(chips):
    width = 1 << (int(math.log2(chips)) // 2)
    height = chips // width
    tour = []
    for row in range(height):
        columns = list(range(1, width))
        if row % 2:
            columns.reverse()
        tour += [row * width + column for column in columns]
    return tour + [row * width for row in reversed(range(height))]


def origin_table(devices, tour):
    chips = len(tour)
    place = {chip: k for k, chip in enumerate(tour)}
    table = np.zeros((devices, chips, 2), np.int32)
    for device in range(devices):
        at = place[device // 2]
        for step in range(chips):
            by_core = [2 * tour[(at - step) % chips], 2 * tour[(at + step) % chips] + 1]
            table[device, step] = by_core[device % 2], by_core[1 - device % 2]
    return table


def expert_kernel(
    origin, a0, a1, b0, b1, table, saved_gate, saved_up, w_down, w_gate, w_up, mine0, mine1, given0, given1,
    block, entry, gate_rows, up_rows, down_v, gate_v, up_v, gate_grad, up_grad, scale, out_mine, out_given,
    block_sem, entry_sem, rows_sem, down_sem, wide_sem, out_sem,
):
    piece, width = a0.shape
    tokens = 2 * piece
    hidden_parts, hidden_block = down_v.shape[0], down_v.shape[1]
    parts, part = gate_v.shape[0], gate_v.shape[1]
    capacity = gate_rows.shape[1]

    def block_copy(n):
        return pltpu.make_async_copy((a0, a1, b0, b1)[n], block.at[pl.ds(n * piece, piece)], block_sem.at[n])

    def entry_copy(n):
        return pltpu.make_async_copy(table.at[origin[n]], entry.at[n], entry_sem.at[n])

    def gate_rows_copy(n):
        return pltpu.make_async_copy(saved_gate.at[origin[n]], gate_rows.at[n], rows_sem.at[n])

    def up_rows_copy(n):
        return pltpu.make_async_copy(saved_up.at[origin[n]], up_rows.at[n], rows_sem.at[2 + n])

    def down_copy(n):
        return pltpu.make_async_copy(w_down.at[pl.ds(n * hidden_block, hidden_block)], down_v.at[n], down_sem.at[n])

    def gate_copy(n):
        return pltpu.make_async_copy(w_gate.at[pl.ds(n * part, part)], gate_v.at[n], wide_sem.at[n])

    def up_copy(n):
        return pltpu.make_async_copy(w_up.at[pl.ds(n * part, part)], up_v.at[n], wide_sem.at[parts + n])

    for n in range(4):
        block_copy(n).start()
    down_copy(0).start()
    for n in range(2):
        entry_copy(n).start()
        gate_rows_copy(n).start()
        up_rows_copy(n).start()
    for n in range(1, hidden_parts):
        down_copy(n).start()
    for n in range(2):
        entry_copy(n).wait()
        gate_rows_copy(n).wait()
        up_rows_copy(n).wait()
    picks = []
    for n in range(2):
        place = jnp.broadcast_to(entry[n, 0:1, :], (tokens, tokens)).T
        slot = lax.broadcasted_iota(jnp.int32, (tokens, tokens), 1).astype(jnp.float32)
        picks.append(jnp.where(place == slot, 1.0, 0.0).astype(jnp.bfloat16)[:, :capacity])
        scale[pl.ds(n * tokens, tokens), :] = jnp.broadcast_to(entry[n, 1:2, :], (tokens, tokens)).T
    for n in range(4):
        block_copy(n).wait()

    for k in range(hidden_parts):
        columns = pl.ds(k * hidden_block, hidden_block)
        down_copy(k).wait()
        for n in range(parts * k // hidden_parts, parts * (k + 1) // hidden_parts):
            gate_copy(n).start()
            up_copy(n).start()
        hidden_grad = lax.dot_general(block[...], down_v[k], CONTRACT, preferred_element_type=jnp.float32)
        for n in range(2):
            gate = jnp.dot(picks[n], gate_rows[n, :, columns], preferred_element_type=jnp.float32)
            up = jnp.dot(picks[n], up_rows[n, :, columns], preferred_element_type=jnp.float32)
            sig = 1.0 / (1.0 + jnp.exp(-gate))
            grad = hidden_grad[n * tokens:(n + 1) * tokens] * sig
            rows = pl.ds(n * tokens, tokens)
            gate_grad[rows, columns] = (grad * up * (1.0 + gate * (1.0 - sig))).astype(jnp.bfloat16)
            up_grad[rows, columns] = (grad * gate).astype(jnp.bfloat16)

    outs = (mine0, mine1, given0, given1)

    def out_copy(j, n):
        held = (out_mine, out_mine, out_given, out_given)[n]
        return pltpu.make_async_copy(
            held.at[j, pl.ds((n % 2) * piece, piece)],
            outs[n].at[:, pl.ds(pl.multiple_of(j * part, part), part)],
            out_sem.at[j, n],
        )

    def wide_step(j, carry):
        gate_copy(j).wait()
        up_copy(j).wait()
        back = lax.dot_general(gate_grad[...], gate_v[j], CONTRACT, preferred_element_type=jnp.float32)
        back = back + lax.dot_general(up_grad[...], up_v[j], CONTRACT, preferred_element_type=jnp.float32)
        back = back.astype(jnp.bfloat16).astype(jnp.float32) * scale[:, 0:1]
        out_mine[j] = back[:tokens]
        out_given[j] = back[tokens:].astype(jnp.bfloat16)
        for n in range(4):
            out_copy(j, n).start()
        return carry

    lax.fori_loop(0, parts, wide_step, 0)

    def drain(j, carry):
        for n in range(4):
            out_copy(j, n).wait()
        return carry

    lax.fori_loop(0, parts, drain, 0)


def expert_step(origin, held, other, table, gate_rows, up_rows, w_down, w_gate, w_up):
    piece, width = held[0].shape
    tokens = 2 * piece
    hidden = w_down.shape[0]
    capacity = gate_rows.shape[1]
    hidden_block, part = 256, 512
    hidden_parts, parts = hidden // hidden_block, width // part
    anywhere = pl.BlockSpec(memory_space=pl.ANY)
    bf16, f32 = jnp.bfloat16, jnp.float32
    dma = pltpu.SemaphoreType.DMA
    flops = 2 * 2 * tokens * hidden * width * 3
    moved = 2 * 3 * hidden * width + 2 * tokens * width * 5
    return pl.pallas_call(
        expert_kernel,
        in_specs=[pl.BlockSpec(memory_space=pltpu.SMEM)] + [anywhere] * 10,
        out_specs=[anywhere] * 4,
        out_shape=[jax.ShapeDtypeStruct((piece, width), f32)] * 2 + [jax.ShapeDtypeStruct((piece, width), bf16)] * 2,
        scratch_shapes=[
            pltpu.VMEM((2 * tokens, width), bf16),
            pltpu.VMEM((2,) + table.shape[1:], f32),
            pltpu.VMEM((2, capacity, hidden), bf16),
            pltpu.VMEM((2, capacity, hidden), bf16),
            pltpu.VMEM((hidden_parts, hidden_block, width), bf16),
            pltpu.VMEM((parts, part, hidden), bf16),
            pltpu.VMEM((parts, part, hidden), bf16),
            pltpu.VMEM((2 * tokens, hidden), bf16),
            pltpu.VMEM((2 * tokens, hidden), bf16),
            pltpu.VMEM((2 * tokens, tokens), f32),
            pltpu.VMEM((parts, tokens, part), f32),
            pltpu.VMEM((parts, tokens, part), bf16),
            dma((4,)),
            dma((2,)),
            dma((4,)),
            dma((hidden_parts,)),
            dma((2 * parts,)),
            dma((parts, 4)),
        ],
        compiler_params=pltpu.CompilerParams(vmem_limit_bytes=40 << 20),
        cost_estimate=pl.CostEstimate(flops=flops, transcendentals=2 * tokens * hidden, bytes_accessed=moved),
        name="expert_step",
    )(origin, *held, *other, table, gate_rows, up_rows, w_down, w_gate, w_up)


def body(grad_out, expert_ids, gate_weights, saved_gate, saved_up, w_gate, w_up, w_down):
    devices = lax.axis_size("expert")
    sections = lax.axis_size("section")
    chips = devices // 2
    tour = chip_ring(chips)
    following = {chip: tour[(k + 1) % chips] for k, chip in enumerate(tour)}
    onward = [(2 * a, 2 * b) for a, b in following.items()] + [(2 * b + 1, 2 * a + 1) for a, b in following.items()]
    swap = [(i, i ^ 1) for i in range(devices)]
    relay = [(s * devices + i, (s - 1) * devices + i) for s in range(1, sections) for i in range(devices)]
    relay_onward = [(s * devices + a, (s - 1) * devices + b) for s in range(1, sections) for a, b in onward]

    me = lax.axis_index("expert")
    origins = lax.dynamic_index_in_dim(jnp.asarray(origin_table(devices, tour)), me, 0, keepdims=False)

    rows = grad_out[0]
    tokens = rows.shape[0]
    hidden = saved_gate.shape[3]
    capacity = saved_gate.shape[2] // devices
    piece = tokens // PIECES
    first = [rows[h * piece:(h + 1) * piece] for h in range(PIECES)]
    first, routing, weights = lax.optimization_barrier((first, expert_ids[0], gate_weights[0]))

    blocks = [first]
    for step in range(1, chips):
        with jax.named_scope(f"gather_{step}"):
            blocks.append([lax.ppermute(b, "expert", onward) for b in blocks[-1]])
    others = []
    for step in range(chips):
        with jax.named_scope(f"share_{step}"):
            others.append([lax.ppermute(b, "expert", swap) for b in blocks[step]])

    with jax.named_scope("routing"):
        experts = jnp.arange(devices, dtype=jnp.int32)
        chosen = routing[:, None, :] == experts[None, :, None]
        named = jnp.any(chosen, axis=2)
        weight_of = jnp.sum(jnp.where(chosen, weights[:, None, :], 0.0), axis=2)
        earlier = jnp.tril(jnp.ones((tokens, tokens), jnp.bfloat16), -1)
        position = lax.dot_general(
            earlier, named.astype(jnp.bfloat16), (((1,), (0,)), ((), ())), preferred_element_type=jnp.float32
        )
        position = jnp.where(named, position, -1.0)
        table = jnp.stack([position.T, weight_of.T], axis=1)
        table = lax.all_to_all(table, "expert", split_axis=0, concat_axis=0, tiled=True)

    gate_rows = saved_gate[0, 0].reshape(devices, capacity, hidden)
    up_rows = saved_up[0, 0].reshape(devices, capacity, hidden)

    running = own = None
    token = origins
    for step in range(chips):
        with jax.named_scope(f"expert_{step}"):
            parts = expert_step(
                token[step], blocks[step], others[step], table, gate_rows, up_rows, w_down[0, 0], w_gate[0, 0], w_up[0, 0]
            )
            token, *parts = lax.optimization_barrier((token, *parts))
        with jax.named_scope(f"give_{step}"):
            given = [lax.ppermute(p, "expert", swap) for p in parts[PIECES:]]
        total = [a + b.astype(jnp.float32) for a, b in zip(parts[:PIECES], given)]
        if step == 0:
            with jax.named_scope("relay_own"):
                own = [lax.ppermute(c.astype(jnp.bfloat16), ("section", "expert"), relay) for c in total]
        elif step == 1:
            running = [c.astype(jnp.bfloat16) for c in total]
        else:
            with jax.named_scope(f"reduce_{step}"):
                arrived = [lax.ppermute(r, "expert", onward) for r in running]
                running = [(a.astype(jnp.float32) + c).astype(jnp.bfloat16) for a, c in zip(arrived, total)]
    with jax.named_scope("relay_last"):
        last = [lax.ppermute(r, ("section", "expert"), relay_onward) for r in running]
    result = [(a.astype(jnp.float32) + b.astype(jnp.float32)).astype(jnp.bfloat16) for a, b in zip(last, own)]
    return jnp.concatenate(result, axis=0)[None]


def solution(mesh):
    placed = (
        P("section", "expert", None),
        P("section", "expert", None),
        P("section", "expert", None),
        P("section", "expert", None, None),
        P("section", "expert", None, None),
        P("section", "expert", None, None),
        P("section", "expert", None, None),
        P("section", "expert", None, None),
    )
    return jax.shard_map(
        body, mesh=mesh, in_specs=placed, out_specs=P("section", "expert", None), check_vma=False
    )
```

profile of v0, /device:TPU:12, one launch (start us, length us, event | category | flops | bytes accessed | tf_op | source)
XLA Modules:
  0.0 241.7 jit_solution(15673889768526002572)
XLA Ops:
  5.6 5.3 %all-to-all-start = ((f32[16,2,128]{2,1,0:T(2,128)}), f32[16,2,128]{2,1,0:T(2,128)S(1)}, u32[]{:S(2)}, u32[]{:S(2)}) async-start(f32[16,2,128]{2,1,0:T(2,128)} %pad_maximum_fusion), calls=%async_computation | async-start | bytes 32768 | tf_op jit(solution)/shard_map/routing/all_to_all | solution.py:227
  11.8 4.7 %collective-permute-done.3.a1 = bf16[64,4096]{1,0:T(8,128)(2,1)S(1)} collective-permute-done((bf16[64,4096]{1,0:T(8,128)(2,1)S(1)}, bf16[64,4096]{1,0:T(8,128)(2,1)S(1)}, u32[]{:S(2)}, u32[]{:S(2)}) %collective-permute-start.3) | collective-permute-done | bytes 524320 | tf_op jit(solution)/shard_map/gather_1/ppermute | solution.py:210
  19.0 12.0 %expert_step.8 = (f32[64,4096]{1,0:T(8,128)S(1)}, f32[64,4096]{1,0:T(8,128)S(1)}, bf16[64,4096]{1,0:T(8,128)(2,1)S(1)}, bf16[64,4096]{1,0:T(8,128)(2,1)S(1)}) custom-call(s32[2]{0:T(128)S(1)} %slice_bitcast_fusion.2.origin, bf16[64,4096]{1,0:T(8,128)(2,1)S(1)} %get-tuple-element.80.a0, bf16[64,4096]{1,0:T(8,128)(2,1)S(1)} %get-tuple-element.81.a1, ...), custom_call_target="tpu_custom_call" | custom-call | flops 4831838208 | bytes 24117248 | tf_op jit(solution)/shard_map/expert_0/expert_step/pallas_call | solution.py:154
  34.1 12.1 %expert_step.9 = (f32[64,4096]{1,0:T(8,128)S(1)}, f32[64,4096]{1,0:T(8,128)S(1)}, bf16[64,4096]{1,0:T(8,128)(2,1)S(1)}, bf16[64,4096]{1,0:T(8,128)(2,1)S(1)}) custom-call(s32[2]{0:T(128)S(1)} %slice_reduce_fusion.6.origin, bf16[64,4096]{1,0:T(8,128)(2,1)} %collective-permute-done.2.a0, bf16[64,4096]{1,0:T(8,128)(2,1)S(1)} %collective-permute-done.3.a1, ...), custom_call_target="tpu_custom_call" | custom-call | flops 4831838208 | bytes 24117248 | tf_op jit(solution)/shard_map/expert_1/expert_step/pallas_call | solution.py:154
  52.5 11.8 %expert_step.10 = (f32[64,4096]{1,0:T(8,128)S(1)}, f32[64,4096]{1,0:T(8,128)S(1)}, bf16[64,4096]{1,0:T(8,128)(2,1)S(1)}, bf16[64,4096]{1,0:T(8,128)(2,1)S(1)}) custom-call(s32[2]{0:T(128)S(1)} %slice_reduce_fusion.5.origin, bf16[64,4096]{1,0:T(8,128)(2,1)S(1)} %collective-permute-done.8.a0, bf16[64,4096]{1,0:T(8,128)(2,1)S(1)} %collective-permute-done.9.a1, ...), custom_call_target="tpu_custom_call" | custom-call | flops 4831838208 | bytes 24117248 | tf_op jit(solution)/shard_map/expert_2/expert_step/pallas_call | solution.py:154
  65.3 1.8 collective-permute-done.16.b0
  67.9 11.8 %expert_step.11 = (f32[64,4096]{1,0:T(8,128)S(1)}, f32[64,4096]{1,0:T(8,128)S(1)}, bf16[64,4096]{1,0:T(8,128)(2,1)S(1)}, bf16[64,4096]{1,0:T(8,128)(2,1)S(1)}) custom-call(s32[2]{0:T(128)S(1)} %slice_reduce_fusion.4.origin, bf16[64,4096]{1,0:T(8,128)(2,1)S(1)} %collective-permute-done.14.a0, bf16[64,4096]{1,0:T(8,128)(2,1)S(1)} %collective-permute-done.15.a1, ...), custom_call_target="tpu_custom_call" | custom-call | flops 4831838208 | bytes 24117248 | tf_op jit(solution)/shard_map/expert_3/expert_step/pallas_call | solution.py:154
  81.8 7.1 %collective-permute-done.20.a0 = bf16[64,4096]{1,0:T(8,128)(2,1)S(1)} collective-permute-done((bf16[64,4096]{1,0:T(8,128)(2,1)S(1)}, bf16[64,4096]{1,0:T(8,128)(2,1)S(1)}, u32[]{:S(2)}, u32[]{:S(2)}) %collective-permute-start.20) | collective-permute-done | bytes 524320 | tf_op jit(solution)/shard_map/gather_4/ppermute | solution.py:210
  89.9 4.6 %collective-permute-done.21.a1 = bf16[64,4096]{1,0:T(8,128)(2,1)S(1)} collective-permute-done((bf16[64,4096]{1,0:T(8,128)(2,1)S(1)}, bf16[64,4096]{1,0:T(8,128)(2,1)S(1)}, u32[]{:S(2)}, u32[]{:S(2)}) %collective-permute-start.21) | collective-permute-done | bytes 524320 | tf_op jit(solution)/shard_map/gather_4/ppermute | solution.py:210
  95.5 1.7 collective-permute-done.22.b0
  98.2 11.8 %expert_step.12 = (f32[64,4096]{1,0:T(8,128)S(1)}, f32[64,4096]{1,0:T(8,128)S(1)}, bf16[64,4096]{1,0:T(8,128)(2,1)S(1)}, bf16[64,4096]{1,0:T(8,128)(2,1)S(1)}) custom-call(s32[2]{0:T(128)S(1)} %slice_reduce_fusion.3.origin, bf16[64,4096]{1,0:T(8,128)(2,1)S(1)} %collective-permute-done.20.a0, bf16[64,4096]{1,0:T(8,128)(2,1)S(1)} %collective-permute-done.21.a1, ...), custom_call_target="tpu_custom_call" | custom-call | flops 4831838208 | bytes 24117248 | tf_op jit(solution)/shard_map/expert_4/expert_step/pallas_call | solution.py:154
  112.1 7.1 %collective-permute-done.26.a0 = bf16[64,4096]{1,0:T(8,128)(2,1)S(1)} collective-permute-done((bf16[64,4096]{1,0:T(8,128)(2,1)S(1)}, bf16[64,4096]{1,0:T(8,128)(2,1)S(1)}, u32[]{:S(2)}, u32[]{:S(2)}) %collective-permute-start.26) | collective-permute-done | bytes 524320 | tf_op jit(solution)/shard_map/gather_5/ppermute | solution.py:210
  120.1 4.7 %collective-permute-done.27.a1 = bf16[64,4096]{1,0:T(8,128)(2,1)S(1)} collective-permute-done((bf16[64,4096]{1,0:T(8,128)(2,1)S(1)}, bf16[64,4096]{1,0:T(8,128)(2,1)S(1)}, u32[]{:S(2)}, u32[]{:S(2)}) %collective-permute-start.27) | collective-permute-done | bytes 524320 | tf_op jit(solution)/shard_map/gather_5/ppermute | solution.py:210
  128.4 11.8 %expert_step.13 = (f32[64,4096]{1,0:T(8,128)S(1)}, f32[64,4096]{1,0:T(8,128)S(1)}, bf16[64,4096]{1,0:T(8,128)(2,1)S(1)}, bf16[64,4096]{1,0:T(8,128)(2,1)S(1)}) custom-call(s32[2]{0:T(128)S(1)} %slice_reduce_fusion.2.origin, bf16[64,4096]{1,0:T(8,128)(2,1)S(1)} %collective-permute-done.26.a0, bf16[64,4096]{1,0:T(8,128)(2,1)S(1)} %collective-permute-done.27.a1, ...), custom_call_target="tpu_custom_call" | custom-call | flops 4831838208 | bytes 24117248 | tf_op jit(solution)/shard_map/expert_5/expert_step/pallas_call | solution.py:154
  142.3 7.1 %collective-permute-done.32.a0 = bf16[64,4096]{1,0:T(8,128)(2,1)S(1)} collective-permute-done((bf16[64,4096]{1,0:T(8,128)(2,1)S(1)}, bf16[64,4096]{1,0:T(8,128)(2,1)S(1)}, u32[]{:S(2)}, u32[]{:S(2)}) %collective-permute-start.32) | collective-permute-done | bytes 524320 | tf_op jit(solution)/shard_map/gather_6/ppermute | solution.py:210
  150.4 4.6 %collective-permute-done.33.a1 = bf16[64,4096]{1,0:T(8,128)(2,1)S(1)} collective-permute-done((bf16[64,4096]{1,0:T(8,128)(2,1)S(1)}, bf16[64,4096]{1,0:T(8,128)(2,1)S(1)}, u32[]{:S(2)}, u32[]{:S(2)}) %collective-permute-start.33) | collective-permute-done | bytes 524320 | tf_op jit(solution)/shard_map/gather_6/ppermute | solution.py:210
  158.7 11.7 %expert_step.14 = (f32[64,4096]{1,0:T(8,128)S(1)}, f32[64,4096]{1,0:T(8,128)S(1)}, bf16[64,4096]{1,0:T(8,128)(2,1)S(1)}, bf16[64,4096]{1,0:T(8,128)(2,1)S(1)}) custom-call(s32[2]{0:T(128)S(1)} %slice_reduce_fusion.1.origin, bf16[64,4096]{1,0:T(8,128)(2,1)S(1)} %collective-permute-done.32.a0, bf16[64,4096]{1,0:T(8,128)(2,1)S(1)} %collective-permute-done.33.a1, ...), custom_call_target="tpu_custom_call" | custom-call | flops 4831838208 | bytes 24117248 | tf_op jit(solution)/shard_map/expert_6/expert_step/pallas_call | solution.py:154
  174.2 5.5 %collective-permute-done.38.a0 = bf16[64,4096]{1,0:T(8,128)(2,1)S(1)} collective-permute-done((bf16[64,4096]{1,0:T(8,128)(2,1)S(1)}, bf16[64,4096]{1,0:T(8,128)(2,1)S(1)}, u32[]{:S(2)}, u32[]{:S(2)}) %collective-permute-start.38) | collective-permute-done | bytes 524320 | tf_op jit(solution)/shard_map/gather_7/ppermute | solution.py:210
  180.6 4.7 %collective-permute-done.39.a1 = bf16[64,4096]{1,0:T(8,128)(2,1)S(1)} collective-permute-done((bf16[64,4096]{1,0:T(8,128)(2,1)S(1)}, bf16[64,4096]{1,0:T(8,128)(2,1)S(1)}, u32[]{:S(2)}, u32[]{:S(2)}) %collective-permute-start.39) | collective-permute-done | bytes 524320 | tf_op jit(solution)/shard_map/gather_7/ppermute | solution.py:210
  185.3 5.6 %collective-permute-done.31 = bf16[64,4096]{1,0:T(8,128)(2,1)S(1)} collective-permute-done((bf16[64,4096]{1,0:T(8,128)(2,1)S(1)}, bf16[64,4096]{1,0:T(8,128)(2,1)S(1)}, u32[]{:S(2)}, u32[]{:S(2)}) %collective-permute-start.31) | collective-permute-done | bytes 524320 | tf_op jit(solution)/shard_map/reduce_6/ppermute | solution.py:250
  195.1 11.8 %expert_step.15 = (f32[64,4096]{1,0:T(8,128)S(1)}, f32[64,4096]{1,0:T(8,128)S(1)}, bf16[64,4096]{1,0:T(8,128)(2,1)S(1)}, bf16[64,4096]{1,0:T(8,128)(2,1)S(1)}) custom-call(s32[2]{0:T(128)S(1)} %slice_reduce_fusion.origin, bf16[64,4096]{1,0:T(8,128)(2,1)S(1)} %collective-permute-done.38.a0, bf16[64,4096]{1,0:T(8,128)(2,1)S(1)} %collective-permute-done.39.a1, ...), custom_call_target="tpu_custom_call" | custom-call | flops 4831838208 | bytes 24117248 | tf_op jit(solution)/shard_map/expert_7/expert_step/pallas_call | solution.py:154
  210.3 6.0 %collective-permute-done.57 = bf16[64,4096]{1,0:T(8,128)(2,1)S(1)} collective-permute-done((bf16[64,4096]{1,0:T(8,128)(2,1)S(1)}, bf16[64,4096]{1,0:T(8,128)(2,1)S(1)}, u32[]{:S(2)}, u32[]{:S(2)}) %collective-permute-start.57) | collective-permute-done | bytes 524320 | tf_op jit(solution)/shard_map/reduce_7/ppermute | solution.py:250
  217.8 11.9 %collective-permute-done.43 = bf16[64,4096]{1,0:T(8,128)(2,1)S(1)} collective-permute-done((bf16[64,4096]{1,0:T(8,128)(2,1)S(1)}, bf16[64,4096]{1,0:T(8,128)(2,1)S(1)}, u32[]{:S(2)}, u32[]{:S(2)}) %collective-permute-start.43) | collective-permute-done | bytes 524320 | tf_op jit(solution)/shard_map/relay_last/ppermute | solution.py:253
  229.9 10.6 %collective-permute-done.59 = bf16[64,4096]{1,0:T(8,128)(2,1)S(1)} collective-permute-done((bf16[64,4096]{1,0:T(8,128)(2,1)S(1)}, bf16[64,4096]{1,0:T(8,128)(2,1)S(1)}, u32[]{:S(2)}, u32[]{:S(2)}) %collective-permute-start.59) | collective-permute-done | bytes 524320 | tf_op jit(solution)/shard_map/relay_last/ppermute | solution.py:253
  (155 shorter events, 53.5 us)
Async XLA Ops:
  11.7 20.9 %collective-permute-start.4 = (bf16[64,4096]{1,0:T(8,128)(2,1)}, bf16[64,4096]{1,0:T(8,128)(2,1)}, u32[]{:S(2)}, u32[]{:S(2)}) collective-permute-start(bf16[64,4096]{1,0:T(8,128)(2,1)} %collective-permute-done.2.a0), channel_id=1, source_target_pairs={{0,1},{1,0},{2,3},{3,2},{4,5},{5,4},{6,7},{7,6},{8,9},{9,8},{10,11... | collective-permute-start | bytes 1572872 | tf_op jit(solution)/shard_map/share_1/ppermute | solution.py:214
  16.5 17.6 %collective-permute-start.5 = (bf16[64,4096]{1,0:T(8,128)(2,1)S(1)}, bf16[64,4096]{1,0:T(8,128)(2,1)}, u32[]{:S(2)}, u32[]{:S(2)}) collective-permute-start(bf16[64,4096]{1,0:T(8,128)(2,1)S(1)} %collective-permute-done.3.a1), channel_id=1, source_target_pairs={{0,1},{1,0},{2,3},{3,2},{4,5},{5,4},{6,7},{7,6},{8,9},{9,8},{10,11... | collective-permute-start | bytes 1572872 | tf_op jit(solution)/shard_map/share_1/ppermute | solution.py:214
  31.2 17.3 %collective-permute-start.60 = (bf16[64,4096]{1,0:T(8,128)(2,1)S(1)}, bf16[64,4096]{1,0:T(8,128)(2,1)S(1)}, u32[]{:S(2)}, u32[]{:S(2)}) collective-permute-start(bf16[64,4096]{1,0:T(8,128)(2,1)S(1)} %get-tuple-element.154), channel_id=1, source_target_pairs={{0,1},{1,0},{2,3},{3,2},{4,5},{5,4},{6,7},{7,6},{8,9},{9,8},{10,11... | collective-permute-start | bytes 1572872 | tf_op jit(solution)/shard_map/give_0/ppermute | solution.py:241
  46.3 18.6 %collective-permute-start.46 = (bf16[64,4096]{1,0:T(8,128)(2,1)S(1)}, bf16[64,4096]{1,0:T(8,128)(2,1)S(1)}, u32[]{:S(2)}, u32[]{:S(2)}) collective-permute-start(bf16[64,4096]{1,0:T(8,128)(2,1)S(1)} %get-tuple-element.140), channel_id=1, source_target_pairs={{0,1},{1,0},{2,3},{3,2},{4,5},{5,4},{6,7},{7,6},{8,9},{9,8},{10,11... | collective-permute-start | bytes 1572872 | tf_op jit(solution)/shard_map/give_1/ppermute | solution.py:241
  46.9 17.4 %collective-permute-start.14 = (bf16[64,4096]{1,0:T(8,128)(2,1)S(1)}, bf16[64,4096]{1,0:T(8,128)(2,1)S(1)}, u32[]{:S(2)}, u32[]{:S(2)}) collective-permute-start(bf16[64,4096]{1,0:T(8,128)(2,1)S(1)} %collective-permute-done.8.a0), channel_id=1, source_target_pairs={{2,6},{6,10},{10,14},{14,12},{12,8},{8,4},{4,0},{0,2},{7,3},{11,7}... | collective-permute-start | bytes 1572872 | tf_op jit(solution)/shard_map/gather_3/ppermute | solution.py:210
  49.8 168.1 %collective-permute-start.45 = (bf16[64,4096]{1,0:T(8,128)(2,1)S(1)}, bf16[64,4096]{1,0:T(8,128)(2,1)S(1)}, u32[]{:S(2)}, u32[]{:S(2)}) collective-permute-start(bf16[64,4096]{1,0:T(8,128)(2,1)S(1)} %add_convert_fusion.10), channel_id=1, source_target_pairs={{16,0},{17,1},{18,2},{19,3},{20,4},{21,5},{22,6},{23,7},{24,8},{25... | collective-permute-start | bytes 1572872 | tf_op jit(solution)/shard_map/relay_own/ppermute | solution.py:245
  51.1 28.6 %collective-permute-start.7 = (bf16[64,4096]{1,0:T(8,128)(2,1)S(1)}, bf16[64,4096]{1,0:T(8,128)(2,1)S(1)}, u32[]{:S(2)}, u32[]{:S(2)}) collective-permute-start(bf16[64,4096]{1,0:T(8,128)(2,1)S(1)} %add_convert_fusion.17), channel_id=1, source_target_pairs={{2,6},{6,10},{10,14},{14,12},{12,8},{8,4},{4,0},{0,2},{7,3},{11,7}... | collective-permute-start | bytes 1572872 | tf_op jit(solution)/shard_map/reduce_2/ppermute | solution.py:250
  64.3 16.4 %collective-permute-start.12 = (bf16[64,4096]{1,0:T(8,128)(2,1)S(1)}, bf16[64,4096]{1,0:T(8,128)(2,1)S(1)}, u32[]{:S(2)}, u32[]{:S(2)}) collective-permute-start(bf16[64,4096]{1,0:T(8,128)(2,1)S(1)} %get-tuple-element.101), channel_id=1, source_target_pairs={{0,1},{1,0},{2,3},{3,2},{4,5},{5,4},{6,7},{7,6},{8,9},{9,8},{10,11... | collective-permute-start | bytes 1572872 | tf_op jit(solution)/shard_map/give_2/ppermute | solution.py:241
  67.0 27.5 %collective-permute-start.47 = (bf16[64,4096]{1,0:T(8,128)(2,1)S(1)}, bf16[64,4096]{1,0:T(8,128)(2,1)S(1)}, u32[]{:S(2)}, u32[]{:S(2)}) collective-permute-start(bf16[64,4096]{1,0:T(8,128)(2,1)S(1)} %add_convert_fusion.8), channel_id=1, source_target_pairs={{2,6},{6,10},{10,14},{14,12},{12,8},{8,4},{4,0},{0,2},{7,3},{11,7}... | collective-permute-start | bytes 1572872 | tf_op jit(solution)/shard_map/reduce_2/ppermute | solution.py:250
  67.8 27.3 %collective-permute-start.48 = (bf16[64,4096]{1,0:T(8,128)(2,1)S(1)}, bf16[64,4096]{1,0:T(8,128)(2,1)S(1)}, u32[]{:S(2)}, u32[]{:S(2)}) collective-permute-start(bf16[64,4096]{1,0:T(8,128)(2,1)S(1)} %get-tuple-element.142), channel_id=1, source_target_pairs={{0,1},{1,0},{2,3},{3,2},{4,5},{5,4},{6,7},{7,6},{8,9},{9,8},{10,11... | collective-permute-start | bytes 1572872 | tf_op jit(solution)/shard_map/give_2/ppermute | solution.py:241
  88.9 21.1 %collective-permute-start.13 = (bf16[64,4096]{1,0:T(8,128)(2,1)S(1)}, bf16[64,4096]{1,0:T(8,128)(2,1)S(1)}, u32[]{:S(2)}, u32[]{:S(2)}) collective-permute-start(bf16[64,4096]{1,0:T(8,128)(2,1)S(1)} %add_convert_fusion.16), channel_id=1, source_target_pairs={{2,6},{6,10},{10,14},{14,12},{12,8},{8,4},{4,0},{0,2},{7,3},{11,7}... | collective-permute-start | bytes 1572872 | tf_op jit(solution)/shard_map/reduce_3/ppermute | solution.py:250
  97.2 27.6 %collective-permute-start.49 = (bf16[64,4096]{1,0:T(8,128)(2,1)S(1)}, bf16[64,4096]{1,0:T(8,128)(2,1)S(1)}, u32[]{:S(2)}, u32[]{:S(2)}) collective-permute-start(bf16[64,4096]{1,0:T(8,128)(2,1)S(1)} %add_convert_fusion.7), channel_id=1, source_target_pairs={{2,6},{6,10},{10,14},{14,12},{12,8},{8,4},{4,0},{0,2},{7,3},{11,7}... | collective-permute-start | bytes 1572872 | tf_op jit(solution)/shard_map/reduce_3/ppermute | solution.py:250
  98.2 27.1 %collective-permute-start.50 = (bf16[64,4096]{1,0:T(8,128)(2,1)S(1)}, bf16[64,4096]{1,0:T(8,128)(2,1)S(1)}, u32[]{:S(2)}, u32[]{:S(2)}) collective-permute-start(bf16[64,4096]{1,0:T(8,128)(2,1)S(1)} %get-tuple-element.144), channel_id=1, source_target_pairs={{0,1},{1,0},{2,3},{3,2},{4,5},{5,4},{6,7},{7,6},{8,9},{9,8},{10,11... | collective-permute-start | bytes 1572872 | tf_op jit(solution)/shard_map/give_3/ppermute | solution.py:241
  119.2 20.9 %collective-permute-start.19 = (bf16[64,4096]{1,0:T(8,128)(2,1)S(1)}, bf16[64,4096]{1,0:T(8,128)(2,1)S(1)}, u32[]{:S(2)}, u32[]{:S(2)}) collective-permute-start(bf16[64,4096]{1,0:T(8,128)(2,1)S(1)} %add_convert_fusion.15), channel_id=1, source_target_pairs={{2,6},{6,10},{10,14},{14,12},{12,8},{8,4},{4,0},{0,2},{7,3},{11,7}... | collective-permute-start | bytes 1572872 | tf_op jit(solution)/shard_map/reduce_4/ppermute | solution.py:250
  127.5 27.5 %collective-permute-start.51 = (bf16[64,4096]{1,0:T(8,128)(2,1)S(1)}, bf16[64,4096]{1,0:T(8,128)(2,1)S(1)}, u32[]{:S(2)}, u32[]{:S(2)}) collective-permute-start(bf16[64,4096]{1,0:T(8,128)(2,1)S(1)} %add_convert_fusion.6), channel_id=1, source_target_pairs={{2,6},{6,10},{10,14},{14,12},{12,8},{8,4},{4,0},{0,2},{7,3},{11,7}... | collective-permute-start | bytes 1572872 | tf_op jit(solution)/shard_map/reduce_4/ppermute | solution.py:250
  128.4 27.1 %collective-permute-start.52 = (bf16[64,4096]{1,0:T(8,128)(2,1)S(1)}, bf16[64,4096]{1,0:T(8,128)(2,1)S(1)}, u32[]{:S(2)}, u32[]{:S(2)}) collective-permute-start(bf16[64,4096]{1,0:T(8,128)(2,1)S(1)} %get-tuple-element.146), channel_id=1, source_target_pairs={{0,1},{1,0},{2,3},{3,2},{4,5},{5,4},{6,7},{7,6},{8,9},{9,8},{10,11... | collective-permute-start | bytes 1572872 | tf_op jit(solution)/shard_map/give_4/ppermute | solution.py:241
  149.4 21.0 %collective-permute-start.25 = (bf16[64,4096]{1,0:T(8,128)(2,1)S(1)}, bf16[64,4096]{1,0:T(8,128)(2,1)S(1)}, u32[]{:S(2)}, u32[]{:S(2)}) collective-permute-start(bf16[64,4096]{1,0:T(8,128)(2,1)S(1)} %add_convert_fusion.14), channel_id=1, source_target_pairs={{2,6},{6,10},{10,14},{14,12},{12,8},{8,4},{4,0},{0,2},{7,3},{11,7}... | collective-permute-start | bytes 1572872 | tf_op jit(solution)/shard_map/reduce_5/ppermute | solution.py:250
  172.9 18.0 %collective-permute-start.31 = (bf16[64,4096]{1,0:T(8,128)(2,1)S(1)}, bf16[64,4096]{1,0:T(8,128)(2,1)S(1)}, u32[]{:S(2)}, u32[]{:S(2)}) collective-permute-start(bf16[64,4096]{1,0:T(8,128)(2,1)S(1)} %add_convert_fusion.13), channel_id=1, source_target_pairs={{2,6},{6,10},{10,14},{14,12},{12,8},{8,4},{4,0},{0,2},{7,3},{11,7}... | collective-permute-start | bytes 1572872 | tf_op jit(solution)/shard_map/reduce_6/ppermute | solution.py:250
  173.8 17.1 %collective-permute-start.36 = (bf16[64,4096]{1,0:T(8,128)(2,1)S(1)}, bf16[64,4096]{1,0:T(8,128)(2,1)S(1)}, u32[]{:S(2)}, u32[]{:S(2)}) collective-permute-start(bf16[64,4096]{1,0:T(8,128)(2,1)S(1)} %get-tuple-element.129), channel_id=1, source_target_pairs={{0,1},{1,0},{2,3},{3,2},{4,5},{5,4},{6,7},{7,6},{8,9},{9,8},{10,11... | collective-permute-start | bytes 1572872 | tf_op jit(solution)/shard_map/give_6/ppermute | solution.py:241
  179.7 27.1 %collective-permute-start.55 = (bf16[64,4096]{1,0:T(8,128)(2,1)S(1)}, bf16[64,4096]{1,0:T(8,128)(2,1)S(1)}, u32[]{:S(2)}, u32[]{:S(2)}) collective-permute-start(bf16[64,4096]{1,0:T(8,128)(2,1)S(1)} %add_convert_fusion.4), channel_id=1, source_target_pairs={{2,6},{6,10},{10,14},{14,12},{12,8},{8,4},{4,0},{0,2},{7,3},{11,7}... | collective-permute-start | bytes 1572872 | tf_op jit(solution)/shard_map/reduce_6/ppermute | solution.py:250
  185.3 21.6 %collective-permute-start.56 = (bf16[64,4096]{1,0:T(8,128)(2,1)S(1)}, bf16[64,4096]{1,0:T(8,128)(2,1)S(1)}, u32[]{:S(2)}, u32[]{:S(2)}) collective-permute-start(bf16[64,4096]{1,0:T(8,128)(2,1)S(1)} %get-tuple-element.150), channel_id=1, source_target_pairs={{0,1},{1,0},{2,3},{3,2},{4,5},{5,4},{6,7},{7,6},{8,9},{9,8},{10,11... | collective-permute-start | bytes 1572872 | tf_op jit(solution)/shard_map/give_6/ppermute | solution.py:241
  192.8 37.0 %collective-permute-start.61 = (bf16[64,4096]{1,0:T(8,128)(2,1)S(1)}, bf16[64,4096]{1,0:T(8,128)(2,1)S(1)}, u32[]{:S(2)}, u32[]{:S(2)}) collective-permute-start(bf16[64,4096]{1,0:T(8,128)(2,1)S(1)} %add_convert_fusion.1), channel_id=1, source_target_pairs={{16,0},{17,1},{18,2},{19,3},{20,4},{21,5},{22,6},{23,7},{24,8},{25... | collective-permute-start | bytes 1572872 | tf_op jit(solution)/shard_map/relay_own/ppermute | solution.py:245
  209.0 20.7 %collective-permute-start.43 = (bf16[64,4096]{1,0:T(8,128)(2,1)S(1)}, bf16[64,4096]{1,0:T(8,128)(2,1)S(1)}, u32[]{:S(2)}, u32[]{:S(2)}) collective-permute-start(bf16[64,4096]{1,0:T(8,128)(2,1)S(1)} %add_convert_fusion.11), channel_id=1, source_target_pairs={{18,6},{22,10},{26,14},{30,12},{28,8},{24,4},{20,0},{16,2},{23,3},... | collective-permute-start | bytes 1572872 | tf_op jit(solution)/shard_map/relay_last/ppermute | solution.py:253
  216.5 23.9 %collective-permute-start.59 = (bf16[64,4096]{1,0:T(8,128)(2,1)S(1)}, bf16[64,4096]{1,0:T(8,128)(2,1)S(1)}, u32[]{:S(2)}, u32[]{:S(2)}) collective-permute-start(bf16[64,4096]{1,0:T(8,128)(2,1)S(1)} %add_convert_fusion.2), channel_id=1, source_target_pairs={{18,6},{22,10},{26,14},{30,12},{28,8},{24,4},{20,0},{16,2},{23,3},... | collective-permute-start | bytes 1572872 | tf_op jit(solution)/shard_map/relay_last/ppermute | solution.py:253
  (44 other events, 411.2 us)
where the time goes:
time: 243 us; the launch traced here: 242 us
  Pallas kernels  94.6 us (39%)
  waiting for transfers between devices  94 us (39%)
  starting transfers between devices  42.9 us (18%)
  local copies, waits for them, and re-layouts  4.94 us (2%)
  other arithmetic  4.57 us (2%)
    pallas_call x8, Pallas kernels, expert_step(): pl.pallas_call(expert_kernel, in_specs=[pl.BlockSpec(memory_space=pltpu.S...  94.6 us
    ppermute x14, waiting for transfers between devices, body(): blocks.append([lax.ppermute(b, 'expert', onward) for b in blocks[-1]])  50.3 us
    ppermute x2, waiting for transfers between devices, body(): lax.ppermute(r, ('section', 'expert'), relay_onward)  22.5 us
    ppermute x14, starting transfers between devices, body(): blocks.append([lax.ppermute(b, 'expert', onward) for b in blocks[-1]])  15.9 us
    ppermute x12, starting transfers between devices, body(): arrived = [lax.ppermute(r, 'expert', onward) for r in running]  11.9 us
    ppermute x12, waiting for transfers between devices, body(): arrived = [lax.ppermute(r, 'expert', onward) for r in running]  11.7 us
    ppermute x16, waiting for transfers between devices, body(): others.append([lax.ppermute(b, 'expert', swap) for b in blocks[step]])  8.27 us
    all_to_all x1, starting transfers between devices, body(): lax.all_to_all(table, 'expert', split_axis=0, concat_axis=0, tiled=True)  5.27 us
  transfers between devices with their start and end apart: 63, of which 21 were waited for; matrix products, arithmetic and copies ran while one was open for 2% of the time, Pallas kernels for 39%

commit v1 on v0

v1 whole, which is shorter than its diff:
```python
import math

import jax
import jax.numpy as jnp
import numpy as np
from jax import lax
from jax.experimental import pallas as pl
from jax.experimental.pallas import tpu as pltpu
from jax.sharding import PartitionSpec as P


PIECES = 2
HIDDEN_BLOCK = 256
PART = 512
VMEM_LIMIT = 16 << 20
CONTRACT = (((1,), (1,)), ((), ()))


def chip_ring(chips):
    width = 1 << (int(math.log2(chips)) // 2)
    height = chips // width
    tour = []
    for row in range(height):
        columns = list(range(1, width))
        if row % 2:
            columns.reverse()
        tour += [row * width + column for column in columns]
    return tour + [row * width for row in reversed(range(height))]


def origin_table(devices, tour):
    chips = len(tour)
    place = {chip: k for k, chip in enumerate(tour)}
    table = np.zeros((devices, chips, 2), np.int32)
    for device in range(devices):
        at = place[device // 2]
        for step in range(chips):
            by_core = [2 * tour[(at - step) % chips], 2 * tour[(at + step) % chips] + 1]
            table[device, step] = by_core[device % 2], by_core[1 - device % 2]
    return table


def expert_kernel(
    origin, a0, a1, b0, b1, table, saved_gate, saved_up, w_down, w_gate, w_up, mine0, mine1, given0, given1,
    block, entry, gate_rows, up_rows, gate_slope, up_slope, gate_grad, up_grad, scale, out_mine, out_given,
    block_sem, entry_sem, rows_sem, out_sem,
):
    piece, _ = a0.shape
    tokens = 2 * piece
    hidden = w_down.shape[0]
    parts, _, part = out_mine.shape
    capacity = gate_rows.shape[1]

    def block_copy(n):
        return pltpu.make_async_copy((a0, a1, b0, b1)[n], block.at[pl.ds(n * piece, piece)], block_sem.at[n])

    def entry_copy(n):
        return pltpu.make_async_copy(table.at[origin[n]], entry.at[n], entry_sem.at[n])

    def gate_rows_copy(n):
        return pltpu.make_async_copy(saved_gate.at[origin[n]], gate_rows.at[n], rows_sem.at[n])

    def up_rows_copy(n):
        return pltpu.make_async_copy(saved_up.at[origin[n]], up_rows.at[n], rows_sem.at[2 + n])

    for n in range(2):
        entry_copy(n).start()
        gate_rows_copy(n).start()
        up_rows_copy(n).start()
    for n in range(4):
        block_copy(n).start()
    for n in range(2):
        entry_copy(n).wait()
        gate_rows_copy(n).wait()
        up_rows_copy(n).wait()
    for n in range(2):
        rows = pl.ds(n * tokens, tokens)
        place = jnp.broadcast_to(entry[n, 0:1, :], (tokens, tokens)).T
        slot = lax.broadcasted_iota(jnp.int32, (tokens, tokens), 1).astype(jnp.float32)
        pick = jnp.where(place == slot, 1.0, 0.0).astype(jnp.bfloat16)[:, :capacity]
        scale[rows, :] = jnp.broadcast_to(entry[n, 1:2, :], (tokens, tokens)).T
        gate = jnp.dot(pick, gate_rows[n], preferred_element_type=jnp.float32)
        up = jnp.dot(pick, up_rows[n], preferred_element_type=jnp.float32)
        sig = 1.0 / (1.0 + jnp.exp(-gate))
        gate_slope[rows, :] = up * sig * (1.0 + gate * (1.0 - sig))
        up_slope[rows, :] = gate * sig
    for n in range(4):
        block_copy(n).wait()

    for k in range(hidden // HIDDEN_BLOCK):
        columns = pl.ds(k * HIDDEN_BLOCK, HIDDEN_BLOCK)
        hidden_grad = lax.dot_general(block[...], w_down[columns, :], CONTRACT, preferred_element_type=jnp.float32)
        gate_grad[:, columns] = (hidden_grad * gate_slope[:, columns]).astype(jnp.bfloat16)
        up_grad[:, columns] = (hidden_grad * up_slope[:, columns]).astype(jnp.bfloat16)

    outs = (mine0, mine1, given0, given1)

    def out_copy(j, n):
        held = (out_mine, out_mine, out_given, out_given)[n]
        return pltpu.make_async_copy(
            held.at[j, pl.ds((n % 2) * piece, piece)],
            outs[n].at[:, pl.ds(pl.multiple_of(j * part, part), part)],
            out_sem.at[j, n],
        )

    def wide_step(j, carry):
        columns = pl.ds(pl.multiple_of(j * part, part), part)
        back = lax.dot_general(gate_grad[...], w_gate[columns, :], CONTRACT, preferred_element_type=jnp.float32)
        back = back + lax.dot_general(up_grad[...], w_up[columns, :], CONTRACT, preferred_element_type=jnp.float32)
        back = back.astype(jnp.bfloat16).astype(jnp.float32) * scale[:, 0:1]
        out_mine[j] = back[:tokens]
        out_given[j] = back[tokens:].astype(jnp.bfloat16)
        for n in range(4):
            out_copy(j, n).start()
        return carry

    lax.fori_loop(0, parts, wide_step, 0)

    def drain(j, carry):
        for n in range(4):
            out_copy(j, n).wait()
        return carry

    lax.fori_loop(0, parts, drain, 0)


def expert_step(origin, held, other, table, gate_rows, up_rows, w_down, w_gate, w_up):
    piece, width = held[0].shape
    tokens = 2 * piece
    hidden = w_down.shape[0]
    capacity = gate_rows.shape[1]
    parts = width // PART
    anywhere, inside = pl.BlockSpec(memory_space=pl.ANY), pl.BlockSpec(memory_space=pltpu.VMEM)
    bf16, f32 = jnp.bfloat16, jnp.float32
    dma = pltpu.SemaphoreType.DMA
    flops = 2 * 2 * tokens * hidden * width * 3
    moved = 2 * tokens * width * 10
    weights = [pltpu.with_memory_space_constraint(w, pltpu.VMEM) for w in (w_down, w_gate, w_up)]
    return pl.pallas_call(
        expert_kernel,
        in_specs=[pl.BlockSpec(memory_space=pltpu.SMEM)] + [anywhere] * 7 + [inside] * 3,
        out_specs=[anywhere] * 4,
        out_shape=[jax.ShapeDtypeStruct((piece, width), f32)] * 2 + [jax.ShapeDtypeStruct((piece, width), bf16)] * 2,
        scratch_shapes=[
            pltpu.VMEM((2 * tokens, width), bf16),
            pltpu.VMEM((2,) + table.shape[1:], f32),
            pltpu.VMEM((2, capacity, hidden), bf16),
            pltpu.VMEM((2, capacity, hidden), bf16),
            pltpu.VMEM((2 * tokens, hidden), f32),
            pltpu.VMEM((2 * tokens, hidden), f32),
            pltpu.VMEM((2 * tokens, hidden), bf16),
            pltpu.VMEM((2 * tokens, hidden), bf16),
            pltpu.VMEM((2 * tokens, tokens), f32),
            pltpu.VMEM((parts, tokens, PART), f32),
            pltpu.VMEM((parts, tokens, PART), bf16),
            dma((4,)),
            dma((2,)),
            dma((4,)),
            dma((parts, 4)),
        ],
        compiler_params=pltpu.CompilerParams(vmem_limit_bytes=VMEM_LIMIT),
        cost_estimate=pl.CostEstimate(flops=flops, transcendentals=2 * tokens * hidden, bytes_accessed=moved),
        name="expert_step",
    )(origin, *held, *other, table, gate_rows, up_rows, *weights)


def load_kernel(*refs):
    count = len(refs) // 2
    sources, targets, sem = refs[:count], refs[count:2 * count], refs[2 * count]
    copies = [pltpu.make_async_copy(sources[n], targets[n], sem.at[n]) for n in range(count)]
    for copy in copies:
        copy.start()
    for copy in copies:
        copy.wait()


def load_inside(*arrays):
    return pl.pallas_call(
        load_kernel,
        in_specs=[pl.BlockSpec(memory_space=pltpu.HBM)] * len(arrays),
        out_specs=[pl.BlockSpec(memory_space=pltpu.VMEM)] * len(arrays),
        out_shape=[pltpu.VMEM(a.shape, a.dtype) for a in arrays],
        scratch_shapes=[pltpu.SemaphoreType.DMA((len(arrays),))],
        compiler_params=pltpu.CompilerParams(vmem_limit_bytes=VMEM_LIMIT),
        name="load_weights",
    )(*[pltpu.with_memory_space_constraint(a, pltpu.HBM) for a in arrays])


def body(grad_out, expert_ids, gate_weights, saved_gate, saved_up, w_gate, w_up, w_down):
    devices = lax.axis_size("expert")
    sections = lax.axis_size("section")
    chips = devices // 2
    tour = chip_ring(chips)
    following = {chip: tour[(k + 1) % chips] for k, chip in enumerate(tour)}
    onward = [(2 * a, 2 * b) for a, b in following.items()] + [(2 * b + 1, 2 * a + 1) for a, b in following.items()]
    swap = [(i, i ^ 1) for i in range(devices)]
    relay = [(s * devices + i, (s - 1) * devices + i) for s in range(1, sections) for i in range(devices)]
    relay_onward = [(s * devices + a, (s - 1) * devices + b) for s in range(1, sections) for a, b in onward]

    me = lax.axis_index("expert")
    origins = lax.dynamic_index_in_dim(jnp.asarray(origin_table(devices, tour)), me, 0, keepdims=False)

    rows = grad_out[0]
    tokens = rows.shape[0]
    hidden = saved_gate.shape[3]
    capacity = saved_gate.shape[2] // devices
    piece = tokens // PIECES
    first = [rows[h * piece:(h + 1) * piece] for h in range(PIECES)]
    first, routing, weights = lax.optimization_barrier((first, expert_ids[0], gate_weights[0]))

    blocks = [first]
    for _ in range(1, chips):
        blocks.append([lax.ppermute(b, "expert", onward) for b in blocks[-1]])
    others = []
    for step in range(chips):
        others.append([lax.ppermute(b, "expert", swap) for b in blocks[step]])

    experts = jnp.arange(devices, dtype=jnp.int32)
    chosen = routing[:, None, :] == experts[None, :, None]
    named = jnp.any(chosen, axis=2)
    weight_of = jnp.sum(jnp.where(chosen, weights[:, None, :], 0.0), axis=2)
    earlier = jnp.tril(jnp.ones((tokens, tokens), jnp.bfloat16), -1)
    position = lax.dot_general(
        earlier, named.astype(jnp.bfloat16), (((1,), (0,)), ((), ())), preferred_element_type=jnp.float32
    )
    position = jnp.where(named, position, -1.0)
    table = jnp.stack([position.T, weight_of.T], axis=1)
    table = lax.all_to_all(table, "expert", split_axis=0, concat_axis=0, tiled=True)

    gate_rows = saved_gate[0, 0].reshape(devices, capacity, hidden)
    up_rows = saved_up[0, 0].reshape(devices, capacity, hidden)

    matrices, others[0], table = lax.optimization_barrier(((w_down[0, 0], w_gate[0, 0], w_up[0, 0]), others[0], table))
    matrices = load_inside(*matrices)
    running = own = None
    token = origins
    for step in range(chips):
        parts = expert_step(
            token[step], blocks[step], others[step], table, gate_rows, up_rows, *matrices
        )
        token, *parts = lax.optimization_barrier((token, *parts))
        given = [lax.ppermute(p, "expert", swap) for p in parts[PIECES:]]
        total = [a + b.astype(jnp.float32) for a, b in zip(parts[:PIECES], given)]
        if step == 0:
            own = [lax.ppermute(c.astype(jnp.bfloat16), ("section", "expert"), relay) for c in total]
        elif step == 1:
            running = [c.astype(jnp.bfloat16) for c in total]
        else:
            arrived = [lax.ppermute(r, "expert", onward) for r in running]
            running = [(a.astype(jnp.float32) + c).astype(jnp.bfloat16) for a, c in zip(arrived, total)]
    last = [lax.ppermute(r, ("section", "expert"), relay_onward) for r in running]
    result = [(a.astype(jnp.float32) + b.astype(jnp.float32)).astype(jnp.bfloat16) for a, b in zip(last, own)]
    return jnp.concatenate(result, axis=0)[None]


def solution(mesh):
    placed = (
        P("section", "expert", None),
        P("section", "expert", None),
        P("section", "expert", None),
        P("section", "expert", None, None),
        P("section", "expert", None, None),
        P("section", "expert", None, None),
        P("section", "expert", None, None),
        P("section", "expert", None, None),
    )
    return jax.shard_map(body, mesh=mesh, in_specs=placed, out_specs=P("section", "expert", None), check_vma=False)
```

time: 243 us -> 232 us (0.955)
  Pallas kernels: 94.6 us -> 83 us
    pallas_call x8, Pallas kernels: 94.6 us -> 76.4 us  [expert_step(): pl.pallas_call(expert_kernel, in_specs=[pl.BlockSpec(memory_space=pltpu.S...]
    pallas_call x0 -> x1, Pallas kernels: none -> 6.57 us  [load_inside(): pl.pallas_call(load_kernel, in_specs=[pl.BlockSpec(memory_space=pltpu.HBM...]
    all_to_all x1, waiting for transfers between devices: 1 us -> 4.43 us  [body(): lax.all_to_all(table, 'expert', split_axis=0, concat_axis=0, tiled=True)]
    ppermute x14, waiting for transfers between devices: 50.3 us -> 47.5 us  [body(): blocks.append([lax.ppermute(b, 'expert', onward) for b in blocks[-1]])]
  transfers between devices with their start and end apart: 63 -> 63, of which waited for: 21 -> 21; matrix products, arithmetic and copies ran while one was open for 2% -> 3% of each run, Pallas kernels for 39% -> 36%
where the time goes in v1:
time: 232 us; the launch traced here: 231 us
  waiting for transfers between devices  94.7 us (41%)
  Pallas kernels  83 us (36%)
  starting transfers between devices  43.3 us (19%)
  other arithmetic  6.02 us (3%)
  local copies, waits for them, and re-layouts  3.55 us (2%)
    pallas_call x8, Pallas kernels, expert_step(): pl.pallas_call(expert_kernel, in_specs=[pl.BlockSpec(memory_space=pltpu.S...  76.4 us
    ppermute x14, waiting for transfers between devices, body(): blocks.append([lax.ppermute(b, 'expert', onward) for b in blocks[-1]])  47.5 us
    ppermute x2, waiting for transfers between devices, body(): lax.ppermute(r, ('section', 'expert'), relay_onward)  22.4 us
    ppermute x14, starting transfers between devices, body(): blocks.append([lax.ppermute(b, 'expert', onward) for b in blocks[-1]])  15.7 us
    ppermute x12, starting transfers between devices, body(): arrived = [lax.ppermute(r, 'expert', onward) for r in running]  11.9 us
    ppermute x12, waiting for transfers between devices, body(): arrived = [lax.ppermute(r, 'expert', onward) for r in running]  11.7 us
    ppermute x16, waiting for transfers between devices, body(): others.append([lax.ppermute(b, 'expert', swap) for b in blocks[step]])  8.29 us
    pallas_call x1, Pallas kernels, load_inside(): pl.pallas_call(load_kernel, in_specs=[pl.BlockSpec(memory_space=pltpu.HBM...  6.57 us
  transfers between devices with their start and end apart: 63, of which 21 were waited for; matrix products, arithmetic and copies ran while one was open for 3% of the time, Pallas kernels for 36%

profile of v1, /device:TPU:12, one launch (start us, length us, event | category | flops | bytes accessed | tf_op | source)
XLA Modules:
  0.0 231.2 jit_solution(6637874602210742586)
XLA Ops:
  6.9 5.3 %all-to-all-start = ((f32[16,2,128]{2,1,0:T(2,128)}), f32[16,2,128]{2,1,0:T(2,128)S(1)}, u32[]{:S(2)}, u32[]{:S(2)}) async-start(f32[16,2,128]{2,1,0:T(2,128)} %pad_maximum_fusion), calls=%async_computation | async-start | bytes 32768 | tf_op jit(solution)/shard_map/all_to_all | solution.py:228
  12.9 4.4 %all-to-all-done.table = f32[16,2,128]{2,1,0:T(2,128)S(1)} async-done(((f32[16,2,128]{2,1,0:T(2,128)}), f32[16,2,128]{2,1,0:T(2,128)S(1)}, u32[]{:S(2)}, u32[]{:S(2)}) %all-to-all-start) | async-done | bytes 16416 | tf_op jit(solution)/shard_map/all_to_all | solution.py:228
  17.4 6.6 %load_weights.1 = (bf16[768,4096]{1,0:T(8,128)(2,1)S(1)}, bf16[4096,768]{1,0:T(8,128)(2,1)S(1)}, bf16[4096,768]{1,0:T(8,128)(2,1)S(1)}) custom-call(bf16[768,4096]{1,0:T(8,128)(2,1)} %bitcast.39, bf16[4096,768]{1,0:T(8,128)(2,1)} %bitcast.40, bf16[4096,768]{1,0:T(8,128)(2,1)} %bitcast.41), custom_call_target="tpu_custom_call" | custom-call | tf_op jit(solution)/shard_map/load_weights/pallas_call | solution.py:178
  24.7 9.5 %expert_step.8 = (f32[64,4096]{1,0:T(8,128)S(1)}, f32[64,4096]{1,0:T(8,128)S(1)}, bf16[64,4096]{1,0:T(8,128)(2,1)S(1)}, bf16[64,4096]{1,0:T(8,128)(2,1)S(1)}) custom-call(s32[2]{0:T(128)S(1)} %slice_bitcast_fusion.2.origin, bf16[64,4096]{1,0:T(8,128)(2,1)S(1)} %get-tuple-element.89.a0, bf16[64,4096]{1,0:T(8,128)(2,1)S(1)} %get-tuple-element.90.a1, ...), custom_call_target="tpu_custom_call" | custom-call | flops 4831838208 | bytes 10485760 | tf_op jit(solution)/shard_map/expert_step/pallas_call | solution.py:139
  37.4 9.5 %expert_step.9 = (f32[64,4096]{1,0:T(8,128)S(1)}, f32[64,4096]{1,0:T(8,128)S(1)}, bf16[64,4096]{1,0:T(8,128)(2,1)S(1)}, bf16[64,4096]{1,0:T(8,128)(2,1)S(1)}) custom-call(s32[2]{0:T(128)S(1)} %slice_reduce_fusion.6.origin, bf16[64,4096]{1,0:T(8,128)(2,1)S(1)} %collective-permute-done.2.a0, bf16[64,4096]{1,0:T(8,128)(2,1)S(1)} %collective-permute-done.3.a1, ...), custom_call_target="tpu_custom_call" | custom-call | flops 4831838208 | bytes 10485760 | tf_op jit(solution)/shard_map/expert_step/pallas_call | solution.py:139
  47.7 2.0 collective-permute-done.9.a1
  55.2 9.5 %expert_step.10 = (f32[64,4096]{1,0:T(8,128)S(1)}, f32[64,4096]{1,0:T(8,128)S(1)}, bf16[64,4096]{1,0:T(8,128)(2,1)S(1)}, bf16[64,4096]{1,0:T(8,128)(2,1)S(1)}) custom-call(s32[2]{0:T(128)S(1)} %slice_reduce_fusion.5.origin, bf16[64,4096]{1,0:T(8,128)(2,1)S(1)} %collective-permute-done.8.a0, bf16[64,4096]{1,0:T(8,128)(2,1)S(1)} %collective-permute-done.9.a1, ...), custom_call_target="tpu_custom_call" | custom-call | flops 4831838208 | bytes 10485760 | tf_op jit(solution)/shard_map/expert_step/pallas_call | solution.py:139
  68.4 9.5 %expert_step.11 = (f32[64,4096]{1,0:T(8,128)S(1)}, f32[64,4096]{1,0:T(8,128)S(1)}, bf16[64,4096]{1,0:T(8,128)(2,1)S(1)}, bf16[64,4096]{1,0:T(8,128)(2,1)S(1)}) custom-call(s32[2]{0:T(128)S(1)} %slice_reduce_fusion.4.origin, bf16[64,4096]{1,0:T(8,128)(2,1)S(1)} %collective-permute-done.14.a0, bf16[64,4096]{1,0:T(8,128)(2,1)S(1)} %collective-permute-done.15.a1, ...), custom_call_target="tpu_custom_call" | custom-call | flops 4831838208 | bytes 10485760 | tf_op jit(solution)/shard_map/expert_step/pallas_call | solution.py:139
  80.1 7.1 %collective-permute-done.20.a0 = bf16[64,4096]{1,0:T(8,128)(2,1)S(1)} collective-permute-done((bf16[64,4096]{1,0:T(8,128)(2,1)S(1)}, bf16[64,4096]{1,0:T(8,128)(2,1)S(1)}, u32[]{:S(2)}, u32[]{:S(2)}) %collective-permute-start.20) | collective-permute-done | bytes 524320 | tf_op jit(solution)/shard_map/ppermute | solution.py:213
  88.2 4.6 %collective-permute-done.21.a1 = bf16[64,4096]{1,0:T(8,128)(2,1)S(1)} collective-permute-done((bf16[64,4096]{1,0:T(8,128)(2,1)S(1)}, bf16[64,4096]{1,0:T(8,128)(2,1)S(1)}, u32[]{:S(2)}, u32[]{:S(2)}) %collective-permute-start.21) | collective-permute-done | bytes 524320 | tf_op jit(solution)/shard_map/ppermute | solution.py:213
  96.5 9.6 %expert_step.12 = (f32[64,4096]{1,0:T(8,128)S(1)}, f32[64,4096]{1,0:T(8,128)S(1)}, bf16[64,4096]{1,0:T(8,128)(2,1)S(1)}, bf16[64,4096]{1,0:T(8,128)(2,1)S(1)}) custom-call(s32[2]{0:T(128)S(1)} %slice_reduce_fusion.3.origin, bf16[64,4096]{1,0:T(8,128)(2,1)S(1)} %collective-permute-done.20.a0, bf16[64,4096]{1,0:T(8,128)(2,1)S(1)} %collective-permute-done.21.a1, ...), custom_call_target="tpu_custom_call" | custom-call | flops 4831838208 | bytes 10485760 | tf_op jit(solution)/shard_map/expert_step/pallas_call | solution.py:139
  108.2 7.1 %collective-permute-done.26.a0 = bf16[64,4096]{1,0:T(8,128)(2,1)S(1)} collective-permute-done((bf16[64,4096]{1,0:T(8,128)(2,1)S(1)}, bf16[64,4096]{1,0:T(8,128)(2,1)S(1)}, u32[]{:S(2)}, u32[]{:S(2)}) %collective-permute-start.26) | collective-permute-done | bytes 524320 | tf_op jit(solution)/shard_map/ppermute | solution.py:213
  116.2 4.7 %collective-permute-done.27.a1 = bf16[64,4096]{1,0:T(8,128)(2,1)S(1)} collective-permute-done((bf16[64,4096]{1,0:T(8,128)(2,1)S(1)}, bf16[64,4096]{1,0:T(8,128)(2,1)S(1)}, u32[]{:S(2)}, u32[]{:S(2)}) %collective-permute-start.27) | collective-permute-done | bytes 524320 | tf_op jit(solution)/shard_map/ppermute | solution.py:213
  124.5 9.5 %expert_step.13 = (f32[64,4096]{1,0:T(8,128)S(1)}, f32[64,4096]{1,0:T(8,128)S(1)}, bf16[64,4096]{1,0:T(8,128)(2,1)S(1)}, bf16[64,4096]{1,0:T(8,128)(2,1)S(1)}) custom-call(s32[2]{0:T(128)S(1)} %slice_reduce_fusion.2.origin, bf16[64,4096]{1,0:T(8,128)(2,1)S(1)} %collective-permute-done.26.a0, bf16[64,4096]{1,0:T(8,128)(2,1)S(1)} %collective-permute-done.27.a1, ...), custom_call_target="tpu_custom_call" | custom-call | flops 4831838208 | bytes 10485760 | tf_op jit(solution)/shard_map/expert_step/pallas_call | solution.py:139
  136.3 7.0 %collective-permute-done.32.a0 = bf16[64,4096]{1,0:T(8,128)(2,1)S(1)} collective-permute-done((bf16[64,4096]{1,0:T(8,128)(2,1)S(1)}, bf16[64,4096]{1,0:T(8,128)(2,1)S(1)}, u32[]{:S(2)}, u32[]{:S(2)}) %collective-permute-start.32) | collective-permute-done | bytes 524320 | tf_op jit(solution)/shard_map/ppermute | solution.py:213
  144.3 4.6 %collective-permute-done.33.a1 = bf16[64,4096]{1,0:T(8,128)(2,1)S(1)} collective-permute-done((bf16[64,4096]{1,0:T(8,128)(2,1)S(1)}, bf16[64,4096]{1,0:T(8,128)(2,1)S(1)}, u32[]{:S(2)}, u32[]{:S(2)}) %collective-permute-start.33) | collective-permute-done | bytes 524320 | tf_op jit(solution)/shard_map/ppermute | solution.py:213
  152.6 9.5 %expert_step.14 = (f32[64,4096]{1,0:T(8,128)S(1)}, f32[64,4096]{1,0:T(8,128)S(1)}, bf16[64,4096]{1,0:T(8,128)(2,1)S(1)}, bf16[64,4096]{1,0:T(8,128)(2,1)S(1)}) custom-call(s32[2]{0:T(128)S(1)} %slice_reduce_fusion.1.origin, bf16[64,4096]{1,0:T(8,128)(2,1)S(1)} %collective-permute-done.32.a0, bf16[64,4096]{1,0:T(8,128)(2,1)S(1)} %collective-permute-done.33.a1, ...), custom_call_target="tpu_custom_call" | custom-call | flops 4831838208 | bytes 10485760 | tf_op jit(solution)/shard_map/expert_step/pallas_call | solution.py:139
  165.7 5.7 %collective-permute-done.38.a0 = bf16[64,4096]{1,0:T(8,128)(2,1)S(1)} collective-permute-done((bf16[64,4096]{1,0:T(8,128)(2,1)S(1)}, bf16[64,4096]{1,0:T(8,128)(2,1)S(1)}, u32[]{:S(2)}, u32[]{:S(2)}) %collective-permute-start.38) | collective-permute-done | bytes 524320 | tf_op jit(solution)/shard_map/ppermute | solution.py:213
  172.4 4.6 %collective-permute-done.39.a1 = bf16[64,4096]{1,0:T(8,128)(2,1)S(1)} collective-permute-done((bf16[64,4096]{1,0:T(8,128)(2,1)S(1)}, bf16[64,4096]{1,0:T(8,128)(2,1)S(1)}, u32[]{:S(2)}, u32[]{:S(2)}) %collective-permute-start.39) | collective-permute-done | bytes 524320 | tf_op jit(solution)/shard_map/ppermute | solution.py:213
  177.0 5.6 %collective-permute-done.31 = bf16[64,4096]{1,0:T(8,128)(2,1)S(1)} collective-permute-done((bf16[64,4096]{1,0:T(8,128)(2,1)S(1)}, bf16[64,4096]{1,0:T(8,128)(2,1)S(1)}, u32[]{:S(2)}, u32[]{:S(2)}) %collective-permute-start.31) | collective-permute-done | bytes 524320 | tf_op jit(solution)/shard_map/ppermute | solution.py:249
  186.9 9.5 %expert_step.15 = (f32[64,4096]{1,0:T(8,128)S(1)}, f32[64,4096]{1,0:T(8,128)S(1)}, bf16[64,4096]{1,0:T(8,128)(2,1)S(1)}, bf16[64,4096]{1,0:T(8,128)(2,1)S(1)}) custom-call(s32[2]{0:T(128)S(1)} %slice_reduce_fusion.origin, bf16[64,4096]{1,0:T(8,128)(2,1)S(1)} %collective-permute-done.38.a0, bf16[64,4096]{1,0:T(8,128)(2,1)S(1)} %collective-permute-done.39.a1, ...), custom_call_target="tpu_custom_call" | custom-call | flops 4831838208 | bytes 10485760 | tf_op jit(solution)/shard_map/expert_step/pallas_call | solution.py:139
  199.9 6.0 %collective-permute-done.57 = bf16[64,4096]{1,0:T(8,128)(2,1)S(1)} collective-permute-done((bf16[64,4096]{1,0:T(8,128)(2,1)S(1)}, bf16[64,4096]{1,0:T(8,128)(2,1)S(1)}, u32[]{:S(2)}, u32[]{:S(2)}) %collective-permute-start.57) | collective-permute-done | bytes 524320 | tf_op jit(solution)/shard_map/ppermute | solution.py:249
  207.4 11.8 %collective-permute-done.43 = bf16[64,4096]{1,0:T(8,128)(2,1)S(1)} collective-permute-done((bf16[64,4096]{1,0:T(8,128)(2,1)S(1)}, bf16[64,4096]{1,0:T(8,128)(2,1)S(1)}, u32[]{:S(2)}, u32[]{:S(2)}) %collective-permute-start.43) | collective-permute-done | bytes 524320 | tf_op jit(solution)/shard_map/ppermute | solution.py:251
  219.4 10.6 %collective-permute-done.59 = bf16[64,4096]{1,0:T(8,128)(2,1)S(1)} collective-permute-done((bf16[64,4096]{1,0:T(8,128)(2,1)S(1)}, bf16[64,4096]{1,0:T(8,128)(2,1)S(1)}, u32[]{:S(2)}, u32[]{:S(2)}) %collective-permute-start.59) | collective-permute-done | bytes 524320 | tf_op jit(solution)/shard_map/ppermute | solution.py:251
  (150 shorter events, 56.6 us)
Async XLA Ops:
  1.3 16.1 %collective-permute-start = (bf16[64,4096]{1,0:T(8,128)(2,1)S(1)}, bf16[64,4096]{1,0:T(8,128)(2,1)S(1)}, u32[]{:S(2)}, u32[]{:S(2)}) collective-permute-start(bf16[64,4096]{1,0:T(8,128)(2,1)S(1)} %get-tuple-element.89.a0), channel_id=1, source_target_pairs={{0,1},{1,0},{2,3},{3,2},{4,5},{5,4},{6,7},{7,6},{8,9},{9,8},{10,11... | collective-permute-start | bytes 1572872 | tf_op jit(solution)/shard_map/ppermute | solution.py:216
  1.4 22.6 %collective-permute-start.2 = (bf16[64,4096]{1,0:T(8,128)(2,1)S(1)}, bf16[64,4096]{1,0:T(8,128)(2,1)S(1)}, u32[]{:S(2)}, u32[]{:S(2)}) collective-permute-start(bf16[64,4096]{1,0:T(8,128)(2,1)S(1)} %get-tuple-element.89.a0), channel_id=1, source_target_pairs={{2,6},{6,10},{10,14},{14,12},{12,8},{8,4},{4,0},{0,2},{7,3},{11,7}... | collective-permute-start | bytes 1572872 | tf_op jit(solution)/shard_map/ppermute | solution.py:213
  3.0 21.1 %collective-permute-start.3 = (bf16[64,4096]{1,0:T(8,128)(2,1)S(1)}, bf16[64,4096]{1,0:T(8,128)(2,1)S(1)}, u32[]{:S(2)}, u32[]{:S(2)}) collective-permute-start(bf16[64,4096]{1,0:T(8,128)(2,1)S(1)} %get-tuple-element.90.a1), channel_id=1, source_target_pairs={{2,6},{6,10},{10,14},{14,12},{12,8},{8,4},{4,0},{0,2},{7,3},{11,7}... | collective-permute-start | bytes 1572872 | tf_op jit(solution)/shard_map/ppermute | solution.py:213
  34.5 16.0 %collective-permute-start.60 = (bf16[64,4096]{1,0:T(8,128)(2,1)S(1)}, bf16[64,4096]{1,0:T(8,128)(2,1)S(1)}, u32[]{:S(2)}, u32[]{:S(2)}) collective-permute-start(bf16[64,4096]{1,0:T(8,128)(2,1)S(1)} %get-tuple-element.172), channel_id=1, source_target_pairs={{0,1},{1,0},{2,3},{3,2},{4,5},{5,4},{6,7},{7,6},{8,9},{9,8},{10,11... | collective-permute-start | bytes 1572872 | tf_op jit(solution)/shard_map/ppermute | solution.py:242
  47.0 18.4 %collective-permute-start.46 = (bf16[64,4096]{1,0:T(8,128)(2,1)S(1)}, bf16[64,4096]{1,0:T(8,128)(2,1)S(1)}, u32[]{:S(2)}, u32[]{:S(2)}) collective-permute-start(bf16[64,4096]{1,0:T(8,128)(2,1)S(1)} %get-tuple-element.158), channel_id=1, source_target_pairs={{0,1},{1,0},{2,3},{3,2},{4,5},{5,4},{6,7},{7,6},{8,9},{9,8},{10,11... | collective-permute-start | bytes 1572872 | tf_op jit(solution)/shard_map/ppermute | solution.py:242
  49.7 15.1 %collective-permute-start.14 = (bf16[64,4096]{1,0:T(8,128)(2,1)S(1)}, bf16[64,4096]{1,0:T(8,128)(2,1)S(1)}, u32[]{:S(2)}, u32[]{:S(2)}) collective-permute-start(bf16[64,4096]{1,0:T(8,128)(2,1)S(1)} %collective-permute-done.8.a0), channel_id=1, source_target_pairs={{2,6},{6,10},{10,14},{14,12},{12,8},{8,4},{4,0},{0,2},{7,3},{11,7}... | collective-permute-start | bytes 1572872 | tf_op jit(solution)/shard_map/ppermute | solution.py:213
  52.4 155.1 %collective-permute-start.45 = (bf16[64,4096]{1,0:T(8,128)(2,1)S(1)}, bf16[64,4096]{1,0:T(8,128)(2,1)S(1)}, u32[]{:S(2)}, u32[]{:S(2)}) collective-permute-start(bf16[64,4096]{1,0:T(8,128)(2,1)S(1)} %add_convert_fusion.10), channel_id=1, source_target_pairs={{16,0},{17,1},{18,2},{19,3},{20,4},{21,5},{22,6},{23,7},{24,8},{25... | collective-permute-start | bytes 1572872 | tf_op jit(solution)/shard_map/ppermute | solution.py:245
  53.7 24.3 %collective-permute-start.7 = (bf16[64,4096]{1,0:T(8,128)(2,1)S(1)}, bf16[64,4096]{1,0:T(8,128)(2,1)S(1)}, u32[]{:S(2)}, u32[]{:S(2)}) collective-permute-start(bf16[64,4096]{1,0:T(8,128)(2,1)S(1)} %add_convert_fusion.17), channel_id=1, source_target_pairs={{2,6},{6,10},{10,14},{14,12},{12,8},{8,4},{4,0},{0,2},{7,3},{11,7}... | collective-permute-start | bytes 1572872 | tf_op jit(solution)/shard_map/ppermute | solution.py:249
  67.5 25.3 %collective-permute-start.47 = (bf16[64,4096]{1,0:T(8,128)(2,1)S(1)}, bf16[64,4096]{1,0:T(8,128)(2,1)S(1)}, u32[]{:S(2)}, u32[]{:S(2)}) collective-permute-start(bf16[64,4096]{1,0:T(8,128)(2,1)S(1)} %add_convert_fusion.8), channel_id=1, source_target_pairs={{2,6},{6,10},{10,14},{14,12},{12,8},{8,4},{4,0},{0,2},{7,3},{11,7}... | collective-permute-start | bytes 1572872 | tf_op jit(solution)/shard_map/ppermute | solution.py:249
  68.3 25.1 %collective-permute-start.48 = (bf16[64,4096]{1,0:T(8,128)(2,1)S(1)}, bf16[64,4096]{1,0:T(8,128)(2,1)S(1)}, u32[]{:S(2)}, u32[]{:S(2)}) collective-permute-start(bf16[64,4096]{1,0:T(8,128)(2,1)S(1)} %get-tuple-element.160), channel_id=1, source_target_pairs={{0,1},{1,0},{2,3},{3,2},{4,5},{5,4},{6,7},{7,6},{8,9},{9,8},{10,11... | collective-permute-start | bytes 1572872 | tf_op jit(solution)/shard_map/ppermute | solution.py:242
  87.2 18.9 %collective-permute-start.13 = (bf16[64,4096]{1,0:T(8,128)(2,1)S(1)}, bf16[64,4096]{1,0:T(8,128)(2,1)S(1)}, u32[]{:S(2)}, u32[]{:S(2)}) collective-permute-start(bf16[64,4096]{1,0:T(8,128)(2,1)S(1)} %add_convert_fusion.16), channel_id=1, source_target_pairs={{2,6},{6,10},{10,14},{14,12},{12,8},{8,4},{4,0},{0,2},{7,3},{11,7}... | collective-permute-start | bytes 1572872 | tf_op jit(solution)/shard_map/ppermute | solution.py:249
  95.5 25.4 %collective-permute-start.49 = (bf16[64,4096]{1,0:T(8,128)(2,1)S(1)}, bf16[64,4096]{1,0:T(8,128)(2,1)S(1)}, u32[]{:S(2)}, u32[]{:S(2)}) collective-permute-start(bf16[64,4096]{1,0:T(8,128)(2,1)S(1)} %add_convert_fusion.7), channel_id=1, source_target_pairs={{2,6},{6,10},{10,14},{14,12},{12,8},{8,4},{4,0},{0,2},{7,3},{11,7}... | collective-permute-start | bytes 1572872 | tf_op jit(solution)/shard_map/ppermute | solution.py:249
  96.5 24.9 %collective-permute-start.50 = (bf16[64,4096]{1,0:T(8,128)(2,1)S(1)}, bf16[64,4096]{1,0:T(8,128)(2,1)S(1)}, u32[]{:S(2)}, u32[]{:S(2)}) collective-permute-start(bf16[64,4096]{1,0:T(8,128)(2,1)S(1)} %get-tuple-element.162), channel_id=1, source_target_pairs={{0,1},{1,0},{2,3},{3,2},{4,5},{5,4},{6,7},{7,6},{8,9},{9,8},{10,11... | collective-permute-start | bytes 1572872 | tf_op jit(solution)/shard_map/ppermute | solution.py:242
  115.3 18.8 %collective-permute-start.19 = (bf16[64,4096]{1,0:T(8,128)(2,1)S(1)}, bf16[64,4096]{1,0:T(8,128)(2,1)S(1)}, u32[]{:S(2)}, u32[]{:S(2)}) collective-permute-start(bf16[64,4096]{1,0:T(8,128)(2,1)S(1)} %add_convert_fusion.15), channel_id=1, source_target_pairs={{2,6},{6,10},{10,14},{14,12},{12,8},{8,4},{4,0},{0,2},{7,3},{11,7}... | collective-permute-start | bytes 1572872 | tf_op jit(solution)/shard_map/ppermute | solution.py:249
  123.6 25.3 %collective-permute-start.51 = (bf16[64,4096]{1,0:T(8,128)(2,1)S(1)}, bf16[64,4096]{1,0:T(8,128)(2,1)S(1)}, u32[]{:S(2)}, u32[]{:S(2)}) collective-permute-start(bf16[64,4096]{1,0:T(8,128)(2,1)S(1)} %add_convert_fusion.6), channel_id=1, source_target_pairs={{2,6},{6,10},{10,14},{14,12},{12,8},{8,4},{4,0},{0,2},{7,3},{11,7}... | collective-permute-start | bytes 1572872 | tf_op jit(solution)/shard_map/ppermute | solution.py:249
  124.5 24.9 %collective-permute-start.52 = (bf16[64,4096]{1,0:T(8,128)(2,1)S(1)}, bf16[64,4096]{1,0:T(8,128)(2,1)S(1)}, u32[]{:S(2)}, u32[]{:S(2)}) collective-permute-start(bf16[64,4096]{1,0:T(8,128)(2,1)S(1)} %get-tuple-element.164), channel_id=1, source_target_pairs={{0,1},{1,0},{2,3},{3,2},{4,5},{5,4},{6,7},{7,6},{8,9},{9,8},{10,11... | collective-permute-start | bytes 1572872 | tf_op jit(solution)/shard_map/ppermute | solution.py:242
  143.3 18.8 %collective-permute-start.25 = (bf16[64,4096]{1,0:T(8,128)(2,1)S(1)}, bf16[64,4096]{1,0:T(8,128)(2,1)S(1)}, u32[]{:S(2)}, u32[]{:S(2)}) collective-permute-start(bf16[64,4096]{1,0:T(8,128)(2,1)S(1)} %add_convert_fusion.14), channel_id=1, source_target_pairs={{2,6},{6,10},{10,14},{14,12},{12,8},{8,4},{4,0},{0,2},{7,3},{11,7}... | collective-permute-start | bytes 1572872 | tf_op jit(solution)/shard_map/ppermute | solution.py:249
  164.4 18.2 %collective-permute-start.31 = (bf16[64,4096]{1,0:T(8,128)(2,1)S(1)}, bf16[64,4096]{1,0:T(8,128)(2,1)S(1)}, u32[]{:S(2)}, u32[]{:S(2)}) collective-permute-start(bf16[64,4096]{1,0:T(8,128)(2,1)S(1)} %add_convert_fusion.13), channel_id=1, source_target_pairs={{2,6},{6,10},{10,14},{14,12},{12,8},{8,4},{4,0},{0,2},{7,3},{11,7}... | collective-permute-start | bytes 1572872 | tf_op jit(solution)/shard_map/ppermute | solution.py:249
  165.3 17.3 %collective-permute-start.36 = (bf16[64,4096]{1,0:T(8,128)(2,1)S(1)}, bf16[64,4096]{1,0:T(8,128)(2,1)S(1)}, u32[]{:S(2)}, u32[]{:S(2)}) collective-permute-start(bf16[64,4096]{1,0:T(8,128)(2,1)S(1)} %get-tuple-element.147), channel_id=1, source_target_pairs={{0,1},{1,0},{2,3},{3,2},{4,5},{5,4},{6,7},{7,6},{8,9},{9,8},{10,11... | collective-permute-start | bytes 1572872 | tf_op jit(solution)/shard_map/ppermute | solution.py:242
  171.4 25.0 %collective-permute-start.55 = (bf16[64,4096]{1,0:T(8,128)(2,1)S(1)}, bf16[64,4096]{1,0:T(8,128)(2,1)S(1)}, u32[]{:S(2)}, u32[]{:S(2)}) collective-permute-start(bf16[64,4096]{1,0:T(8,128)(2,1)S(1)} %add_convert_fusion.4), channel_id=1, source_target_pairs={{2,6},{6,10},{10,14},{14,12},{12,8},{8,4},{4,0},{0,2},{7,3},{11,7}... | collective-permute-start | bytes 1572872 | tf_op jit(solution)/shard_map/ppermute | solution.py:249
  177.0 19.5 %collective-permute-start.56 = (bf16[64,4096]{1,0:T(8,128)(2,1)S(1)}, bf16[64,4096]{1,0:T(8,128)(2,1)S(1)}, u32[]{:S(2)}, u32[]{:S(2)}) collective-permute-start(bf16[64,4096]{1,0:T(8,128)(2,1)S(1)} %get-tuple-element.168), channel_id=1, source_target_pairs={{0,1},{1,0},{2,3},{3,2},{4,5},{5,4},{6,7},{7,6},{8,9},{9,8},{10,11... | collective-permute-start | bytes 1572872 | tf_op jit(solution)/shard_map/ppermute | solution.py:242
  184.5 34.9 %collective-permute-start.61 = (bf16[64,4096]{1,0:T(8,128)(2,1)S(1)}, bf16[64,4096]{1,0:T(8,128)(2,1)S(1)}, u32[]{:S(2)}, u32[]{:S(2)}) collective-permute-start(bf16[64,4096]{1,0:T(8,128)(2,1)S(1)} %add_convert_fusion.1), channel_id=1, source_target_pairs={{16,0},{17,1},{18,2},{19,3},{20,4},{21,5},{22,6},{23,7},{24,8},{25... | collective-permute-start | bytes 1572872 | tf_op jit(solution)/shard_map/ppermute | solution.py:245
  198.6 20.7 %collective-permute-start.43 = (bf16[64,4096]{1,0:T(8,128)(2,1)S(1)}, bf16[64,4096]{1,0:T(8,128)(2,1)S(1)}, u32[]{:S(2)}, u32[]{:S(2)}) collective-permute-start(bf16[64,4096]{1,0:T(8,128)(2,1)S(1)} %add_convert_fusion.11), channel_id=1, source_target_pairs={{18,6},{22,10},{26,14},{30,12},{28,8},{24,4},{20,0},{16,2},{23,3},... | collective-permute-start | bytes 1572872 | tf_op jit(solution)/shard_map/ppermute | solution.py:251
  206.1 23.9 %collective-permute-start.59 = (bf16[64,4096]{1,0:T(8,128)(2,1)S(1)}, bf16[64,4096]{1,0:T(8,128)(2,1)S(1)}, u32[]{:S(2)}, u32[]{:S(2)}) collective-permute-start(bf16[64,4096]{1,0:T(8,128)(2,1)S(1)} %add_convert_fusion.2), channel_id=1, source_target_pairs={{18,6},{22,10},{26,14},{30,12},{28,8},{24,4},{20,0},{16,2},{23,3},... | collective-permute-start | bytes 1572872 | tf_op jit(solution)/shard_map/ppermute | solution.py:251
  (41 other events, 363.6 us)

commit v2 on v1

--- a/solution.py
+++ b/solution.py
@@ -11,7 +11,7 @@
 
 PIECES = 2
 HIDDEN_BLOCK = 256
-PART = 512
+PART = 1024
 VMEM_LIMIT = 16 << 20
 CONTRACT = (((1,), (1,)), ((), ()))
 
@@ -41,8 +41,8 @@
 
 
 def expert_kernel(
-    origin, a0, a1, b0, b1, table, saved_gate, saved_up, w_down, w_gate, w_up, mine0, mine1, given0, given1,
-    block, entry, gate_rows, up_rows, gate_slope, up_slope, gate_grad, up_grad, scale, out_mine, out_given,
+    origin, a0, a1, b0, b1, table, saved_gate, saved_up, w_down, w_wide, mine, given,
+    block, entry, gate_rows, up_rows, gate_slope, up_slope, joined_grad, scale, out_mine, out_given,
     block_sem, entry_sem, rows_sem, out_sem,
 ):
     piece, _ = a0.shape
@@ -90,41 +90,38 @@
     for k in range(hidden // HIDDEN_BLOCK):
         columns = pl.ds(k * HIDDEN_BLOCK, HIDDEN_BLOCK)
         hidden_grad = lax.dot_general(block[...], w_down[columns, :], CONTRACT, preferred_element_type=jnp.float32)
-        gate_grad[:, columns] = (hidden_grad * gate_slope[:, columns]).astype(jnp.bfloat16)
-        up_grad[:, columns] = (hidden_grad * up_slope[:, columns]).astype(jnp.bfloat16)
-
-    outs = (mine0, mine1, given0, given1)
+        joined_grad[:, columns] = (hidden_grad * gate_slope[:, columns]).astype(jnp.bfloat16)
+        up_columns = pl.ds(hidden + k * HIDDEN_BLOCK, HIDDEN_BLOCK)
+        joined_grad[:, up_columns] = (hidden_grad * up_slope[:, columns]).astype(jnp.bfloat16)
+
+    outs = (mine, given)
 
     def out_copy(j, n):
-        held = (out_mine, out_mine, out_given, out_given)[n]
-        return pltpu.make_async_copy(
-            held.at[j, pl.ds((n % 2) * piece, piece)],
-            outs[n].at[:, pl.ds(pl.multiple_of(j * part, part), part)],
-            out_sem.at[j, n],
-        )
+        columns = pl.ds(pl.multiple_of(j * part, part), part)
+        return pltpu.make_async_copy((out_mine, out_given)[n].at[j], outs[n].at[:, columns], out_sem.at[j, n])
 
     def wide_step(j, carry):
         columns = pl.ds(pl.multiple_of(j * part, part), part)
-        back = lax.dot_general(gate_grad[...], w_gate[columns, :], CONTRACT, preferred_element_type=jnp.float32)
-        back = back + lax.dot_general(up_grad[...], w_up[columns, :], CONTRACT, preferred_element_type=jnp.float32)
-        back = back.astype(jnp.bfloat16).astype(jnp.float32) * scale[:, 0:1]
+        back = lax.dot_general(joined_grad[...], w_wide[columns, :], CONTRACT, preferred_element_type=jnp.float32)
+        weight = jnp.concatenate([scale[...]] * (part // tokens), axis=1)
+        back = back.astype(jnp.bfloat16).astype(jnp.float32) * weight
         out_mine[j] = back[:tokens]
         out_given[j] = back[tokens:].astype(jnp.bfloat16)
-        for n in range(4):
+        for n in range(2):
             out_copy(j, n).start()
         return carry
 
     lax.fori_loop(0, parts, wide_step, 0)
 
     def drain(j, carry):
-        for n in range(4):
+        for n in range(2):
             out_copy(j, n).wait()
         return carry
 
     lax.fori_loop(0, parts, drain, 0)
 
 
-def expert_step(origin, held, other, table, gate_rows, up_rows, w_down, w_gate, w_up):
+def expert_step(origin, held, other, table, gate_rows, up_rows, w_down, w_wide):
     piece, width = held[0].shape
     tokens = 2 * piece
     hidden = w_down.shape[0]
@@ -135,12 +132,12 @@
     dma = pltpu.SemaphoreType.DMA
     flops = 2 * 2 * tokens * hidden * width * 3
     moved = 2 * tokens * width * 10
-    weights = [pltpu.with_memory_space_constraint(w, pltpu.VMEM) for w in (w_down, w_gate, w_up)]
+    weights = [pltpu.with_memory_space_constraint(w, pltpu.VMEM) for w in (w_down, w_wide)]
     return pl.pallas_call(
         expert_kernel,
-        in_specs=[pl.BlockSpec(memory_space=pltpu.SMEM)] + [anywhere] * 7 + [inside] * 3,
-        out_specs=[anywhere] * 4,
-        out_shape=[jax.ShapeDtypeStruct((piece, width), f32)] * 2 + [jax.ShapeDtypeStruct((piece, width), bf16)] * 2,
+        in_specs=[pl.BlockSpec(memory_space=pltpu.SMEM)] + [anywhere] * 7 + [inside] * 2,
+        out_specs=[anywhere] * 2,
+        out_shape=[jax.ShapeDtypeStruct((tokens, width), f32), jax.ShapeDtypeStruct((tokens, width), bf16)],
         scratch_shapes=[
             pltpu.VMEM((2 * tokens, width), bf16),
             pltpu.VMEM((2,) + table.shape[1:], f32),
@@ -148,15 +145,14 @@
             pltpu.VMEM((2, capacity, hidden), bf16),
             pltpu.VMEM((2 * tokens, hidden), f32),
             pltpu.VMEM((2 * tokens, hidden), f32),
-            pltpu.VMEM((2 * tokens, hidden), bf16),
-            pltpu.VMEM((2 * tokens, hidden), bf16),
+            pltpu.VMEM((2 * tokens, 2 * hidden), bf16),
             pltpu.VMEM((2 * tokens, tokens), f32),
             pltpu.VMEM((parts, tokens, PART), f32),
             pltpu.VMEM((parts, tokens, PART), bf16),
             dma((4,)),
             dma((2,)),
             dma((4,)),
-            dma((parts, 4)),
+            dma((parts, 2)),
         ],
         compiler_params=pltpu.CompilerParams(vmem_limit_bytes=VMEM_LIMIT),
         cost_estimate=pl.CostEstimate(flops=flops, transcendentals=2 * tokens * hidden, bytes_accessed=moved),
@@ -164,10 +160,13 @@
     )(origin, *held, *other, table, gate_rows, up_rows, *weights)
 
 
-def load_kernel(*refs):
-    count = len(refs) // 2
-    sources, targets, sem = refs[:count], refs[count:2 * count], refs[2 * count]
-    copies = [pltpu.make_async_copy(sources[n], targets[n], sem.at[n]) for n in range(count)]
+def load_kernel(w_down, w_gate, w_up, down, wide, sem):
+    hidden = w_gate.shape[1]
+    copies = [
+        pltpu.make_async_copy(w_down, down, sem.at[0]),
+        pltpu.make_async_copy(w_gate, wide.at[:, pl.ds(0, hidden)], sem.at[1]),
+        pltpu.make_async_copy(w_up, wide.at[:, pl.ds(hidden, hidden)], sem.at[2]),
+    ]
     for copy in copies:
         copy.start()
     for copy in copies:
@@ -175,12 +174,16 @@
 
 
 def load_inside(*arrays):
+    w_down, w_gate, w_up = arrays
     return pl.pallas_call(
         load_kernel,
-        in_specs=[pl.BlockSpec(memory_space=pltpu.HBM)] * len(arrays),
-        out_specs=[pl.BlockSpec(memory_space=pltpu.VMEM)] * len(arrays),
-        out_shape=[pltpu.VMEM(a.shape, a.dtype) for a in arrays],
-        scratch_shapes=[pltpu.SemaphoreType.DMA((len(arrays),))],
+        in_specs=[pl.BlockSpec(memory_space=pltpu.HBM)] * 3,
+        out_specs=[pl.BlockSpec(memory_space=pltpu.VMEM)] * 2,
+        out_shape=[
+            pltpu.VMEM(w_down.shape, w_down.dtype),
+            pltpu.VMEM((w_gate.shape[0], w_gate.shape[1] + w_up.shape[1]), w_gate.dtype),
+        ],
+        scratch_shapes=[pltpu.SemaphoreType.DMA((3,))],
         compiler_params=pltpu.CompilerParams(vmem_limit_bytes=VMEM_LIMIT),
         name="load_weights",
     )(*[pltpu.with_memory_space_constraint(a, pltpu.HBM) for a in arrays])
@@ -232,22 +235,29 @@
 
     matrices, others[0], table = lax.optimization_barrier(((w_down[0, 0], w_gate[0, 0], w_up[0, 0]), others[0], table))
     matrices = load_inside(*matrices)
-    running = own = None
+    running, own = [], []
     token = origins
     for step in range(chips):
-        parts = expert_step(
+        mine, given = expert_step(
             token[step], blocks[step], others[step], table, gate_rows, up_rows, *matrices
         )
-        token, *parts = lax.optimization_barrier((token, *parts))
-        given = [lax.ppermute(p, "expert", swap) for p in parts[PIECES:]]
-        total = [a + b.astype(jnp.float32) for a, b in zip(parts[:PIECES], given)]
-        if step == 0:
-            own = [lax.ppermute(c.astype(jnp.bfloat16), ("section", "expert"), relay) for c in total]
-        elif step == 1:
-            running = [c.astype(jnp.bfloat16) for c in total]
-        else:
-            arrived = [lax.ppermute(r, "expert", onward) for r in running]
-            running = [(a.astype(jnp.float32) + c).astype(jnp.bfloat16) for a, c in zip(arrived, total)]
+        token, mine, given = lax.optimization_barrier((token, mine, given))
+        given = lax.ppermute(given, "expert", swap)
+        if step == 1:
+            running = [None] * PIECES
+        for h in range(PIECES):
+            rows = slice(h * piece, (h + 1) * piece)
+            total = mine[rows] + given[rows].astype(jnp.float32)
+            if step == 0:
+                own.append(lax.ppermute(total.astype(jnp.bfloat16), ("section", "expert"), relay))
+                kept = own
+            else:
+                if step > 1:
+                    total = lax.ppermute(running[h], "expert", onward).astype(jnp.float32) + total
+                running[h] = total.astype(jnp.bfloat16)
+                kept = running
+            if step > 0 and h + 1 < PIECES:
+                kept[h], mine, given = lax.optimization_barrier((kept[h], mine, given))
     last = [lax.ppermute(r, ("section", "expert"), relay_onward) for r in running]
     result = [(a.astype(jnp.float32) + b.astype(jnp.float32)).astype(jnp.bfloat16) for a, b in zip(last, own)]
     return jnp.concatenate(result, axis=0)[None]

time: 232 us -> 234 us (level)
  waiting for transfers between devices: 94.7 us -> 106 us
  Pallas kernels: 83 us -> 72.4 us
    ppermute x30 -> x22, waiting for transfers between devices: 12.1 us -> 78.7 us  [the longest x12 58.1 us: body(): lax.ppermute(running[h], 'expert', onward).astype(jnp.float32) + total]
    ppermute x14, waiting for transfers between devices: 47.5 us -> 2.13 us  [body(): blocks.append([lax.ppermute(b, 'expert', onward) for b in blocks[-1]])]
    pallas_call x8, Pallas kernels: 76.4 us -> 65.8 us  [expert_step(): pl.pallas_call(expert_kernel, in_specs=[pl.BlockSpec(memory_space=pltpu.S...]
    ppermute x2, waiting for transfers between devices: 22.4 us -> 13.8 us  [body(): lax.ppermute(r, ('section', 'expert'), relay_onward)]
    ppermute x16, waiting for transfers between devices: 8.29 us -> 5.31 us  [body(): others.append([lax.ppermute(b, 'expert', swap) for b in blocks[step]])]
    ppermute x30 -> x22, starting transfers between devices: 16.2 us -> 18.3 us  [the longest x12 14.1 us: body(): lax.ppermute(running[h], 'expert', onward).astype(jnp.float32) + total]
  transfers between devices with their start and end apart: 63 -> 55, of which waited for: 21 -> 21; matrix products, arithmetic and copies ran while one was open for 3% -> 2% of each run, Pallas kernels for 36% -> 31%
where the time goes in v2:
time: 234 us; the launch traced here: 232 us
  waiting for transfers between devices  106 us (45%)
  Pallas kernels  72.4 us (31%)
  starting transfers between devices  44.9 us (19%)
  other arithmetic  4.52 us (2%)
  local copies, waits for them, and re-layouts  3.58 us (2%)
    pallas_call x8, Pallas kernels, expert_step(): pl.pallas_call(expert_kernel, in_specs=[pl.BlockSpec(memory_space=pltpu.S...  65.8 us
    ppermute x12, waiting for transfers between devices, body(): lax.ppermute(running[h], 'expert', onward).astype(jnp.float32) + total  58.1 us
    ppermute x2, waiting for transfers between devices, body(): lax.ppermute(total.astype(jnp.bfloat16), ('section', 'expert'), relay)  20.6 us
    ppermute x14, starting transfers between devices, body(): blocks.append([lax.ppermute(b, 'expert', onward) for b in blocks[-1]])  16.9 us
    ppermute x12, starting transfers between devices, body(): lax.ppermute(running[h], 'expert', onward).astype(jnp.float32) + total  14.1 us
    ppermute x2, waiting for transfers between devices, body(): lax.ppermute(r, ('section', 'expert'), relay_onward)  13.8 us
    pallas_call x1, Pallas kernels, load_inside(): pl.pallas_call(load_kernel, in_specs=[pl.BlockSpec(memory_space=pltpu.HBM...  6.57 us
    all_to_all x1, waiting for transfers between devices, body(): lax.all_to_all(table, 'expert', split_axis=0, concat_axis=0, tiled=True)  5.81 us
  transfers between devices with their start and end apart: 55, of which 21 were waited for; matrix products, arithmetic and copies ran while one was open for 2% of the time, Pallas kernels for 31%

profile of v2, /device:TPU:12, one launch (start us, length us, event | category | flops | bytes accessed | tf_op | source)
XLA Modules:
  0.0 231.7 jit_solution(13599347299558098730)
XLA Ops:
  5.5 5.3 %all-to-all-start = ((f32[16,2,128]{2,1,0:T(2,128)}), f32[16,2,128]{2,1,0:T(2,128)S(1)}, u32[]{:S(2)}, u32[]{:S(2)}) async-start(f32[16,2,128]{2,1,0:T(2,128)} %pad_maximum_fusion), calls=%async_computation | async-start | bytes 32768 | tf_op jit(solution)/shard_map/all_to_all | solution.py:231
  11.6 5.8 %all-to-all-done.table = f32[16,2,128]{2,1,0:T(2,128)S(1)} async-done(((f32[16,2,128]{2,1,0:T(2,128)}), f32[16,2,128]{2,1,0:T(2,128)S(1)}, u32[]{:S(2)}, u32[]{:S(2)}) %all-to-all-start) | async-done | bytes 16416 | tf_op jit(solution)/shard_map/all_to_all | solution.py:231
  17.4 6.6 %load_weights.1 = (bf16[768,4096]{1,0:T(8,128)(2,1)S(1)}, bf16[4096,1536]{1,0:T(8,128)(2,1)S(1)}) custom-call(bf16[768,4096]{1,0:T(8,128)(2,1)} %bitcast.39, bf16[4096,768]{1,0:T(8,128)(2,1)} %bitcast.40, bf16[4096,768]{1,0:T(8,128)(2,1)} %bitcast.41), custom_call_target="tpu_custom_call" | custom-call | tf_op jit(solution)/shard_map/load_weights/pallas_call | solution.py:178
  24.8 8.2 %expert_step.8 = (f32[128,4096]{1,0:T(8,128)S(1)}, bf16[128,4096]{1,0:T(8,128)(2,1)S(1)}) custom-call(s32[2]{0:T(128)S(1)} %slice_bitcast_fusion.2.origin, bf16[64,4096]{1,0:T(8,128)(2,1)S(1)} %get-tuple-element.77.a0, bf16[64,4096]{1,0:T(8,128)(2,1)S(1)} %get-tuple-element.78.a1, bf16[64,4096]{1,0:T(8,128)(2,1)S(1)} %collective-permute-done.b0, ...), custom_call_target="tpu_custom_call" | custom-call | flops 4831838208 | bytes 10485760 | tf_op jit(solution)/shard_map/expert_step/pallas_call | solution.py:136
  35.6 8.2 %expert_step.9 = (f32[128,4096]{1,0:T(8,128)S(1)}, bf16[128,4096]{1,0:T(8,128)(2,1)S(1)}) custom-call(s32[2]{0:T(128)S(1)} %slice_reduce_fusion.6.origin, bf16[64,4096]{1,0:T(8,128)(2,1)S(1)} %collective-permute-done.2.a0, bf16[64,4096]{1,0:T(8,128)(2,1)S(1)} %collective-permute-done.3.a1, bf16[64,4096]{1,0:T(8,128)(2,1)S(1)} %collective-permute-done.4.b0, ...), custom_call_target="tpu_custom_call" | custom-call | flops 4831838208 | bytes 10485760 | tf_op jit(solution)/shard_map/expert_step/pallas_call | solution.py:136
  50.5 8.2 %expert_step.10 = (f32[128,4096]{1,0:T(8,128)S(1)}, bf16[128,4096]{1,0:T(8,128)(2,1)S(1)}) custom-call(s32[2]{0:T(128)S(1)} %slice_reduce_fusion.5.origin, bf16[64,4096]{1,0:T(8,128)(2,1)S(1)} %collective-permute-done.8.a0, bf16[64,4096]{1,0:T(8,128)(2,1)S(1)} %collective-permute-done.9.a1, bf16[64,4096]{1,0:T(8,128)(2,1)S(1)} %collective-permute-done.10.b0, ...), custom_call_target="tpu_custom_call" | custom-call | flops 4831838208 | bytes 10485760 | tf_op jit(solution)/shard_map/expert_step/pallas_call | solution.py:136
  65.1 8.2 %expert_step.11 = (f32[128,4096]{1,0:T(8,128)S(1)}, bf16[128,4096]{1,0:T(8,128)(2,1)S(1)}) custom-call(s32[2]{0:T(128)S(1)} %slice_reduce_fusion.4.origin, bf16[64,4096]{1,0:T(8,128)(2,1)S(1)} %collective-permute-done.14.a0, bf16[64,4096]{1,0:T(8,128)(2,1)S(1)} %collective-permute-done.15.a1, bf16[64,4096]{1,0:T(8,128)(2,1)S(1)} %collective-permute-done.16.b0, ...), custom_call_target="tpu_custom_call" | custom-call | flops 4831838208 | bytes 10485760 | tf_op jit(solution)/shard_map/expert_step/pallas_call | solution.py:136
  73.6 6.8 %collective-permute-done.7 = bf16[64,4096]{1,0:T(8,128)(2,1)S(1)} collective-permute-done((bf16[64,4096]{1,0:T(8,128)(2,1)S(1)}, bf16[64,4096]{1,0:T(8,128)(2,1)S(1)}, u32[]{:S(2)}, u32[]{:S(2)}) %collective-permute-start.7) | collective-permute-done | bytes 524320 | tf_op jit(solution)/shard_map/ppermute | solution.py:256
  83.1 6.5 %collective-permute-done.46 = bf16[64,4096]{1,0:T(8,128)(2,1)S(1)} collective-permute-done((bf16[64,4096]{1,0:T(8,128)(2,1)S(1)}, bf16[64,4096]{1,0:T(8,128)(2,1)S(1)}, u32[]{:S(2)}, u32[]{:S(2)}) %collective-permute-start.46) | collective-permute-done | bytes 524320 | tf_op jit(solution)/shard_map/ppermute | solution.py:256
  92.5 8.2 %expert_step.12 = (f32[128,4096]{1,0:T(8,128)S(1)}, bf16[128,4096]{1,0:T(8,128)(2,1)S(1)}) custom-call(s32[2]{0:T(128)S(1)} %slice_reduce_fusion.3.origin, bf16[64,4096]{1,0:T(8,128)(2,1)S(1)} %collective-permute-done.20.a0, bf16[64,4096]{1,0:T(8,128)(2,1)S(1)} %collective-permute-done.21.a1, bf16[64,4096]{1,0:T(8,128)(2,1)S(1)} %collective-permute-done.22.b0, ...), custom_call_target="tpu_custom_call" | custom-call | flops 4831838208 | bytes 10485760 | tf_op jit(solution)/shard_map/expert_step/pallas_call | solution.py:136
  102.6 3.9 %collective-permute-done.13 = bf16[64,4096]{1,0:T(8,128)(2,1)S(1)} collective-permute-done((bf16[64,4096]{1,0:T(8,128)(2,1)S(1)}, bf16[64,4096]{1,0:T(8,128)(2,1)S(1)}, u32[]{:S(2)}, u32[]{:S(2)}) %collective-permute-start.13) | collective-permute-done | bytes 524320 | tf_op jit(solution)/shard_map/ppermute | solution.py:256
  107.7 4.4 %collective-permute-done.47 = bf16[64,4096]{1,0:T(8,128)(2,1)S(1)} collective-permute-done((bf16[64,4096]{1,0:T(8,128)(2,1)S(1)}, bf16[64,4096]{1,0:T(8,128)(2,1)S(1)}, u32[]{:S(2)}, u32[]{:S(2)}) %collective-permute-start.47) | collective-permute-done | bytes 524320 | tf_op jit(solution)/shard_map/ppermute | solution.py:256
  115.0 8.2 %expert_step.13 = (f32[128,4096]{1,0:T(8,128)S(1)}, bf16[128,4096]{1,0:T(8,128)(2,1)S(1)}) custom-call(s32[2]{0:T(128)S(1)} %slice_reduce_fusion.2.origin, bf16[64,4096]{1,0:T(8,128)(2,1)S(1)} %collective-permute-done.26.a0, bf16[64,4096]{1,0:T(8,128)(2,1)S(1)} %collective-permute-done.27.a1, bf16[64,4096]{1,0:T(8,128)(2,1)S(1)} %collective-permute-done.28.b0, ...), custom_call_target="tpu_custom_call" | custom-call | flops 4831838208 | bytes 10485760 | tf_op jit(solution)/shard_map/expert_step/pallas_call | solution.py:136
  123.5 5.4 %collective-permute-done.19 = bf16[64,4096]{1,0:T(8,128)(2,1)S(1)} collective-permute-done((bf16[64,4096]{1,0:T(8,128)(2,1)S(1)}, bf16[64,4096]{1,0:T(8,128)(2,1)S(1)}, u32[]{:S(2)}, u32[]{:S(2)}) %collective-permute-start.19) | collective-permute-done | bytes 524320 | tf_op jit(solution)/shard_map/ppermute | solution.py:256
  131.6 6.5 %collective-permute-done.48 = bf16[64,4096]{1,0:T(8,128)(2,1)S(1)} collective-permute-done((bf16[64,4096]{1,0:T(8,128)(2,1)S(1)}, bf16[64,4096]{1,0:T(8,128)(2,1)S(1)}, u32[]{:S(2)}, u32[]{:S(2)}) %collective-permute-start.48) | collective-permute-done | bytes 524320 | tf_op jit(solution)/shard_map/ppermute | solution.py:256
  141.0 8.2 %expert_step.14 = (f32[128,4096]{1,0:T(8,128)S(1)}, bf16[128,4096]{1,0:T(8,128)(2,1)S(1)}) custom-call(s32[2]{0:T(128)S(1)} %slice_reduce_fusion.1.origin, bf16[64,4096]{1,0:T(8,128)(2,1)S(1)} %collective-permute-done.32.a0, bf16[64,4096]{1,0:T(8,128)(2,1)S(1)} %collective-permute-done.33.a1, bf16[64,4096]{1,0:T(8,128)(2,1)S(1)} %collective-permute-done.34.b0, ...), custom_call_target="tpu_custom_call" | custom-call | flops 4831838208 | bytes 10485760 | tf_op jit(solution)/shard_map/expert_step/pallas_call | solution.py:136
  151.1 3.9 %collective-permute-done.25 = bf16[64,4096]{1,0:T(8,128)(2,1)S(1)} collective-permute-done((bf16[64,4096]{1,0:T(8,128)(2,1)S(1)}, bf16[64,4096]{1,0:T(8,128)(2,1)S(1)}, u32[]{:S(2)}, u32[]{:S(2)}) %collective-permute-start.25) | collective-permute-done | bytes 524320 | tf_op jit(solution)/shard_map/ppermute | solution.py:256
  157.6 8.2 %expert_step.15 = (f32[128,4096]{1,0:T(8,128)S(1)}, bf16[128,4096]{1,0:T(8,128)(2,1)S(1)}) custom-call(s32[2]{0:T(128)S(1)} %slice_reduce_fusion.origin, bf16[64,4096]{1,0:T(8,128)(2,1)S(1)} %collective-permute-done.38.a0, bf16[64,4096]{1,0:T(8,128)(2,1)S(1)} %collective-permute-done.39.a1, bf16[64,4096]{1,0:T(8,128)(2,1)S(1)} %collective-permute-done.40.b0, ...), custom_call_target="tpu_custom_call" | custom-call | flops 4831838208 | bytes 10485760 | tf_op jit(solution)/shard_map/expert_step/pallas_call | solution.py:136
  168.6 6.5 %collective-permute-done.31 = bf16[64,4096]{1,0:T(8,128)(2,1)S(1)} collective-permute-done((bf16[64,4096]{1,0:T(8,128)(2,1)S(1)}, bf16[64,4096]{1,0:T(8,128)(2,1)S(1)}, u32[]{:S(2)}, u32[]{:S(2)}) %collective-permute-start.31) | collective-permute-done | bytes 524320 | tf_op jit(solution)/shard_map/ppermute | solution.py:256
  176.3 4.4 %collective-permute-done.50 = bf16[64,4096]{1,0:T(8,128)(2,1)S(1)} collective-permute-done((bf16[64,4096]{1,0:T(8,128)(2,1)S(1)}, bf16[64,4096]{1,0:T(8,128)(2,1)S(1)}, u32[]{:S(2)}, u32[]{:S(2)}) %collective-permute-start.50) | collective-permute-done | bytes 524320 | tf_op jit(solution)/shard_map/ppermute | solution.py:256
  182.0 4.4 %collective-permute-done.37 = bf16[64,4096]{1,0:T(8,128)(2,1)S(1)} collective-permute-done((bf16[64,4096]{1,0:T(8,128)(2,1)S(1)}, bf16[64,4096]{1,0:T(8,128)(2,1)S(1)}, u32[]{:S(2)}, u32[]{:S(2)}) %collective-permute-start.37) | collective-permute-done | bytes 524320 | tf_op jit(solution)/shard_map/ppermute | solution.py:256
  186.5 5.4 %collective-permute-done.51 = bf16[64,4096]{1,0:T(8,128)(2,1)S(1)} collective-permute-done((bf16[64,4096]{1,0:T(8,128)(2,1)S(1)}, bf16[64,4096]{1,0:T(8,128)(2,1)S(1)}, u32[]{:S(2)}, u32[]{:S(2)}) %collective-permute-start.51) | collective-permute-done | bytes 524320 | tf_op jit(solution)/shard_map/ppermute | solution.py:256
  196.1 13.8 %collective-permute-done.52 = bf16[64,4096]{1,0:T(8,128)(2,1)S(1)} collective-permute-done((bf16[64,4096]{1,0:T(8,128)(2,1)S(1)}, bf16[64,4096]{1,0:T(8,128)(2,1)S(1)}, u32[]{:S(2)}, u32[]{:S(2)}) %collective-permute-start.52) | collective-permute-done | bytes 524320 | tf_op jit(solution)/shard_map/ppermute | solution.py:261
  210.0 20.6 %collective-permute-done.45 = bf16[64,4096]{1,0:T(8,128)(2,1)S(1)} collective-permute-done((bf16[64,4096]{1,0:T(8,128)(2,1)S(1)}, bf16[64,4096]{1,0:T(8,128)(2,1)S(1)}, u32[]{:S(2)}, u32[]{:S(2)}) %collective-permute-start.45) | collective-permute-done | bytes 524320 | tf_op jit(solution)/shard_map/ppermute | solution.py:252
  (137 shorter events, 55.4 us)
Async XLA Ops:
  1.3 16.1 %collective-permute-start = (bf16[64,4096]{1,0:T(8,128)(2,1)S(1)}, bf16[64,4096]{1,0:T(8,128)(2,1)S(1)}, u32[]{:S(2)}, u32[]{:S(2)}) collective-permute-start(bf16[64,4096]{1,0:T(8,128)(2,1)S(1)} %get-tuple-element.77.a0), channel_id=1, source_target_pairs={{0,1},{1,0},{2,3},{3,2},{4,5},{5,4},{6,7},{7,6},{8,9},{9,8},{10,11... | collective-permute-start | bytes 1572872 | tf_op jit(solution)/shard_map/ppermute | solution.py:219
  1.4 22.6 %collective-permute-start.2 = (bf16[64,4096]{1,0:T(8,128)(2,1)S(1)}, bf16[64,4096]{1,0:T(8,128)(2,1)S(1)}, u32[]{:S(2)}, u32[]{:S(2)}) collective-permute-start(bf16[64,4096]{1,0:T(8,128)(2,1)S(1)} %get-tuple-element.77.a0), channel_id=1, source_target_pairs={{2,6},{6,10},{10,14},{14,12},{12,8},{8,4},{4,0},{0,2},{7,3},{11,7}... | collective-permute-start | bytes 1572872 | tf_op jit(solution)/shard_map/ppermute | solution.py:216
  3.0 21.1 %collective-permute-start.3 = (bf16[64,4096]{1,0:T(8,128)(2,1)S(1)}, bf16[64,4096]{1,0:T(8,128)(2,1)S(1)}, u32[]{:S(2)}, u32[]{:S(2)}) collective-permute-start(bf16[64,4096]{1,0:T(8,128)(2,1)S(1)} %get-tuple-element.78.a1), channel_id=1, source_target_pairs={{2,6},{6,10},{10,14},{14,12},{12,8},{8,4},{4,0},{0,2},{7,3},{11,7}... | collective-permute-start | bytes 1572872 | tf_op jit(solution)/shard_map/ppermute | solution.py:216
  33.0 15.2 %collective-permute-start.44 = (bf16[128,4096]{1,0:T(8,128)(2,1)S(1)}, bf16[128,4096]{1,0:T(8,128)(2,1)S(1)}, u32[]{:S(2)}, u32[]{:S(2)}) collective-permute-start(bf16[128,4096]{1,0:T(8,128)(2,1)S(1)} %get-tuple-element.134), channel_id=1, source_target_pairs={{0,1},{1,0},{2,3},{3,2},{4,5},{5,4},{6,7},{7,6},{8,9},{9,8},{10,11... | collective-permute-start | bytes 3145736 | tf_op jit(solution)/shard_map/ppermute | solution.py:245
  43.8 17.2 %collective-permute-start.6 = (bf16[128,4096]{1,0:T(8,128)(2,1)S(1)}, bf16[128,4096]{1,0:T(8,128)(2,1)S(1)}, u32[]{:S(2)}, u32[]{:S(2)}) collective-permute-start(bf16[128,4096]{1,0:T(8,128)(2,1)S(1)} %get-tuple-element.95), channel_id=1, source_target_pairs={{0,1},{1,0},{2,3},{3,2},{4,5},{5,4},{6,7},{7,6},{8,9},{9,8},{10,11... | collective-permute-start | bytes 3145736 | tf_op jit(solution)/shard_map/ppermute | solution.py:245
  44.4 15.3 %collective-permute-start.14 = (bf16[64,4096]{1,0:T(8,128)(2,1)S(1)}, bf16[64,4096]{1,0:T(8,128)(2,1)S(1)}, u32[]{:S(2)}, u32[]{:S(2)}) collective-permute-start(bf16[64,4096]{1,0:T(8,128)(2,1)S(1)} %collective-permute-done.8.a0), channel_id=1, source_target_pairs={{2,6},{6,10},{10,14},{14,12},{12,8},{8,4},{4,0},{0,2},{7,3},{11,7}... | collective-permute-start | bytes 1572872 | tf_op jit(solution)/shard_map/ppermute | solution.py:216
  49.1 146.9 %collective-permute-start.53 = (bf16[64,4096]{1,0:T(8,128)(2,1)S(1)}, bf16[64,4096]{1,0:T(8,128)(2,1)S(1)}, u32[]{:S(2)}, u32[]{:S(2)}) collective-permute-start(bf16[64,4096]{1,0:T(8,128)(2,1)S(1)} %get-tuple-element.150), channel_id=1, source_target_pairs={{16,0},{17,1},{18,2},{19,3},{20,4},{21,5},{22,6},{23,7},{24,8},{25... | collective-permute-start | bytes 1572872 | tf_op jit(solution)/shard_map/ppermute | solution.py:252
  58.7 22.7 %collective-permute-start.12 = (bf16[128,4096]{1,0:T(8,128)(2,1)S(1)}, bf16[128,4096]{1,0:T(8,128)(2,1)S(1)}, u32[]{:S(2)}, u32[]{:S(2)}) collective-permute-start(bf16[128,4096]{1,0:T(8,128)(2,1)S(1)} %get-tuple-element.101), channel_id=1, source_target_pairs={{0,1},{1,0},{2,3},{3,2},{4,5},{5,4},{6,7},{7,6},{8,9},{9,8},{10,11... | collective-permute-start | bytes 3145736 | tf_op jit(solution)/shard_map/ppermute | solution.py:245
  62.7 18.9 %collective-permute-start.21 = (bf16[64,4096]{1,0:T(8,128)(2,1)S(1)}, bf16[64,4096]{1,0:T(8,128)(2,1)S(1)}, u32[]{:S(2)}, u32[]{:S(2)}) collective-permute-start(bf16[64,4096]{1,0:T(8,128)(2,1)S(1)} %collective-permute-done.15.a1), channel_id=1, source_target_pairs={{2,6},{6,10},{10,14},{14,12},{12,8},{8,4},{4,0},{0,2},{7,3},{11,7}... | collective-permute-start | bytes 1572872 | tf_op jit(solution)/shard_map/ppermute | solution.py:216
  63.7 16.8 %collective-permute-start.7 = (bf16[64,4096]{1,0:T(8,128)(2,1)S(1)}, bf16[64,4096]{1,0:T(8,128)(2,1)S(1)}, u32[]{:S(2)}, u32[]{:S(2)}) collective-permute-start(bf16[64,4096]{1,0:T(8,128)(2,1)S(1)} %add_convert_fusion.17), channel_id=1, source_target_pairs={{2,6},{6,10},{10,14},{14,12},{12,8},{8,4},{4,0},{0,2},{7,3},{11,7}... | collective-permute-start | bytes 1572872 | tf_op jit(solution)/shard_map/ppermute | solution.py:256
  73.6 27.5 %collective-permute-start.18 = (bf16[128,4096]{1,0:T(8,128)(2,1)S(1)}, bf16[128,4096]{1,0:T(8,128)(2,1)S(1)}, u32[]{:S(2)}, u32[]{:S(2)}) collective-permute-start(bf16[128,4096]{1,0:T(8,128)(2,1)S(1)} %get-tuple-element.107), channel_id=1, source_target_pairs={{0,1},{1,0},{2,3},{3,2},{4,5},{5,4},{6,7},{7,6},{8,9},{9,8},{10,11... | collective-permute-start | bytes 3145736 | tf_op jit(solution)/shard_map/ppermute | solution.py:245
  81.6 19.3 %collective-permute-start.26 = (bf16[64,4096]{1,0:T(8,128)(2,1)S(1)}, bf16[64,4096]{1,0:T(8,128)(2,1)S(1)}, u32[]{:S(2)}, u32[]{:S(2)}) collective-permute-start(bf16[64,4096]{1,0:T(8,128)(2,1)S(1)} %collective-permute-done.20.a0), channel_id=1, source_target_pairs={{2,6},{6,10},{10,14},{14,12},{12,8},{8,4},{4,0},{0,2},{7,3},{11,7}... | collective-permute-start | bytes 1572872 | tf_op jit(solution)/shard_map/ppermute | solution.py:216
  89.8 16.9 %collective-permute-start.27 = (bf16[64,4096]{1,0:T(8,128)(2,1)S(1)}, bf16[64,4096]{1,0:T(8,128)(2,1)S(1)}, u32[]{:S(2)}, u32[]{:S(2)}) collective-permute-start(bf16[64,4096]{1,0:T(8,128)(2,1)S(1)} %collective-permute-done.21.a1), channel_id=1, source_target_pairs={{2,6},{6,10},{10,14},{14,12},{12,8},{8,4},{4,0},{0,2},{7,3},{11,7}... | collective-permute-start | bytes 1572872 | tf_op jit(solution)/shard_map/ppermute | solution.py:216
  100.9 29.0 %collective-permute-start.24 = (bf16[128,4096]{1,0:T(8,128)(2,1)S(1)}, bf16[128,4096]{1,0:T(8,128)(2,1)S(1)}, u32[]{:S(2)}, u32[]{:S(2)}) collective-permute-start(bf16[128,4096]{1,0:T(8,128)(2,1)S(1)} %get-tuple-element.113), channel_id=1, source_target_pairs={{0,1},{1,0},{2,3},{3,2},{4,5},{5,4},{6,7},{7,6},{8,9},{9,8},{10,11... | collective-permute-start | bytes 3145736 | tf_op jit(solution)/shard_map/ppermute | solution.py:245
  106.7 16.7 %collective-permute-start.32 = (bf16[64,4096]{1,0:T(8,128)(2,1)S(1)}, bf16[64,4096]{1,0:T(8,128)(2,1)S(1)}, u32[]{:S(2)}, u32[]{:S(2)}) collective-permute-start(bf16[64,4096]{1,0:T(8,128)(2,1)S(1)} %collective-permute-done.26.a0), channel_id=1, source_target_pairs={{2,6},{6,10},{10,14},{14,12},{12,8},{8,4},{4,0},{0,2},{7,3},{11,7}... | collective-permute-start | bytes 1572872 | tf_op jit(solution)/shard_map/ppermute | solution.py:216
  112.3 17.8 %collective-permute-start.33 = (bf16[64,4096]{1,0:T(8,128)(2,1)S(1)}, bf16[64,4096]{1,0:T(8,128)(2,1)S(1)}, u32[]{:S(2)}, u32[]{:S(2)}) collective-permute-start(bf16[64,4096]{1,0:T(8,128)(2,1)S(1)} %collective-permute-done.27.a1), channel_id=1, source_target_pairs={{2,6},{6,10},{10,14},{14,12},{12,8},{8,4},{4,0},{0,2},{7,3},{11,7}... | collective-permute-start | bytes 1572872 | tf_op jit(solution)/shard_map/ppermute | solution.py:216
  123.4 31.6 %collective-permute-start.30 = (bf16[128,4096]{1,0:T(8,128)(2,1)S(1)}, bf16[128,4096]{1,0:T(8,128)(2,1)S(1)}, u32[]{:S(2)}, u32[]{:S(2)}) collective-permute-start(bf16[128,4096]{1,0:T(8,128)(2,1)S(1)} %get-tuple-element.119), channel_id=1, source_target_pairs={{0,1},{1,0},{2,3},{3,2},{4,5},{5,4},{6,7},{7,6},{8,9},{9,8},{10,11... | collective-permute-start | bytes 3145736 | tf_op jit(solution)/shard_map/ppermute | solution.py:245
  130.1 19.3 %collective-permute-start.38 = (bf16[64,4096]{1,0:T(8,128)(2,1)S(1)}, bf16[64,4096]{1,0:T(8,128)(2,1)S(1)}, u32[]{:S(2)}, u32[]{:S(2)}) collective-permute-start(bf16[64,4096]{1,0:T(8,128)(2,1)S(1)} %collective-permute-done.32.a0), channel_id=1, source_target_pairs={{2,6},{6,10},{10,14},{14,12},{12,8},{8,4},{4,0},{0,2},{7,3},{11,7}... | collective-permute-start | bytes 1572872 | tf_op jit(solution)/shard_map/ppermute | solution.py:216
  149.4 25.7 %collective-permute-start.36 = (bf16[128,4096]{1,0:T(8,128)(2,1)S(1)}, bf16[128,4096]{1,0:T(8,128)(2,1)S(1)}, u32[]{:S(2)}, u32[]{:S(2)}) collective-permute-start(bf16[128,4096]{1,0:T(8,128)(2,1)S(1)} %get-tuple-element.125), channel_id=1, source_target_pairs={{0,1},{1,0},{2,3},{3,2},{4,5},{5,4},{6,7},{7,6},{8,9},{9,8},{10,11... | collective-permute-start | bytes 3145736 | tf_op jit(solution)/shard_map/ppermute | solution.py:245
  149.5 17.4 %collective-permute-start.49 = (bf16[64,4096]{1,0:T(8,128)(2,1)S(1)}, bf16[64,4096]{1,0:T(8,128)(2,1)S(1)}, u32[]{:S(2)}, u32[]{:S(2)}) collective-permute-start(bf16[64,4096]{1,0:T(8,128)(2,1)S(1)} %add_convert_fusion.5), channel_id=1, source_target_pairs={{2,6},{6,10},{10,14},{14,12},{12,8},{8,4},{4,0},{0,2},{7,3},{11,7}... | collective-permute-start | bytes 1572872 | tf_op jit(solution)/shard_map/ppermute | solution.py:256
  166.9 19.4 %collective-permute-start.42 = (bf16[128,4096]{1,0:T(8,128)(2,1)S(1)}, bf16[128,4096]{1,0:T(8,128)(2,1)S(1)}, u32[]{:S(2)}, u32[]{:S(2)}) collective-permute-start(bf16[128,4096]{1,0:T(8,128)(2,1)S(1)} %get-tuple-element.131), channel_id=1, source_target_pairs={{0,1},{1,0},{2,3},{3,2},{4,5},{5,4},{6,7},{7,6},{8,9},{9,8},{10,11... | collective-permute-start | bytes 3145736 | tf_op jit(solution)/shard_map/ppermute | solution.py:245
  192.2 17.7 %collective-permute-start.52 = (bf16[64,4096]{1,0:T(8,128)(2,1)S(1)}, bf16[64,4096]{1,0:T(8,128)(2,1)S(1)}, u32[]{:S(2)}, u32[]{:S(2)}) collective-permute-start(bf16[64,4096]{1,0:T(8,128)(2,1)S(1)} %add_convert_fusion.2), channel_id=1, source_target_pairs={{18,6},{22,10},{26,14},{30,12},{28,8},{24,4},{20,0},{16,2},{23,3},... | collective-permute-start | bytes 1572872 | tf_op jit(solution)/shard_map/ppermute | solution.py:261
  193.4 37.1 %collective-permute-start.45 = (bf16[64,4096]{1,0:T(8,128)(2,1)S(1)}, bf16[64,4096]{1,0:T(8,128)(2,1)S(1)}, u32[]{:S(2)}, u32[]{:S(2)}) collective-permute-start(bf16[64,4096]{1,0:T(8,128)(2,1)S(1)} %get-tuple-element.149), channel_id=1, source_target_pairs={{16,0},{17,1},{18,2},{19,3},{20,4},{21,5},{22,6},{23,7},{24,8},{25... | collective-permute-start | bytes 1572872 | tf_op jit(solution)/shard_map/ppermute | solution.py:252
  194.8 35.8 %collective-permute-start.43 = (bf16[64,4096]{1,0:T(8,128)(2,1)S(1)}, bf16[64,4096]{1,0:T(8,128)(2,1)S(1)}, u32[]{:S(2)}, u32[]{:S(2)}) collective-permute-start(bf16[64,4096]{1,0:T(8,128)(2,1)S(1)} %add_convert_fusion.11), channel_id=1, source_target_pairs={{18,6},{22,10},{26,14},{30,12},{28,8},{24,4},{20,0},{16,2},{23,3},... | collective-permute-start | bytes 1572872 | tf_op jit(solution)/shard_map/ppermute | solution.py:261
  (35 other events, 300.1 us)

commit v3 on v2

--- a/solution.py
+++ b/solution.py
@@ -12,7 +12,7 @@
 PIECES = 2
 HIDDEN_BLOCK = 256
 PART = 1024
-VMEM_LIMIT = 16 << 20
+VMEM_LIMIT = 10 << 20
 CONTRACT = (((1,), (1,)), ((), ()))
 
 
@@ -189,6 +189,19 @@
     )(*[pltpu.with_memory_space_constraint(a, pltpu.HBM) for a in arrays])
 
 
+def widen_kernel(held, out):
+    out[...] = held[...].astype(jnp.float32)
+
+
+def widen(held):
+    return pl.pallas_call(
+        widen_kernel,
+        out_shape=jax.ShapeDtypeStruct(held.shape, jnp.float32),
+        compiler_params=pltpu.CompilerParams(vmem_limit_bytes=VMEM_LIMIT),
+        name="widen",
+    )(held)
+
+
 def body(grad_out, expert_ids, gate_weights, saved_gate, saved_up, w_gate, w_up, w_down):
     devices = lax.axis_size("expert")
     sections = lax.axis_size("section")
@@ -258,7 +271,10 @@
                 kept = running
             if step > 0 and h + 1 < PIECES:
                 kept[h], mine, given = lax.optimization_barrier((kept[h], mine, given))
-    last = [lax.ppermute(r, ("section", "expert"), relay_onward) for r in running]
+    last = []
+    for h in range(PIECES):
+        last.append(lax.ppermute(running[h], ("section", "expert"), relay_onward))
+    own[0] = widen(own[0])
     result = [(a.astype(jnp.float32) + b.astype(jnp.float32)).astype(jnp.bfloat16) for a, b in zip(last, own)]
     return jnp.concatenate(result, axis=0)[None]
 

time: 234 us -> 227 us (0.970)
  waiting for transfers between devices: 106 us -> 97 us
    ppermute x2, waiting for transfers between devices: 20.6 us -> 0.01 us  [body(): lax.ppermute(total.astype(jnp.bfloat16), ('section', 'expert'), relay)]
    ppermute x2, waiting for transfers between devices: 13.8 us -> 23.5 us  [body(): last.append(lax.ppermute(running[h], ('section', 'expert'), relay_onward))]
  transfers between devices with their start and end apart: 55 -> 55, of which waited for: 21 -> 21; matrix products, arithmetic and copies ran while one was open for 2% -> 3% of each run, Pallas kernels for 31% -> 33%
where the time goes in v3:
time: 227 us; the launch traced here: 223 us
  waiting for transfers between devices  97 us (43%)
  Pallas kernels  72.8 us (32%)
  starting transfers between devices  44.7 us (20%)
  other arithmetic  4.62 us (2%)
  local copies, waits for them, and re-layouts  3.58 us (2%)
    pallas_call x8, Pallas kernels, expert_step(): pl.pallas_call(expert_kernel, in_specs=[pl.BlockSpec(memory_space=pltpu.S...  66.2 us
    ppermute x12, waiting for transfers between devices, body(): lax.ppermute(running[h], 'expert', onward).astype(jnp.float32) + total  60.4 us
    ppermute x2, waiting for transfers between devices, body(): last.append(lax.ppermute(running[h], ('section', 'expert'), relay_onward))  23.5 us
    ppermute x14, starting transfers between devices, body(): blocks.append([lax.ppermute(b, 'expert', onward) for b in blocks[-1]])  16.7 us
    ppermute x12, starting transfers between devices, body(): lax.ppermute(running[h], 'expert', onward).astype(jnp.float32) + total  14 us
    pallas_call x1, Pallas kernels, load_inside(): pl.pallas_call(load_kernel, in_specs=[pl.BlockSpec(memory_space=pltpu.HBM...  6.57 us
    all_to_all x1, waiting for transfers between devices, body(): lax.all_to_all(table, 'expert', split_axis=0, concat_axis=0, tiled=True)  5.81 us
    all_to_all x1, starting transfers between devices, body(): lax.all_to_all(table, 'expert', split_axis=0, concat_axis=0, tiled=True)  5.28 us
  transfers between devices with their start and end apart: 55, of which 21 were waited for; matrix products, arithmetic and copies ran while one was open for 3% of the time, Pallas kernels for 33%

profile of v3, /device:TPU:12, one launch (start us, length us, event | category | flops | bytes accessed | tf_op | source)
XLA Modules:
  0.0 223.4 jit_solution(9653765783980017831)
XLA Ops:
  5.5 5.3 %all-to-all-start = ((f32[16,2,128]{2,1,0:T(2,128)}), f32[16,2,128]{2,1,0:T(2,128)S(1)}, u32[]{:S(2)}, u32[]{:S(2)}) async-start(f32[16,2,128]{2,1,0:T(2,128)} %pad_maximum_fusion), calls=%async_computation | async-start | bytes 32768 | tf_op jit(solution)/shard_map/all_to_all | solution.py:244
  11.6 5.8 %all-to-all-done.table = f32[16,2,128]{2,1,0:T(2,128)S(1)} async-done(((f32[16,2,128]{2,1,0:T(2,128)}), f32[16,2,128]{2,1,0:T(2,128)S(1)}, u32[]{:S(2)}, u32[]{:S(2)}) %all-to-all-start) | async-done | bytes 16416 | tf_op jit(solution)/shard_map/all_to_all | solution.py:244
  17.4 6.6 %load_weights.1 = (bf16[768,4096]{1,0:T(8,128)(2,1)S(1)}, bf16[4096,1536]{1,0:T(8,128)(2,1)S(1)}) custom-call(bf16[768,4096]{1,0:T(8,128)(2,1)} %bitcast.39, bf16[4096,768]{1,0:T(8,128)(2,1)} %bitcast.40, bf16[4096,768]{1,0:T(8,128)(2,1)} %bitcast.41), custom_call_target="tpu_custom_call" | custom-call | tf_op jit(solution)/shard_map/load_weights/pallas_call | solution.py:178
  24.8 8.3 %expert_step.8 = (f32[128,4096]{1,0:T(8,128)S(1)}, bf16[128,4096]{1,0:T(8,128)(2,1)S(1)}) custom-call(s32[2]{0:T(128)S(1)} %slice_bitcast_fusion.2.origin, bf16[64,4096]{1,0:T(8,128)(2,1)S(1)} %get-tuple-element.77.a0, bf16[64,4096]{1,0:T(8,128)(2,1)S(1)} %get-tuple-element.78.a1, bf16[64,4096]{1,0:T(8,128)(2,1)S(1)} %collective-permute-done.b0, ...), custom_call_target="tpu_custom_call" | custom-call | flops 4831838208 | bytes 10485760 | tf_op jit(solution)/shard_map/expert_step/pallas_call | solution.py:136
  35.6 8.3 %expert_step.9 = (f32[128,4096]{1,0:T(8,128)S(1)}, bf16[128,4096]{1,0:T(8,128)(2,1)S(1)}) custom-call(s32[2]{0:T(128)S(1)} %slice_reduce_fusion.6.origin, bf16[64,4096]{1,0:T(8,128)(2,1)S(1)} %collective-permute-done.2.a0, bf16[64,4096]{1,0:T(8,128)(2,1)S(1)} %collective-permute-done.3.a1, bf16[64,4096]{1,0:T(8,128)(2,1)S(1)} %collective-permute-done.4.b0, ...), custom_call_target="tpu_custom_call" | custom-call | flops 4831838208 | bytes 10485760 | tf_op jit(solution)/shard_map/expert_step/pallas_call | solution.py:136
  50.5 8.3 %expert_step.10 = (f32[128,4096]{1,0:T(8,128)S(1)}, bf16[128,4096]{1,0:T(8,128)(2,1)S(1)}) custom-call(s32[2]{0:T(128)S(1)} %slice_reduce_fusion.5.origin, bf16[64,4096]{1,0:T(8,128)(2,1)S(1)} %collective-permute-done.8.a0, bf16[64,4096]{1,0:T(8,128)(2,1)S(1)} %collective-permute-done.9.a1, bf16[64,4096]{1,0:T(8,128)(2,1)S(1)} %collective-permute-done.10.b0, ...), custom_call_target="tpu_custom_call" | custom-call | flops 4831838208 | bytes 10485760 | tf_op jit(solution)/shard_map/expert_step/pallas_call | solution.py:136
  65.3 8.3 %expert_step.11 = (f32[128,4096]{1,0:T(8,128)S(1)}, bf16[128,4096]{1,0:T(8,128)(2,1)S(1)}) custom-call(s32[2]{0:T(128)S(1)} %slice_reduce_fusion.4.origin, bf16[64,4096]{1,0:T(8,128)(2,1)S(1)} %collective-permute-done.14.a0, bf16[64,4096]{1,0:T(8,128)(2,1)S(1)} %collective-permute-done.15.a1, bf16[64,4096]{1,0:T(8,128)(2,1)S(1)} %collective-permute-done.16.b0, ...), custom_call_target="tpu_custom_call" | custom-call | flops 4831838208 | bytes 10485760 | tf_op jit(solution)/shard_map/expert_step/pallas_call | solution.py:136
  73.8 6.7 %collective-permute-done.7 = bf16[64,4096]{1,0:T(8,128)(2,1)S(1)} collective-permute-done((bf16[64,4096]{1,0:T(8,128)(2,1)S(1)}, bf16[64,4096]{1,0:T(8,128)(2,1)S(1)}, u32[]{:S(2)}, u32[]{:S(2)}) %collective-permute-start.7) | collective-permute-done | bytes 524320 | tf_op jit(solution)/shard_map/ppermute | solution.py:269
  83.3 6.5 %collective-permute-done.46 = bf16[64,4096]{1,0:T(8,128)(2,1)S(1)} collective-permute-done((bf16[64,4096]{1,0:T(8,128)(2,1)S(1)}, bf16[64,4096]{1,0:T(8,128)(2,1)S(1)}, u32[]{:S(2)}, u32[]{:S(2)}) %collective-permute-start.46) | collective-permute-done | bytes 524320 | tf_op jit(solution)/shard_map/ppermute | solution.py:269
  92.6 8.3 %expert_step.12 = (f32[128,4096]{1,0:T(8,128)S(1)}, bf16[128,4096]{1,0:T(8,128)(2,1)S(1)}) custom-call(s32[2]{0:T(128)S(1)} %slice_reduce_fusion.3.origin, bf16[64,4096]{1,0:T(8,128)(2,1)S(1)} %collective-permute-done.20.a0, bf16[64,4096]{1,0:T(8,128)(2,1)S(1)} %collective-permute-done.21.a1, bf16[64,4096]{1,0:T(8,128)(2,1)S(1)} %collective-permute-done.22.b0, ...), custom_call_target="tpu_custom_call" | custom-call | flops 4831838208 | bytes 10485760 | tf_op jit(solution)/shard_map/expert_step/pallas_call | solution.py:136
  102.7 3.9 %collective-permute-done.13 = bf16[64,4096]{1,0:T(8,128)(2,1)S(1)} collective-permute-done((bf16[64,4096]{1,0:T(8,128)(2,1)S(1)}, bf16[64,4096]{1,0:T(8,128)(2,1)S(1)}, u32[]{:S(2)}, u32[]{:S(2)}) %collective-permute-start.13) | collective-permute-done | bytes 524320 | tf_op jit(solution)/shard_map/ppermute | solution.py:269
  107.8 4.4 %collective-permute-done.47 = bf16[64,4096]{1,0:T(8,128)(2,1)S(1)} collective-permute-done((bf16[64,4096]{1,0:T(8,128)(2,1)S(1)}, bf16[64,4096]{1,0:T(8,128)(2,1)S(1)}, u32[]{:S(2)}, u32[]{:S(2)}) %collective-permute-start.47) | collective-permute-done | bytes 524320 | tf_op jit(solution)/shard_map/ppermute | solution.py:269
  115.1 8.3 %expert_step.13 = (f32[128,4096]{1,0:T(8,128)S(1)}, bf16[128,4096]{1,0:T(8,128)(2,1)S(1)}) custom-call(s32[2]{0:T(128)S(1)} %slice_reduce_fusion.2.origin, bf16[64,4096]{1,0:T(8,128)(2,1)S(1)} %collective-permute-done.26.a0, bf16[64,4096]{1,0:T(8,128)(2,1)S(1)} %collective-permute-done.27.a1, bf16[64,4096]{1,0:T(8,128)(2,1)S(1)} %collective-permute-done.28.b0, ...), custom_call_target="tpu_custom_call" | custom-call | flops 4831838208 | bytes 10485760 | tf_op jit(solution)/shard_map/expert_step/pallas_call | solution.py:136
  123.6 5.4 %collective-permute-done.19 = bf16[64,4096]{1,0:T(8,128)(2,1)S(1)} collective-permute-done((bf16[64,4096]{1,0:T(8,128)(2,1)S(1)}, bf16[64,4096]{1,0:T(8,128)(2,1)S(1)}, u32[]{:S(2)}, u32[]{:S(2)}) %collective-permute-start.19) | collective-permute-done | bytes 524320 | tf_op jit(solution)/shard_map/ppermute | solution.py:269
  131.8 6.5 %collective-permute-done.48 = bf16[64,4096]{1,0:T(8,128)(2,1)S(1)} collective-permute-done((bf16[64,4096]{1,0:T(8,128)(2,1)S(1)}, bf16[64,4096]{1,0:T(8,128)(2,1)S(1)}, u32[]{:S(2)}, u32[]{:S(2)}) %collective-permute-start.48) | collective-permute-done | bytes 524320 | tf_op jit(solution)/shard_map/ppermute | solution.py:269
  141.1 8.3 %expert_step.14 = (f32[128,4096]{1,0:T(8,128)S(1)}, bf16[128,4096]{1,0:T(8,128)(2,1)S(1)}) custom-call(s32[2]{0:T(128)S(1)} %slice_reduce_fusion.1.origin, bf16[64,4096]{1,0:T(8,128)(2,1)S(1)} %collective-permute-done.32.a0, bf16[64,4096]{1,0:T(8,128)(2,1)S(1)} %collective-permute-done.33.a1, bf16[64,4096]{1,0:T(8,128)(2,1)S(1)} %collective-permute-done.34.b0, ...), custom_call_target="tpu_custom_call" | custom-call | flops 4831838208 | bytes 10485760 | tf_op jit(solution)/shard_map/expert_step/pallas_call | solution.py:136
  152.4 2.7 %collective-permute-done.25 = bf16[64,4096]{1,0:T(8,128)(2,1)S(1)} collective-permute-done((bf16[64,4096]{1,0:T(8,128)(2,1)S(1)}, bf16[64,4096]{1,0:T(8,128)(2,1)S(1)}, u32[]{:S(2)}, u32[]{:S(2)}) %collective-permute-start.25) | collective-permute-done | bytes 524320 | tf_op jit(solution)/shard_map/ppermute | solution.py:269
  157.8 8.3 %expert_step.15 = (f32[128,4096]{1,0:T(8,128)S(1)}, bf16[128,4096]{1,0:T(8,128)(2,1)S(1)}) custom-call(s32[2]{0:T(128)S(1)} %slice_reduce_fusion.origin, bf16[64,4096]{1,0:T(8,128)(2,1)S(1)} %collective-permute-done.38.a0, bf16[64,4096]{1,0:T(8,128)(2,1)S(1)} %collective-permute-done.39.a1, bf16[64,4096]{1,0:T(8,128)(2,1)S(1)} %collective-permute-done.40.b0, ...), custom_call_target="tpu_custom_call" | custom-call | flops 4831838208 | bytes 10485760 | tf_op jit(solution)/shard_map/expert_step/pallas_call | solution.py:136
  167.2 8.0 %collective-permute-done.31 = bf16[64,4096]{1,0:T(8,128)(2,1)S(1)} collective-permute-done((bf16[64,4096]{1,0:T(8,128)(2,1)S(1)}, bf16[64,4096]{1,0:T(8,128)(2,1)S(1)}, u32[]{:S(2)}, u32[]{:S(2)}) %collective-permute-start.31) | collective-permute-done | bytes 524320 | tf_op jit(solution)/shard_map/ppermute | solution.py:269
  178.0 6.5 %collective-permute-done.50 = bf16[64,4096]{1,0:T(8,128)(2,1)S(1)} collective-permute-done((bf16[64,4096]{1,0:T(8,128)(2,1)S(1)}, bf16[64,4096]{1,0:T(8,128)(2,1)S(1)}, u32[]{:S(2)}, u32[]{:S(2)}) %collective-permute-start.50) | collective-permute-done | bytes 524320 | tf_op jit(solution)/shard_map/ppermute | solution.py:269
  185.6 4.4 %collective-permute-done.37 = bf16[64,4096]{1,0:T(8,128)(2,1)S(1)} collective-permute-done((bf16[64,4096]{1,0:T(8,128)(2,1)S(1)}, bf16[64,4096]{1,0:T(8,128)(2,1)S(1)}, u32[]{:S(2)}, u32[]{:S(2)}) %collective-permute-start.37) | collective-permute-done | bytes 524320 | tf_op jit(solution)/shard_map/ppermute | solution.py:269
  190.3 5.4 %collective-permute-done.51 = bf16[64,4096]{1,0:T(8,128)(2,1)S(1)} collective-permute-done((bf16[64,4096]{1,0:T(8,128)(2,1)S(1)}, bf16[64,4096]{1,0:T(8,128)(2,1)S(1)}, u32[]{:S(2)}, u32[]{:S(2)}) %collective-permute-start.51) | collective-permute-done | bytes 524320 | tf_op jit(solution)/shard_map/ppermute | solution.py:269
  198.6 14.9 %collective-permute-done.52 = bf16[64,4096]{1,0:T(8,128)(2,1)S(1)} collective-permute-done((bf16[64,4096]{1,0:T(8,128)(2,1)S(1)}, bf16[64,4096]{1,0:T(8,128)(2,1)S(1)}, u32[]{:S(2)}, u32[]{:S(2)}) %collective-permute-start.52) | collective-permute-done | bytes 524320 | tf_op jit(solution)/shard_map/ppermute | solution.py:276
  213.6 8.6 %collective-permute-done.43 = bf16[64,4096]{1,0:T(8,128)(2,1)S(1)} collective-permute-done((bf16[64,4096]{1,0:T(8,128)(2,1)S(1)}, bf16[64,4096]{1,0:T(8,128)(2,1)S(1)}, u32[]{:S(2)}, u32[]{:S(2)}) %collective-permute-start.43) | collective-permute-done | bytes 524320 | tf_op jit(solution)/shard_map/ppermute | solution.py:276
  (138 shorter events, 55.3 us)
Async XLA Ops:
  1.3 16.1 %collective-permute-start = (bf16[64,4096]{1,0:T(8,128)(2,1)S(1)}, bf16[64,4096]{1,0:T(8,128)(2,1)S(1)}, u32[]{:S(2)}, u32[]{:S(2)}) collective-permute-start(bf16[64,4096]{1,0:T(8,128)(2,1)S(1)} %get-tuple-element.77.a0), channel_id=1, source_target_pairs={{0,1},{1,0},{2,3},{3,2},{4,5},{5,4},{6,7},{7,6},{8,9},{9,8},{10,11... | collective-permute-start | bytes 1572872 | tf_op jit(solution)/shard_map/ppermute | solution.py:232
  1.4 22.6 %collective-permute-start.2 = (bf16[64,4096]{1,0:T(8,128)(2,1)S(1)}, bf16[64,4096]{1,0:T(8,128)(2,1)S(1)}, u32[]{:S(2)}, u32[]{:S(2)}) collective-permute-start(bf16[64,4096]{1,0:T(8,128)(2,1)S(1)} %get-tuple-element.77.a0), channel_id=1, source_target_pairs={{2,6},{6,10},{10,14},{14,12},{12,8},{8,4},{4,0},{0,2},{7,3},{11,7}... | collective-permute-start | bytes 1572872 | tf_op jit(solution)/shard_map/ppermute | solution.py:229
  3.0 21.1 %collective-permute-start.3 = (bf16[64,4096]{1,0:T(8,128)(2,1)S(1)}, bf16[64,4096]{1,0:T(8,128)(2,1)S(1)}, u32[]{:S(2)}, u32[]{:S(2)}) collective-permute-start(bf16[64,4096]{1,0:T(8,128)(2,1)S(1)} %get-tuple-element.78.a1), channel_id=1, source_target_pairs={{2,6},{6,10},{10,14},{14,12},{12,8},{8,4},{4,0},{0,2},{7,3},{11,7}... | collective-permute-start | bytes 1572872 | tf_op jit(solution)/shard_map/ppermute | solution.py:229
  33.1 15.2 %collective-permute-start.44 = (bf16[128,4096]{1,0:T(8,128)(2,1)S(1)}, bf16[128,4096]{1,0:T(8,128)(2,1)S(1)}, u32[]{:S(2)}, u32[]{:S(2)}) collective-permute-start(bf16[128,4096]{1,0:T(8,128)(2,1)S(1)} %get-tuple-element.134), channel_id=1, source_target_pairs={{0,1},{1,0},{2,3},{3,2},{4,5},{5,4},{6,7},{7,6},{8,9},{9,8},{10,11... | collective-permute-start | bytes 3145736 | tf_op jit(solution)/shard_map/ppermute | solution.py:258
  43.9 17.2 %collective-permute-start.6 = (bf16[128,4096]{1,0:T(8,128)(2,1)S(1)}, bf16[128,4096]{1,0:T(8,128)(2,1)S(1)}, u32[]{:S(2)}, u32[]{:S(2)}) collective-permute-start(bf16[128,4096]{1,0:T(8,128)(2,1)S(1)} %get-tuple-element.95), channel_id=1, source_target_pairs={{0,1},{1,0},{2,3},{3,2},{4,5},{5,4},{6,7},{7,6},{8,9},{9,8},{10,11... | collective-permute-start | bytes 3145736 | tf_op jit(solution)/shard_map/ppermute | solution.py:258
  44.5 15.3 %collective-permute-start.14 = (bf16[64,4096]{1,0:T(8,128)(2,1)S(1)}, bf16[64,4096]{1,0:T(8,128)(2,1)S(1)}, u32[]{:S(2)}, u32[]{:S(2)}) collective-permute-start(bf16[64,4096]{1,0:T(8,128)(2,1)S(1)} %collective-permute-done.8.a0), channel_id=1, source_target_pairs={{2,6},{6,10},{10,14},{14,12},{12,8},{8,4},{4,0},{0,2},{7,3},{11,7}... | collective-permute-start | bytes 1572872 | tf_op jit(solution)/shard_map/ppermute | solution.py:229
  49.2 149.4 %collective-permute-start.53 = (bf16[64,4096]{1,0:T(8,128)(2,1)S(1)}, bf16[64,4096]{1,0:T(8,128)(2,1)S(1)}, u32[]{:S(2)}, u32[]{:S(2)}) collective-permute-start(bf16[64,4096]{1,0:T(8,128)(2,1)S(1)} %get-tuple-element.150), channel_id=1, source_target_pairs={{16,0},{17,1},{18,2},{19,3},{20,4},{21,5},{22,6},{23,7},{24,8},{25... | collective-permute-start | bytes 1572872 | tf_op jit(solution)/shard_map/ppermute | solution.py:265
  58.8 22.7 %collective-permute-start.12 = (bf16[128,4096]{1,0:T(8,128)(2,1)S(1)}, bf16[128,4096]{1,0:T(8,128)(2,1)S(1)}, u32[]{:S(2)}, u32[]{:S(2)}) collective-permute-start(bf16[128,4096]{1,0:T(8,128)(2,1)S(1)} %get-tuple-element.101), channel_id=1, source_target_pairs={{0,1},{1,0},{2,3},{3,2},{4,5},{5,4},{6,7},{7,6},{8,9},{9,8},{10,11... | collective-permute-start | bytes 3145736 | tf_op jit(solution)/shard_map/ppermute | solution.py:258
  62.9 18.9 %collective-permute-start.21 = (bf16[64,4096]{1,0:T(8,128)(2,1)S(1)}, bf16[64,4096]{1,0:T(8,128)(2,1)S(1)}, u32[]{:S(2)}, u32[]{:S(2)}) collective-permute-start(bf16[64,4096]{1,0:T(8,128)(2,1)S(1)} %collective-permute-done.15.a1), channel_id=1, source_target_pairs={{2,6},{6,10},{10,14},{14,12},{12,8},{8,4},{4,0},{0,2},{7,3},{11,7}... | collective-permute-start | bytes 1572872 | tf_op jit(solution)/shard_map/ppermute | solution.py:229
  63.8 16.8 %collective-permute-start.7 = (bf16[64,4096]{1,0:T(8,128)(2,1)S(1)}, bf16[64,4096]{1,0:T(8,128)(2,1)S(1)}, u32[]{:S(2)}, u32[]{:S(2)}) collective-permute-start(bf16[64,4096]{1,0:T(8,128)(2,1)S(1)} %add_convert_fusion.17), channel_id=1, source_target_pairs={{2,6},{6,10},{10,14},{14,12},{12,8},{8,4},{4,0},{0,2},{7,3},{11,7}... | collective-permute-start | bytes 1572872 | tf_op jit(solution)/shard_map/ppermute | solution.py:269
  73.7 27.4 %collective-permute-start.18 = (bf16[128,4096]{1,0:T(8,128)(2,1)S(1)}, bf16[128,4096]{1,0:T(8,128)(2,1)S(1)}, u32[]{:S(2)}, u32[]{:S(2)}) collective-permute-start(bf16[128,4096]{1,0:T(8,128)(2,1)S(1)} %get-tuple-element.107), channel_id=1, source_target_pairs={{0,1},{1,0},{2,3},{3,2},{4,5},{5,4},{6,7},{7,6},{8,9},{9,8},{10,11... | collective-permute-start | bytes 3145736 | tf_op jit(solution)/shard_map/ppermute | solution.py:258
  81.7 19.3 %collective-permute-start.26 = (bf16[64,4096]{1,0:T(8,128)(2,1)S(1)}, bf16[64,4096]{1,0:T(8,128)(2,1)S(1)}, u32[]{:S(2)}, u32[]{:S(2)}) collective-permute-start(bf16[64,4096]{1,0:T(8,128)(2,1)S(1)} %collective-permute-done.20.a0), channel_id=1, source_target_pairs={{2,6},{6,10},{10,14},{14,12},{12,8},{8,4},{4,0},{0,2},{7,3},{11,7}... | collective-permute-start | bytes 1572872 | tf_op jit(solution)/shard_map/ppermute | solution.py:229
  89.9 16.9 %collective-permute-start.27 = (bf16[64,4096]{1,0:T(8,128)(2,1)S(1)}, bf16[64,4096]{1,0:T(8,128)(2,1)S(1)}, u32[]{:S(2)}, u32[]{:S(2)}) collective-permute-start(bf16[64,4096]{1,0:T(8,128)(2,1)S(1)} %collective-permute-done.21.a1), channel_id=1, source_target_pairs={{2,6},{6,10},{10,14},{14,12},{12,8},{8,4},{4,0},{0,2},{7,3},{11,7}... | collective-permute-start | bytes 1572872 | tf_op jit(solution)/shard_map/ppermute | solution.py:229
  101.1 29.0 %collective-permute-start.24 = (bf16[128,4096]{1,0:T(8,128)(2,1)S(1)}, bf16[128,4096]{1,0:T(8,128)(2,1)S(1)}, u32[]{:S(2)}, u32[]{:S(2)}) collective-permute-start(bf16[128,4096]{1,0:T(8,128)(2,1)S(1)} %get-tuple-element.113), channel_id=1, source_target_pairs={{0,1},{1,0},{2,3},{3,2},{4,5},{5,4},{6,7},{7,6},{8,9},{9,8},{10,11... | collective-permute-start | bytes 3145736 | tf_op jit(solution)/shard_map/ppermute | solution.py:258
  106.8 16.7 %collective-permute-start.32 = (bf16[64,4096]{1,0:T(8,128)(2,1)S(1)}, bf16[64,4096]{1,0:T(8,128)(2,1)S(1)}, u32[]{:S(2)}, u32[]{:S(2)}) collective-permute-start(bf16[64,4096]{1,0:T(8,128)(2,1)S(1)} %collective-permute-done.26.a0), channel_id=1, source_target_pairs={{2,6},{6,10},{10,14},{14,12},{12,8},{8,4},{4,0},{0,2},{7,3},{11,7}... | collective-permute-start | bytes 1572872 | tf_op jit(solution)/shard_map/ppermute | solution.py:229
  112.4 17.8 %collective-permute-start.33 = (bf16[64,4096]{1,0:T(8,128)(2,1)S(1)}, bf16[64,4096]{1,0:T(8,128)(2,1)S(1)}, u32[]{:S(2)}, u32[]{:S(2)}) collective-permute-start(bf16[64,4096]{1,0:T(8,128)(2,1)S(1)} %collective-permute-done.27.a1), channel_id=1, source_target_pairs={{2,6},{6,10},{10,14},{14,12},{12,8},{8,4},{4,0},{0,2},{7,3},{11,7}... | collective-permute-start | bytes 1572872 | tf_op jit(solution)/shard_map/ppermute | solution.py:229
  123.5 31.6 %collective-permute-start.30 = (bf16[128,4096]{1,0:T(8,128)(2,1)S(1)}, bf16[128,4096]{1,0:T(8,128)(2,1)S(1)}, u32[]{:S(2)}, u32[]{:S(2)}) collective-permute-start(bf16[128,4096]{1,0:T(8,128)(2,1)S(1)} %get-tuple-element.119), channel_id=1, source_target_pairs={{0,1},{1,0},{2,3},{3,2},{4,5},{5,4},{6,7},{7,6},{8,9},{9,8},{10,11... | collective-permute-start | bytes 3145736 | tf_op jit(solution)/shard_map/ppermute | solution.py:258
  130.2 19.3 %collective-permute-start.38 = (bf16[64,4096]{1,0:T(8,128)(2,1)S(1)}, bf16[64,4096]{1,0:T(8,128)(2,1)S(1)}, u32[]{:S(2)}, u32[]{:S(2)}) collective-permute-start(bf16[64,4096]{1,0:T(8,128)(2,1)S(1)} %collective-permute-done.32.a0), channel_id=1, source_target_pairs={{2,6},{6,10},{10,14},{14,12},{12,8},{8,4},{4,0},{0,2},{7,3},{11,7}... | collective-permute-start | bytes 1572872 | tf_op jit(solution)/shard_map/ppermute | solution.py:229
  149.6 47.6 %collective-permute-start.45 = (bf16[64,4096]{1,0:T(8,128)(2,1)S(1)}, bf16[64,4096]{1,0:T(8,128)(2,1)S(1)}, u32[]{:S(2)}, u32[]{:S(2)}) collective-permute-start(bf16[64,4096]{1,0:T(8,128)(2,1)S(1)} %get-tuple-element.149), channel_id=1, source_target_pairs={{16,0},{17,1},{18,2},{19,3},{20,4},{21,5},{22,6},{23,7},{24,8},{25... | collective-permute-start | bytes 1572872 | tf_op jit(solution)/shard_map/ppermute | solution.py:265
  150.9 16.2 %collective-permute-start.49 = (bf16[64,4096]{1,0:T(8,128)(2,1)S(1)}, bf16[64,4096]{1,0:T(8,128)(2,1)S(1)}, u32[]{:S(2)}, u32[]{:S(2)}) collective-permute-start(bf16[64,4096]{1,0:T(8,128)(2,1)S(1)} %add_convert_fusion.5), channel_id=1, source_target_pairs={{2,6},{6,10},{10,14},{14,12},{12,8},{8,4},{4,0},{0,2},{7,3},{11,7}... | collective-permute-start | bytes 1572872 | tf_op jit(solution)/shard_map/ppermute | solution.py:269
  157.0 19.2 %collective-permute-start.36 = (bf16[128,4096]{1,0:T(8,128)(2,1)S(1)}, bf16[128,4096]{1,0:T(8,128)(2,1)S(1)}, u32[]{:S(2)}, u32[]{:S(2)}) collective-permute-start(bf16[128,4096]{1,0:T(8,128)(2,1)S(1)} %get-tuple-element.125), channel_id=1, source_target_pairs={{0,1},{1,0},{2,3},{3,2},{4,5},{5,4},{6,7},{7,6},{8,9},{9,8},{10,11... | collective-permute-start | bytes 3145736 | tf_op jit(solution)/shard_map/ppermute | solution.py:258
  167.0 23.0 %collective-permute-start.42 = (bf16[128,4096]{1,0:T(8,128)(2,1)S(1)}, bf16[128,4096]{1,0:T(8,128)(2,1)S(1)}, u32[]{:S(2)}, u32[]{:S(2)}) collective-permute-start(bf16[128,4096]{1,0:T(8,128)(2,1)S(1)} %get-tuple-element.131), channel_id=1, source_target_pairs={{0,1},{1,0},{2,3},{3,2},{4,5},{5,4},{6,7},{7,6},{8,9},{9,8},{10,11... | collective-permute-start | bytes 3145736 | tf_op jit(solution)/shard_map/ppermute | solution.py:258
  195.9 17.6 %collective-permute-start.52 = (bf16[64,4096]{1,0:T(8,128)(2,1)S(1)}, bf16[64,4096]{1,0:T(8,128)(2,1)S(1)}, u32[]{:S(2)}, u32[]{:S(2)}) collective-permute-start(bf16[64,4096]{1,0:T(8,128)(2,1)S(1)} %add_convert_fusion.2), channel_id=1, source_target_pairs={{18,6},{22,10},{26,14},{30,12},{28,8},{24,4},{20,0},{16,2},{23,3},... | collective-permute-start | bytes 1572872 | tf_op jit(solution)/shard_map/ppermute | solution.py:276
  197.3 24.9 %collective-permute-start.43 = (bf16[64,4096]{1,0:T(8,128)(2,1)S(1)}, bf16[64,4096]{1,0:T(8,128)(2,1)S(1)}, u32[]{:S(2)}, u32[]{:S(2)}) collective-permute-start(bf16[64,4096]{1,0:T(8,128)(2,1)S(1)} %add_convert_fusion.11), channel_id=1, source_target_pairs={{18,6},{22,10},{26,14},{30,12},{28,8},{24,4},{20,0},{16,2},{23,3},... | collective-permute-start | bytes 1572872 | tf_op jit(solution)/shard_map/ppermute | solution.py:276
  (35 other events, 299.7 us)

commit v4 on v3

--- a/solution.py
+++ b/solution.py
@@ -73,26 +73,29 @@
         entry_copy(n).wait()
         gate_rows_copy(n).wait()
         up_rows_copy(n).wait()
+    picks = []
     for n in range(2):
         rows = pl.ds(n * tokens, tokens)
         place = jnp.broadcast_to(entry[n, 0:1, :], (tokens, tokens)).T
         slot = lax.broadcasted_iota(jnp.int32, (tokens, tokens), 1).astype(jnp.float32)
         pick = jnp.where(place == slot, 1.0, 0.0).astype(jnp.bfloat16)[:, :capacity]
         scale[rows, :] = jnp.broadcast_to(entry[n, 1:2, :], (tokens, tokens)).T
-        gate = jnp.dot(pick, gate_rows[n], preferred_element_type=jnp.float32)
-        up = jnp.dot(pick, up_rows[n], preferred_element_type=jnp.float32)
-        sig = 1.0 / (1.0 + jnp.exp(-gate))
-        gate_slope[rows, :] = up * sig * (1.0 + gate * (1.0 - sig))
-        up_slope[rows, :] = gate * sig
+        picks.append(pick)
     for n in range(4):
         block_copy(n).wait()
 
     for k in range(hidden // HIDDEN_BLOCK):
         columns = pl.ds(k * HIDDEN_BLOCK, HIDDEN_BLOCK)
         hidden_grad = lax.dot_general(block[...], w_down[columns, :], CONTRACT, preferred_element_type=jnp.float32)
-        joined_grad[:, columns] = (hidden_grad * gate_slope[:, columns]).astype(jnp.bfloat16)
         up_columns = pl.ds(hidden + k * HIDDEN_BLOCK, HIDDEN_BLOCK)
-        joined_grad[:, up_columns] = (hidden_grad * up_slope[:, columns]).astype(jnp.bfloat16)
+        for n in range(2):
+            rows = pl.ds(n * tokens, tokens)
+            gate = jnp.dot(picks[n], gate_rows[n, :, columns], preferred_element_type=jnp.float32)
+            up = jnp.dot(picks[n], up_rows[n, :, columns], preferred_element_type=jnp.float32)
+            sig = 1.0 / (1.0 + jnp.exp(-gate))
+            grad = hidden_grad[n * tokens:(n + 1) * tokens]
+            joined_grad[rows, columns] = (grad * (up * sig * (1.0 + gate * (1.0 - sig)))).astype(jnp.bfloat16)
+            joined_grad[rows, up_columns] = (grad * (gate * sig)).astype(jnp.bfloat16)
 
     outs = (mine, given)
 

time: 227 us -> 226 us (level)
  transfers between devices with their start and end apart: 55 -> 55, of which waited for: 21 -> 21; matrix products, arithmetic and copies ran while one was open for 3% -> 3% of each run, Pallas kernels for 33% -> 32%
where the time goes in v4:
time: 226 us; the launch traced here: 223 us
  waiting for transfers between devices  97.9 us (43%)
  Pallas kernels  71.4 us (32%)
  starting transfers between devices  44.8 us (20%)
  other arithmetic  4.62 us (2%)
  local copies, waits for them, and re-layouts  3.58 us (2%)
    pallas_call x8, Pallas kernels, expert_step(): pl.pallas_call(expert_kernel, in_specs=[pl.BlockSpec(memory_space=pltpu.S...  64.7 us
    ppermute x12, waiting for transfers between devices, body(): lax.ppermute(running[h], 'expert', onward).astype(jnp.float32) + total  61.1 us
    ppermute x2, waiting for transfers between devices, body(): last.append(lax.ppermute(running[h], ('section', 'expert'), relay_onward))  23.4 us
    ppermute x14, starting transfers between devices, body(): blocks.append([lax.ppermute(b, 'expert', onward) for b in blocks[-1]])  16.8 us
    ppermute x12, starting transfers between devices, body(): lax.ppermute(running[h], 'expert', onward).astype(jnp.float32) + total  14 us
    pallas_call x1, Pallas kernels, load_inside(): pl.pallas_call(load_kernel, in_specs=[pl.BlockSpec(memory_space=pltpu.HBM...  6.57 us
    all_to_all x1, waiting for transfers between devices, body(): lax.all_to_all(table, 'expert', split_axis=0, concat_axis=0, tiled=True)  5.81 us
    all_to_all x1, starting transfers between devices, body(): lax.all_to_all(table, 'expert', split_axis=0, concat_axis=0, tiled=True)  5.28 us
  transfers between devices with their start and end apart: 55, of which 21 were waited for; matrix products, arithmetic and copies ran while one was open for 3% of the time, Pallas kernels for 32%

profile of v4, /device:TPU:12, one launch (start us, length us, event | category | flops | bytes accessed | tf_op | source)
XLA Modules:
  0.0 222.8 jit_solution(5028378004228117123)
XLA Ops:
  5.5 5.3 %all-to-all-start = ((f32[16,2,128]{2,1,0:T(2,128)}), f32[16,2,128]{2,1,0:T(2,128)S(1)}, u32[]{:S(2)}, u32[]{:S(2)}) async-start(f32[16,2,128]{2,1,0:T(2,128)} %pad_maximum_fusion), calls=%async_computation | async-start | bytes 32768 | tf_op jit(solution)/shard_map/all_to_all | solution.py:247
  11.6 5.8 %all-to-all-done.table = f32[16,2,128]{2,1,0:T(2,128)S(1)} async-done(((f32[16,2,128]{2,1,0:T(2,128)}), f32[16,2,128]{2,1,0:T(2,128)S(1)}, u32[]{:S(2)}, u32[]{:S(2)}) %all-to-all-start) | async-done | bytes 16416 | tf_op jit(solution)/shard_map/all_to_all | solution.py:247
  17.4 6.6 %load_weights.1 = (bf16[768,4096]{1,0:T(8,128)(2,1)S(1)}, bf16[4096,1536]{1,0:T(8,128)(2,1)S(1)}) custom-call(bf16[768,4096]{1,0:T(8,128)(2,1)} %bitcast.39, bf16[4096,768]{1,0:T(8,128)(2,1)} %bitcast.40, bf16[4096,768]{1,0:T(8,128)(2,1)} %bitcast.41), custom_call_target="tpu_custom_call" | custom-call | tf_op jit(solution)/shard_map/load_weights/pallas_call | solution.py:181
  24.8 8.1 %expert_step.8 = (f32[128,4096]{1,0:T(8,128)S(1)}, bf16[128,4096]{1,0:T(8,128)(2,1)S(1)}) custom-call(s32[2]{0:T(128)S(1)} %slice_bitcast_fusion.2.origin, bf16[64,4096]{1,0:T(8,128)(2,1)S(1)} %get-tuple-element.77.a0, bf16[64,4096]{1,0:T(8,128)(2,1)S(1)} %get-tuple-element.78.a1, bf16[64,4096]{1,0:T(8,128)(2,1)S(1)} %collective-permute-done.b0, ...), custom_call_target="tpu_custom_call" | custom-call | flops 4831838208 | bytes 10485760 | tf_op jit(solution)/shard_map/expert_step/pallas_call | solution.py:139
  35.5 8.1 %expert_step.9 = (f32[128,4096]{1,0:T(8,128)S(1)}, bf16[128,4096]{1,0:T(8,128)(2,1)S(1)}) custom-call(s32[2]{0:T(128)S(1)} %slice_reduce_fusion.6.origin, bf16[64,4096]{1,0:T(8,128)(2,1)S(1)} %collective-permute-done.2.a0, bf16[64,4096]{1,0:T(8,128)(2,1)S(1)} %collective-permute-done.3.a1, bf16[64,4096]{1,0:T(8,128)(2,1)S(1)} %collective-permute-done.4.b0, ...), custom_call_target="tpu_custom_call" | custom-call | flops 4831838208 | bytes 10485760 | tf_op jit(solution)/shard_map/expert_step/pallas_call | solution.py:139
  50.3 8.1 %expert_step.10 = (f32[128,4096]{1,0:T(8,128)S(1)}, bf16[128,4096]{1,0:T(8,128)(2,1)S(1)}) custom-call(s32[2]{0:T(128)S(1)} %slice_reduce_fusion.5.origin, bf16[64,4096]{1,0:T(8,128)(2,1)S(1)} %collective-permute-done.8.a0, bf16[64,4096]{1,0:T(8,128)(2,1)S(1)} %collective-permute-done.9.a1, bf16[64,4096]{1,0:T(8,128)(2,1)S(1)} %collective-permute-done.10.b0, ...), custom_call_target="tpu_custom_call" | custom-call | flops 4831838208 | bytes 10485760 | tf_op jit(solution)/shard_map/expert_step/pallas_call | solution.py:139
  64.9 8.1 %expert_step.11 = (f32[128,4096]{1,0:T(8,128)S(1)}, bf16[128,4096]{1,0:T(8,128)(2,1)S(1)}) custom-call(s32[2]{0:T(128)S(1)} %slice_reduce_fusion.4.origin, bf16[64,4096]{1,0:T(8,128)(2,1)S(1)} %collective-permute-done.14.a0, bf16[64,4096]{1,0:T(8,128)(2,1)S(1)} %collective-permute-done.15.a1, bf16[64,4096]{1,0:T(8,128)(2,1)S(1)} %collective-permute-done.16.b0, ...), custom_call_target="tpu_custom_call" | custom-call | flops 4831838208 | bytes 10485760 | tf_op jit(solution)/shard_map/expert_step/pallas_call | solution.py:139
  73.3 6.9 %collective-permute-done.7 = bf16[64,4096]{1,0:T(8,128)(2,1)S(1)} collective-permute-done((bf16[64,4096]{1,0:T(8,128)(2,1)S(1)}, bf16[64,4096]{1,0:T(8,128)(2,1)S(1)}, u32[]{:S(2)}, u32[]{:S(2)}) %collective-permute-start.7) | collective-permute-done | bytes 524320 | tf_op jit(solution)/shard_map/ppermute | solution.py:272
  82.9 6.5 %collective-permute-done.46 = bf16[64,4096]{1,0:T(8,128)(2,1)S(1)} collective-permute-done((bf16[64,4096]{1,0:T(8,128)(2,1)S(1)}, bf16[64,4096]{1,0:T(8,128)(2,1)S(1)}, u32[]{:S(2)}, u32[]{:S(2)}) %collective-permute-start.46) | collective-permute-done | bytes 524320 | tf_op jit(solution)/shard_map/ppermute | solution.py:272
  92.3 8.1 %expert_step.12 = (f32[128,4096]{1,0:T(8,128)S(1)}, bf16[128,4096]{1,0:T(8,128)(2,1)S(1)}) custom-call(s32[2]{0:T(128)S(1)} %slice_reduce_fusion.3.origin, bf16[64,4096]{1,0:T(8,128)(2,1)S(1)} %collective-permute-done.20.a0, bf16[64,4096]{1,0:T(8,128)(2,1)S(1)} %collective-permute-done.21.a1, bf16[64,4096]{1,0:T(8,128)(2,1)S(1)} %collective-permute-done.22.b0, ...), custom_call_target="tpu_custom_call" | custom-call | flops 4831838208 | bytes 10485760 | tf_op jit(solution)/shard_map/expert_step/pallas_call | solution.py:139
  102.2 4.1 %collective-permute-done.13 = bf16[64,4096]{1,0:T(8,128)(2,1)S(1)} collective-permute-done((bf16[64,4096]{1,0:T(8,128)(2,1)S(1)}, bf16[64,4096]{1,0:T(8,128)(2,1)S(1)}, u32[]{:S(2)}, u32[]{:S(2)}) %collective-permute-start.13) | collective-permute-done | bytes 524320 | tf_op jit(solution)/shard_map/ppermute | solution.py:272
  107.5 4.4 %collective-permute-done.47 = bf16[64,4096]{1,0:T(8,128)(2,1)S(1)} collective-permute-done((bf16[64,4096]{1,0:T(8,128)(2,1)S(1)}, bf16[64,4096]{1,0:T(8,128)(2,1)S(1)}, u32[]{:S(2)}, u32[]{:S(2)}) %collective-permute-start.47) | collective-permute-done | bytes 524320 | tf_op jit(solution)/shard_map/ppermute | solution.py:272
  114.7 8.1 %expert_step.13 = (f32[128,4096]{1,0:T(8,128)S(1)}, bf16[128,4096]{1,0:T(8,128)(2,1)S(1)}) custom-call(s32[2]{0:T(128)S(1)} %slice_reduce_fusion.2.origin, bf16[64,4096]{1,0:T(8,128)(2,1)S(1)} %collective-permute-done.26.a0, bf16[64,4096]{1,0:T(8,128)(2,1)S(1)} %collective-permute-done.27.a1, bf16[64,4096]{1,0:T(8,128)(2,1)S(1)} %collective-permute-done.28.b0, ...), custom_call_target="tpu_custom_call" | custom-call | flops 4831838208 | bytes 10485760 | tf_op jit(solution)/shard_map/expert_step/pallas_call | solution.py:139
  123.1 5.6 %collective-permute-done.19 = bf16[64,4096]{1,0:T(8,128)(2,1)S(1)} collective-permute-done((bf16[64,4096]{1,0:T(8,128)(2,1)S(1)}, bf16[64,4096]{1,0:T(8,128)(2,1)S(1)}, u32[]{:S(2)}, u32[]{:S(2)}) %collective-permute-start.19) | collective-permute-done | bytes 524320 | tf_op jit(solution)/shard_map/ppermute | solution.py:272
  131.4 6.5 %collective-permute-done.48 = bf16[64,4096]{1,0:T(8,128)(2,1)S(1)} collective-permute-done((bf16[64,4096]{1,0:T(8,128)(2,1)S(1)}, bf16[64,4096]{1,0:T(8,128)(2,1)S(1)}, u32[]{:S(2)}, u32[]{:S(2)}) %collective-permute-start.48) | collective-permute-done | bytes 524320 | tf_op jit(solution)/shard_map/ppermute | solution.py:272
  140.8 8.1 %expert_step.14 = (f32[128,4096]{1,0:T(8,128)S(1)}, bf16[128,4096]{1,0:T(8,128)(2,1)S(1)}) custom-call(s32[2]{0:T(128)S(1)} %slice_reduce_fusion.1.origin, bf16[64,4096]{1,0:T(8,128)(2,1)S(1)} %collective-permute-done.32.a0, bf16[64,4096]{1,0:T(8,128)(2,1)S(1)} %collective-permute-done.33.a1, bf16[64,4096]{1,0:T(8,128)(2,1)S(1)} %collective-permute-done.34.b0, ...), custom_call_target="tpu_custom_call" | custom-call | flops 4831838208 | bytes 10485760 | tf_op jit(solution)/shard_map/expert_step/pallas_call | solution.py:139
  151.9 2.8 %collective-permute-done.25 = bf16[64,4096]{1,0:T(8,128)(2,1)S(1)} collective-permute-done((bf16[64,4096]{1,0:T(8,128)(2,1)S(1)}, bf16[64,4096]{1,0:T(8,128)(2,1)S(1)}, u32[]{:S(2)}, u32[]{:S(2)}) %collective-permute-start.25) | collective-permute-done | bytes 524320 | tf_op jit(solution)/shard_map/ppermute | solution.py:272
  157.4 8.1 %expert_step.15 = (f32[128,4096]{1,0:T(8,128)S(1)}, bf16[128,4096]{1,0:T(8,128)(2,1)S(1)}) custom-call(s32[2]{0:T(128)S(1)} %slice_reduce_fusion.origin, bf16[64,4096]{1,0:T(8,128)(2,1)S(1)} %collective-permute-done.38.a0, bf16[64,4096]{1,0:T(8,128)(2,1)S(1)} %collective-permute-done.39.a1, bf16[64,4096]{1,0:T(8,128)(2,1)S(1)} %collective-permute-done.40.b0, ...), custom_call_target="tpu_custom_call" | custom-call | flops 4831838208 | bytes 10485760 | tf_op jit(solution)/shard_map/expert_step/pallas_call | solution.py:139
  166.7 8.0 %collective-permute-done.31 = bf16[64,4096]{1,0:T(8,128)(2,1)S(1)} collective-permute-done((bf16[64,4096]{1,0:T(8,128)(2,1)S(1)}, bf16[64,4096]{1,0:T(8,128)(2,1)S(1)}, u32[]{:S(2)}, u32[]{:S(2)}) %collective-permute-start.31) | collective-permute-done | bytes 524320 | tf_op jit(solution)/shard_map/ppermute | solution.py:272
  177.4 6.5 %collective-permute-done.50 = bf16[64,4096]{1,0:T(8,128)(2,1)S(1)} collective-permute-done((bf16[64,4096]{1,0:T(8,128)(2,1)S(1)}, bf16[64,4096]{1,0:T(8,128)(2,1)S(1)}, u32[]{:S(2)}, u32[]{:S(2)}) %collective-permute-start.50) | collective-permute-done | bytes 524320 | tf_op jit(solution)/shard_map/ppermute | solution.py:272
  185.1 4.4 %collective-permute-done.37 = bf16[64,4096]{1,0:T(8,128)(2,1)S(1)} collective-permute-done((bf16[64,4096]{1,0:T(8,128)(2,1)S(1)}, bf16[64,4096]{1,0:T(8,128)(2,1)S(1)}, u32[]{:S(2)}, u32[]{:S(2)}) %collective-permute-start.37) | collective-permute-done | bytes 524320 | tf_op jit(solution)/shard_map/ppermute | solution.py:272
  189.7 5.4 %collective-permute-done.51 = bf16[64,4096]{1,0:T(8,128)(2,1)S(1)} collective-permute-done((bf16[64,4096]{1,0:T(8,128)(2,1)S(1)}, bf16[64,4096]{1,0:T(8,128)(2,1)S(1)}, u32[]{:S(2)}, u32[]{:S(2)}) %collective-permute-start.51) | collective-permute-done | bytes 524320 | tf_op jit(solution)/shard_map/ppermute | solution.py:272
  198.0 14.9 %collective-permute-done.52 = bf16[64,4096]{1,0:T(8,128)(2,1)S(1)} collective-permute-done((bf16[64,4096]{1,0:T(8,128)(2,1)S(1)}, bf16[64,4096]{1,0:T(8,128)(2,1)S(1)}, u32[]{:S(2)}, u32[]{:S(2)}) %collective-permute-start.52) | collective-permute-done | bytes 524320 | tf_op jit(solution)/shard_map/ppermute | solution.py:279
  213.1 8.6 %collective-permute-done.43 = bf16[64,4096]{1,0:T(8,128)(2,1)S(1)} collective-permute-done((bf16[64,4096]{1,0:T(8,128)(2,1)S(1)}, bf16[64,4096]{1,0:T(8,128)(2,1)S(1)}, u32[]{:S(2)}, u32[]{:S(2)}) %collective-permute-start.43) | collective-permute-done | bytes 524320 | tf_op jit(solution)/shard_map/ppermute | solution.py:279
  (138 shorter events, 55.5 us)
Async XLA Ops:
  1.3 16.1 %collective-permute-start = (bf16[64,4096]{1,0:T(8,128)(2,1)S(1)}, bf16[64,4096]{1,0:T(8,128)(2,1)S(1)}, u32[]{:S(2)}, u32[]{:S(2)}) collective-permute-start(bf16[64,4096]{1,0:T(8,128)(2,1)S(1)} %get-tuple-element.77.a0), channel_id=1, source_target_pairs={{0,1},{1,0},{2,3},{3,2},{4,5},{5,4},{6,7},{7,6},{8,9},{9,8},{10,11... | collective-permute-start | bytes 1572872 | tf_op jit(solution)/shard_map/ppermute | solution.py:235
  1.4 22.6 %collective-permute-start.2 = (bf16[64,4096]{1,0:T(8,128)(2,1)S(1)}, bf16[64,4096]{1,0:T(8,128)(2,1)S(1)}, u32[]{:S(2)}, u32[]{:S(2)}) collective-permute-start(bf16[64,4096]{1,0:T(8,128)(2,1)S(1)} %get-tuple-element.77.a0), channel_id=1, source_target_pairs={{2,6},{6,10},{10,14},{14,12},{12,8},{8,4},{4,0},{0,2},{7,3},{11,7}... | collective-permute-start | bytes 1572872 | tf_op jit(solution)/shard_map/ppermute | solution.py:232
  3.0 21.1 %collective-permute-start.3 = (bf16[64,4096]{1,0:T(8,128)(2,1)S(1)}, bf16[64,4096]{1,0:T(8,128)(2,1)S(1)}, u32[]{:S(2)}, u32[]{:S(2)}) collective-permute-start(bf16[64,4096]{1,0:T(8,128)(2,1)S(1)} %get-tuple-element.78.a1), channel_id=1, source_target_pairs={{2,6},{6,10},{10,14},{14,12},{12,8},{8,4},{4,0},{0,2},{7,3},{11,7}... | collective-permute-start | bytes 1572872 | tf_op jit(solution)/shard_map/ppermute | solution.py:232
  32.9 15.2 %collective-permute-start.44 = (bf16[128,4096]{1,0:T(8,128)(2,1)S(1)}, bf16[128,4096]{1,0:T(8,128)(2,1)S(1)}, u32[]{:S(2)}, u32[]{:S(2)}) collective-permute-start(bf16[128,4096]{1,0:T(8,128)(2,1)S(1)} %get-tuple-element.134), channel_id=1, source_target_pairs={{0,1},{1,0},{2,3},{3,2},{4,5},{5,4},{6,7},{7,6},{8,9},{9,8},{10,11... | collective-permute-start | bytes 3145736 | tf_op jit(solution)/shard_map/ppermute | solution.py:261
  43.6 17.2 %collective-permute-start.6 = (bf16[128,4096]{1,0:T(8,128)(2,1)S(1)}, bf16[128,4096]{1,0:T(8,128)(2,1)S(1)}, u32[]{:S(2)}, u32[]{:S(2)}) collective-permute-start(bf16[128,4096]{1,0:T(8,128)(2,1)S(1)} %get-tuple-element.95), channel_id=1, source_target_pairs={{0,1},{1,0},{2,3},{3,2},{4,5},{5,4},{6,7},{7,6},{8,9},{9,8},{10,11... | collective-permute-start | bytes 3145736 | tf_op jit(solution)/shard_map/ppermute | solution.py:261
  44.1 15.3 %collective-permute-start.14 = (bf16[64,4096]{1,0:T(8,128)(2,1)S(1)}, bf16[64,4096]{1,0:T(8,128)(2,1)S(1)}, u32[]{:S(2)}, u32[]{:S(2)}) collective-permute-start(bf16[64,4096]{1,0:T(8,128)(2,1)S(1)} %collective-permute-done.8.a0), channel_id=1, source_target_pairs={{2,6},{6,10},{10,14},{14,12},{12,8},{8,4},{4,0},{0,2},{7,3},{11,7}... | collective-permute-start | bytes 1572872 | tf_op jit(solution)/shard_map/ppermute | solution.py:232
  49.0 149.0 %collective-permute-start.53 = (bf16[64,4096]{1,0:T(8,128)(2,1)S(1)}, bf16[64,4096]{1,0:T(8,128)(2,1)S(1)}, u32[]{:S(2)}, u32[]{:S(2)}) collective-permute-start(bf16[64,4096]{1,0:T(8,128)(2,1)S(1)} %get-tuple-element.150), channel_id=1, source_target_pairs={{16,0},{17,1},{18,2},{19,3},{20,4},{21,5},{22,6},{23,7},{24,8},{25... | collective-permute-start | bytes 1572872 | tf_op jit(solution)/shard_map/ppermute | solution.py:268
  58.4 22.7 %collective-permute-start.12 = (bf16[128,4096]{1,0:T(8,128)(2,1)S(1)}, bf16[128,4096]{1,0:T(8,128)(2,1)S(1)}, u32[]{:S(2)}, u32[]{:S(2)}) collective-permute-start(bf16[128,4096]{1,0:T(8,128)(2,1)S(1)} %get-tuple-element.101), channel_id=1, source_target_pairs={{0,1},{1,0},{2,3},{3,2},{4,5},{5,4},{6,7},{7,6},{8,9},{9,8},{10,11... | collective-permute-start | bytes 3145736 | tf_op jit(solution)/shard_map/ppermute | solution.py:261
  62.5 18.9 %collective-permute-start.21 = (bf16[64,4096]{1,0:T(8,128)(2,1)S(1)}, bf16[64,4096]{1,0:T(8,128)(2,1)S(1)}, u32[]{:S(2)}, u32[]{:S(2)}) collective-permute-start(bf16[64,4096]{1,0:T(8,128)(2,1)S(1)} %collective-permute-done.15.a1), channel_id=1, source_target_pairs={{2,6},{6,10},{10,14},{14,12},{12,8},{8,4},{4,0},{0,2},{7,3},{11,7}... | collective-permute-start | bytes 1572872 | tf_op jit(solution)/shard_map/ppermute | solution.py:232
  63.4 16.8 %collective-permute-start.7 = (bf16[64,4096]{1,0:T(8,128)(2,1)S(1)}, bf16[64,4096]{1,0:T(8,128)(2,1)S(1)}, u32[]{:S(2)}, u32[]{:S(2)}) collective-permute-start(bf16[64,4096]{1,0:T(8,128)(2,1)S(1)} %add_convert_fusion.17), channel_id=1, source_target_pairs={{2,6},{6,10},{10,14},{14,12},{12,8},{8,4},{4,0},{0,2},{7,3},{11,7}... | collective-permute-start | bytes 1572872 | tf_op jit(solution)/shard_map/ppermute | solution.py:272
  73.2 27.4 %collective-permute-start.18 = (bf16[128,4096]{1,0:T(8,128)(2,1)S(1)}, bf16[128,4096]{1,0:T(8,128)(2,1)S(1)}, u32[]{:S(2)}, u32[]{:S(2)}) collective-permute-start(bf16[128,4096]{1,0:T(8,128)(2,1)S(1)} %get-tuple-element.107), channel_id=1, source_target_pairs={{0,1},{1,0},{2,3},{3,2},{4,5},{5,4},{6,7},{7,6},{8,9},{9,8},{10,11... | collective-permute-start | bytes 3145736 | tf_op jit(solution)/shard_map/ppermute | solution.py:261
  81.4 19.2 %collective-permute-start.26 = (bf16[64,4096]{1,0:T(8,128)(2,1)S(1)}, bf16[64,4096]{1,0:T(8,128)(2,1)S(1)}, u32[]{:S(2)}, u32[]{:S(2)}) collective-permute-start(bf16[64,4096]{1,0:T(8,128)(2,1)S(1)} %collective-permute-done.20.a0), channel_id=1, source_target_pairs={{2,6},{6,10},{10,14},{14,12},{12,8},{8,4},{4,0},{0,2},{7,3},{11,7}... | collective-permute-start | bytes 1572872 | tf_op jit(solution)/shard_map/ppermute | solution.py:232
  89.6 16.9 %collective-permute-start.27 = (bf16[64,4096]{1,0:T(8,128)(2,1)S(1)}, bf16[64,4096]{1,0:T(8,128)(2,1)S(1)}, u32[]{:S(2)}, u32[]{:S(2)}) collective-permute-start(bf16[64,4096]{1,0:T(8,128)(2,1)S(1)} %collective-permute-done.21.a1), channel_id=1, source_target_pairs={{2,6},{6,10},{10,14},{14,12},{12,8},{8,4},{4,0},{0,2},{7,3},{11,7}... | collective-permute-start | bytes 1572872 | tf_op jit(solution)/shard_map/ppermute | solution.py:232
  100.5 29.1 %collective-permute-start.24 = (bf16[128,4096]{1,0:T(8,128)(2,1)S(1)}, bf16[128,4096]{1,0:T(8,128)(2,1)S(1)}, u32[]{:S(2)}, u32[]{:S(2)}) collective-permute-start(bf16[128,4096]{1,0:T(8,128)(2,1)S(1)} %get-tuple-element.113), channel_id=1, source_target_pairs={{0,1},{1,0},{2,3},{3,2},{4,5},{5,4},{6,7},{7,6},{8,9},{9,8},{10,11... | collective-permute-start | bytes 3145736 | tf_op jit(solution)/shard_map/ppermute | solution.py:261
  106.4 16.6 %collective-permute-start.32 = (bf16[64,4096]{1,0:T(8,128)(2,1)S(1)}, bf16[64,4096]{1,0:T(8,128)(2,1)S(1)}, u32[]{:S(2)}, u32[]{:S(2)}) collective-permute-start(bf16[64,4096]{1,0:T(8,128)(2,1)S(1)} %collective-permute-done.26.a0), channel_id=1, source_target_pairs={{2,6},{6,10},{10,14},{14,12},{12,8},{8,4},{4,0},{0,2},{7,3},{11,7}... | collective-permute-start | bytes 1572872 | tf_op jit(solution)/shard_map/ppermute | solution.py:232
  112.0 17.8 %collective-permute-start.33 = (bf16[64,4096]{1,0:T(8,128)(2,1)S(1)}, bf16[64,4096]{1,0:T(8,128)(2,1)S(1)}, u32[]{:S(2)}, u32[]{:S(2)}) collective-permute-start(bf16[64,4096]{1,0:T(8,128)(2,1)S(1)} %collective-permute-done.27.a1), channel_id=1, source_target_pairs={{2,6},{6,10},{10,14},{14,12},{12,8},{8,4},{4,0},{0,2},{7,3},{11,7}... | collective-permute-start | bytes 1572872 | tf_op jit(solution)/shard_map/ppermute | solution.py:232
  123.0 31.7 %collective-permute-start.30 = (bf16[128,4096]{1,0:T(8,128)(2,1)S(1)}, bf16[128,4096]{1,0:T(8,128)(2,1)S(1)}, u32[]{:S(2)}, u32[]{:S(2)}) collective-permute-start(bf16[128,4096]{1,0:T(8,128)(2,1)S(1)} %get-tuple-element.119), channel_id=1, source_target_pairs={{0,1},{1,0},{2,3},{3,2},{4,5},{5,4},{6,7},{7,6},{8,9},{9,8},{10,11... | collective-permute-start | bytes 3145736 | tf_op jit(solution)/shard_map/ppermute | solution.py:261
  129.9 19.2 %collective-permute-start.38 = (bf16[64,4096]{1,0:T(8,128)(2,1)S(1)}, bf16[64,4096]{1,0:T(8,128)(2,1)S(1)}, u32[]{:S(2)}, u32[]{:S(2)}) collective-permute-start(bf16[64,4096]{1,0:T(8,128)(2,1)S(1)} %collective-permute-done.32.a0), channel_id=1, source_target_pairs={{2,6},{6,10},{10,14},{14,12},{12,8},{8,4},{4,0},{0,2},{7,3},{11,7}... | collective-permute-start | bytes 1572872 | tf_op jit(solution)/shard_map/ppermute | solution.py:232
  149.0 47.6 %collective-permute-start.45 = (bf16[64,4096]{1,0:T(8,128)(2,1)S(1)}, bf16[64,4096]{1,0:T(8,128)(2,1)S(1)}, u32[]{:S(2)}, u32[]{:S(2)}) collective-permute-start(bf16[64,4096]{1,0:T(8,128)(2,1)S(1)} %get-tuple-element.149), channel_id=1, source_target_pairs={{16,0},{17,1},{18,2},{19,3},{20,4},{21,5},{22,6},{23,7},{24,8},{25... | collective-permute-start | bytes 1572872 | tf_op jit(solution)/shard_map/ppermute | solution.py:268
  150.4 16.2 %collective-permute-start.49 = (bf16[64,4096]{1,0:T(8,128)(2,1)S(1)}, bf16[64,4096]{1,0:T(8,128)(2,1)S(1)}, u32[]{:S(2)}, u32[]{:S(2)}) collective-permute-start(bf16[64,4096]{1,0:T(8,128)(2,1)S(1)} %add_convert_fusion.5), channel_id=1, source_target_pairs={{2,6},{6,10},{10,14},{14,12},{12,8},{8,4},{4,0},{0,2},{7,3},{11,7}... | collective-permute-start | bytes 1572872 | tf_op jit(solution)/shard_map/ppermute | solution.py:272
  156.7 19.1 %collective-permute-start.36 = (bf16[128,4096]{1,0:T(8,128)(2,1)S(1)}, bf16[128,4096]{1,0:T(8,128)(2,1)S(1)}, u32[]{:S(2)}, u32[]{:S(2)}) collective-permute-start(bf16[128,4096]{1,0:T(8,128)(2,1)S(1)} %get-tuple-element.125), channel_id=1, source_target_pairs={{0,1},{1,0},{2,3},{3,2},{4,5},{5,4},{6,7},{7,6},{8,9},{9,8},{10,11... | collective-permute-start | bytes 3145736 | tf_op jit(solution)/shard_map/ppermute | solution.py:261
  166.5 23.0 %collective-permute-start.42 = (bf16[128,4096]{1,0:T(8,128)(2,1)S(1)}, bf16[128,4096]{1,0:T(8,128)(2,1)S(1)}, u32[]{:S(2)}, u32[]{:S(2)}) collective-permute-start(bf16[128,4096]{1,0:T(8,128)(2,1)S(1)} %get-tuple-element.131), channel_id=1, source_target_pairs={{0,1},{1,0},{2,3},{3,2},{4,5},{5,4},{6,7},{7,6},{8,9},{9,8},{10,11... | collective-permute-start | bytes 3145736 | tf_op jit(solution)/shard_map/ppermute | solution.py:261
  195.3 17.6 %collective-permute-start.52 = (bf16[64,4096]{1,0:T(8,128)(2,1)S(1)}, bf16[64,4096]{1,0:T(8,128)(2,1)S(1)}, u32[]{:S(2)}, u32[]{:S(2)}) collective-permute-start(bf16[64,4096]{1,0:T(8,128)(2,1)S(1)} %add_convert_fusion.2), channel_id=1, source_target_pairs={{18,6},{22,10},{26,14},{30,12},{28,8},{24,4},{20,0},{16,2},{23,3},... | collective-permute-start | bytes 1572872 | tf_op jit(solution)/shard_map/ppermute | solution.py:279
  196.7 24.9 %collective-permute-start.43 = (bf16[64,4096]{1,0:T(8,128)(2,1)S(1)}, bf16[64,4096]{1,0:T(8,128)(2,1)S(1)}, u32[]{:S(2)}, u32[]{:S(2)}) collective-permute-start(bf16[64,4096]{1,0:T(8,128)(2,1)S(1)} %add_convert_fusion.11), channel_id=1, source_target_pairs={{18,6},{22,10},{26,14},{30,12},{28,8},{24,4},{20,0},{16,2},{23,3},... | collective-permute-start | bytes 1572872 | tf_op jit(solution)/shard_map/ppermute | solution.py:279
  (35 other events, 299.0 us)
